TPU v7x, 256 devices: a whole 4x4x8 slice. The times are simulated.
256 devices in a mesh: row: 32 (over z, y), col: 8 (over x, core).
Axes of the slice: x: 4, y: 4, z: 8, core: 2. Of those that a mesh axis runs over, the one named last changes fastest.
Arguments:
- features: bfloat16 [96, 256, 2048], P(None, 'row', 'col'), may hold values from -6 to 6
- cotangent: bfloat16 [96, 256, 2048], P(None, 'row', 'col'), may hold values from -6 to 6
- weight_one: bfloat16 [3, 3, 96, 96], replicated, may hold values from -0.21875 to 0.21875
- bias_one: float32 [96], replicated, may hold values from -3 to 3
- weight_two: bfloat16 [3, 3, 96, 96], replicated, may hold values from -0.21875 to 0.21875
Outputs:
- input_grad: bfloat16 [96, 256, 2048], P(None, 'row', 'col')
- grad_one: float32 [82944], P(('row', 'col'))
- grad_two: float32 [82944], P(('row', 'col'))
All inputs are finite; a program needn't handle non-finite values.
Results may differ from a plain program's by a relative error of at most 0.0032.
Values may be sent and summed in bfloat16 or wider, within the bound.
A program may use at most 64 MiB of HBM per device.

v0:
```python
import jax
import jax.numpy as jnp
from jax import lax
from jax.sharding import PartitionSpec as P


def padded_2(cells, sides, width):
    for axis, dim in sides:
        count = lax.axis_size(axis)
        ends = count - 1
        head = lax.slice_in_dim(cells, 0, width, axis=dim)
        tail = lax.slice_in_dim(cells, cells.shape[dim] - width, cells.shape[dim], axis=dim)
        cells = jnp.concatenate(
            [
                lax.ppermute(tail, axis, [(i, (i + 1) % count) for i in range(ends)]),
                cells,
                lax.ppermute(head, axis, [((i + 1) % count, i) for i in range(ends)]),
            ],
            axis=dim,
        )
    return cells


def window(padded, start_y, start_x, tile_rows, tile_cols):
    channels = padded.shape[0]
    piece = lax.slice(
        padded, (0, start_y, start_x), (channels, start_y + tile_rows, start_x + tile_cols)
    )
    return piece.reshape(channels, tile_rows * tile_cols)


def backward_taps(padded, kernel, other, tile_rows, tile_cols):
    channels = padded.shape[0]
    total = jnp.zeros((channels, tile_rows * tile_cols), jnp.float32)
    grads = []
    for offset_y in range(3):
        for offset_x in range(3):
            patch = window(padded, 2 - offset_y, 2 - offset_x, tile_rows, tile_cols)
            total = total + lax.dot_general(
                kernel[offset_y, offset_x],
                patch,
                (((0,), (0,)), ((), ())),
                preferred_element_type=jnp.float32,
            )
            grads.append(
                lax.dot_general(
                    patch, other, (((1,), (1,)), ((), ())), preferred_element_type=jnp.float32
                )
            )
    return (total, jnp.stack(grads).reshape(-1))


def reduce_weights(grads):
    return (
        lax.psum_scatter(grads[0], ("row", "col"), scatter_dimension=0, tiled=True),
        lax.psum_scatter(grads[1], ("row", "col"), scatter_dimension=0, tiled=True),
    )


def local(features, cotangent, weight_one, bias_one, weight_two):
    channels, tile_rows, tile_cols = features.shape
    cell_count = tile_rows * tile_cols
    scale = float(cell_count * lax.axis_size("row") * lax.axis_size("col")) ** (-0.5)
    padded_input = padded_2(features, (("row", 1), ("col", 2)), 1)
    padded_cot = padded_2(cotangent, (("row", 1), ("col", 2)), 1)
    hidden = jnp.zeros((channels, cell_count), jnp.float32)
    for offset_y in range(3):
        for offset_x in range(3):
            patch = window(padded_input, offset_y, offset_x, tile_rows, tile_cols)
            hidden = hidden + jnp.dot(
                weight_one[offset_y, offset_x], patch, preferred_element_type=jnp.float32
            )
    hidden = hidden + bias_one[:, None]
    act = jax.nn.silu(hidden).astype(jnp.bfloat16)
    act_grad, grad_two = backward_taps(padded_cot, weight_two, act, tile_rows, tile_cols)
    grad_two = grad_two * scale
    sig = jax.nn.sigmoid(hidden)
    hidden_grad = (act_grad * sig * (1.0 + hidden * (1.0 - sig))).astype(jnp.bfloat16)
    padded_hid = padded_2(
        hidden_grad.reshape(channels, tile_rows, tile_cols), (("row", 1), ("col", 2)), 1
    )
    back_input, grad_one = backward_taps(
        padded_hid, weight_one, features.reshape(channels, cell_count), tile_rows, tile_cols
    )
    grad_one = grad_one * scale
    input_grad = (cotangent.reshape(channels, cell_count).astype(jnp.float32) + back_input).astype(
        jnp.bfloat16
    )
    input_grad = input_grad.reshape(channels, tile_rows, tile_cols)
    summed_one, summed_two = reduce_weights((grad_one, grad_two))
    return (input_grad, summed_one, summed_two)


def solution(mesh):
    placed = (P(None, "row", "col"), P(None, "row", "col"), P(), P(), P())
    return jax.shard_map(
        local,
        mesh=mesh,
        in_specs=placed,
        out_specs=(P(None, "row", "col"), P(("row", "col")), P(("row", "col"))),
        check_vma=False,
    )
```

profile of v0, /device:TPU:1, one launch (start us, length us, event | category | flops | bytes accessed | tf_op | source)
XLA Modules:
  0.0 358.9 jit_solution(12760716250751119651)
XLA Ops:
  7.2 1.4 fusion.126
  8.6 4.0 %collective-permute-start.4 = (bf16[96,1,256]{2,1,0:T(2,128)(2,1)S(1)}, bf16[96,1,256]{2,1,0:T(2,128)(2,1)S(1)}, u32[]{:S(2)}, u32[]{:S(2)}) collective-permute-start(bf16[96,1,256]{2,1,0:T(2,128)(2,1)S(1)} %get-tuple-element.43), channel_id=1, source_target_pairs={{0,8},{8,16},{16,24},{24,32},{32,40},{40,48},{48,56},{56,64},{64,7... | collective-permute-start | bytes 147464 | tf_op jit(solution)/shard_map/ppermute | solution.py:15
  12.6 1.4 collective-permute-start.5
  14.1 1.4 fusion.127
  15.4 4.0 %collective-permute-start = (bf16[96,1,256]{2,1,0:T(2,128)(2,1)S(1)}, bf16[96,1,256]{2,1,0:T(2,128)(2,1)S(1)}, u32[]{:S(2)}, u32[]{:S(2)}) collective-permute-start(bf16[96,1,256]{2,1,0:T(2,128)(2,1)S(1)} %get-tuple-element.47), channel_id=1, source_target_pairs={{0,8},{8,16},{16,24},{24,32},{32,40},{40,48},{48,56},{56,64},{64,7... | collective-permute-start | bytes 147464 | tf_op jit(solution)/shard_map/ppermute | solution.py:15
  19.4 1.3 collective-permute-start.1
  20.7 1.1 copy.89
  22.2 0.6 copy-done
  23.5 4.5 %collective-permute-start.6 = (bf16[96,10,1]{2,1,0:T(8,128)(2,1)S(1)}, bf16[96,10,1]{2,1,0:T(8,128)(2,1)S(1)}, u32[]{:S(2)}, u32[]{:S(2)}) collective-permute-start(bf16[96,10,1]{2,1,0:T(8,128)(2,1)S(1)} %get-tuple-element.17), channel_id=1, source_target_pairs={{0,1},{1,2},{2,3},{3,4},{4,5},{5,6},{6,7},{8,9},{9,10},{10,11},{11... | collective-permute-start | bytes 5768 | tf_op jit(solution)/shard_map/ppermute | solution.py:15
  28.0 1.9 collective-permute-start.7
  31.9 0.5 pad_maximum_fusion.2
  32.7 1.9 collective-permute-start.2
  34.6 3.8 %collective-permute-start.3 = (bf16[96,10,1]{2,1,0:T(8,128)(2,1)S(1)}, bf16[96,10,1]{2,1,0:T(8,128)(2,1)S(1)}, u32[]{:S(2)}, u32[]{:S(2)}) collective-permute-start(bf16[96,10,1]{2,1,0:T(8,128)(2,1)S(1)} %get-tuple-element.20), channel_id=1, source_target_pairs={{0,1},{1,2},{2,3},{3,4},{4,5},{5,6},{6,7},{8,9},{9,10},{10,11},{11... | collective-permute-start | bytes 5768 | tf_op jit(solution)/shard_map/ppermute | solution.py:15
  38.6 2.0 maximum_maximum_fusion.1
  40.6 1.0 fusion.118
  43.0 2.0 pad_maximum_fusion
  45.0 1.0 fusion.120
  52.8 0.6 fusion.16
  53.4 4.5 %collective-permute-start.8 = (bf16[96,1,256]{2,0,1:T(8,128)(2,1)S(1)}, bf16[96,1,256]{2,0,1:T(8,128)(2,1)S(1)}, u32[]{:S(2)}, u32[]{:S(2)}) collective-permute-start(bf16[96,1,256]{2,0,1:T(8,128)(2,1)S(1)} %get-tuple-element.40), channel_id=1, source_target_pairs={{0,8},{8,16},{16,24},{24,32},{32,40},{40,48},{48,56},{56,64},{64,7... | collective-permute-start | bytes 147464 | tf_op jit(solution)/shard_map/ppermute | solution.py:15
  57.9 1.0 mul.32
  58.9 1.3 collective-permute-start.9
  60.4 3.4 collective-permute-done.9
  63.9 2.1 collective-permute-start.10
  66.0 5.6 %collective-permute-start.11 = (bf16[96,10,1]{2,0,1:T(8,128)(2,1)S(1)}, bf16[96,10,1]{2,0,1:T(8,128)(2,1)S(1)}, u32[]{:S(2)}, u32[]{:S(2)}) collective-permute-start(bf16[96,10,1]{2,0,1:T(8,128)(2,1)S(1)} %get-tuple-element.34), channel_id=1, source_target_pairs={{0,1},{1,2},{2,3},{3,4},{4,5},{5,6},{6,7},{8,9},{9,10},{10,11},{11... | collective-permute-start | bytes 5768 | tf_op jit(solution)/shard_map/ppermute | solution.py:15
  71.8 1.8 collective-permute-done.10
  74.3 0.5 collective-permute-done.11
  77.2 1.0 mul.29
  78.3 2.1 fusion.41
  83.5 0.8 copy.94
  84.3 265.0 %all-reduce.5.cloned.1.call-done = (f32[82944]{0:T(1024)}, f32[82944]{0:T(1024)}) async-done(((f32[82944]{0:T(1024)}, f32[82944]{0:T(1024)}), (f32[82944]{0:T(1024)}, f32[82944]{0:T(1024)})) %all-reduce.5.cloned.1.call-update) | async-done | bytes 663568
  349.3 1.3 dynamic-slice
  350.7 1.3 dynamic-slice.1
  (106 shorter events, 17.7 us)
Async XLA Ops:
  7.2 14.7 %copy-start.2 = (bf16[3,3,96,96]{3,2,1,0:T(8,128)(2,1)S(1)}, bf16[3,3,96,96]{3,2,1,0:T(8,128)(2,1)}, u32[]{:S(2)}) copy-start(bf16[3,3,96,96]{3,2,1,0:T(8,128)(2,1)} %param.7) | copy-start | bytes 497668
  7.2 342.1 %all-reduce.5.cloned.1.call-start = ((), (), s32[]{:S(2)}) async-start(), calls=%async_computation | async-start | bytes 1327104
  8.6 13.6 %collective-permute-start.4 = (bf16[96,1,256]{2,1,0:T(2,128)(2,1)S(1)}, bf16[96,1,256]{2,1,0:T(2,128)(2,1)S(1)}, u32[]{:S(2)}, u32[]{:S(2)}) collective-permute-start(bf16[96,1,256]{2,1,0:T(2,128)(2,1)S(1)} %get-tuple-element.43), channel_id=1, source_target_pairs={{0,8},{8,16},{16,24},{24,32},{32,40},{40,48},{48,56},{56,64},{64,7... | collective-permute-start | bytes 147464 | tf_op jit(solution)/shard_map/ppermute | solution.py:15
  12.6 9.5 %copy-start.1 = (bf16[96,8,256]{2,1,0:T(8,128)(2,1)S(1)}, bf16[96,8,256]{2,1,0:T(8,128)(2,1)}, u32[]{:S(2)}) copy-start(bf16[96,8,256]{2,1,0:T(8,128)(2,1)} %param.6) | copy-start | bytes 1179652
  12.6 9.6 %collective-permute-start.5 = (bf16[96,1,256]{2,1,0:T(2,128)(2,1)S(1)}, bf16[96,1,256]{2,1,0:T(2,128)(2,1)S(1)}, u32[]{:S(2)}, u32[]{:S(2)}) collective-permute-start(bf16[96,1,256]{2,1,0:T(2,128)(2,1)S(1)} %get-tuple-element.44), channel_id=1, source_target_pairs={{8,0},{16,8},{24,16},{32,24},{40,32},{48,40},{56,48},{64,56},{72,6... | collective-permute-start | bytes 147464 | tf_op jit(solution)/shard_map/ppermute | solution.py:17
  15.4 15.3 %collective-permute-start = (bf16[96,1,256]{2,1,0:T(2,128)(2,1)S(1)}, bf16[96,1,256]{2,1,0:T(2,128)(2,1)S(1)}, u32[]{:S(2)}, u32[]{:S(2)}) collective-permute-start(bf16[96,1,256]{2,1,0:T(2,128)(2,1)S(1)} %get-tuple-element.47), channel_id=1, source_target_pairs={{0,8},{8,16},{16,24},{24,32},{32,40},{40,48},{48,56},{56,64},{64,7... | collective-permute-start | bytes 147464 | tf_op jit(solution)/shard_map/ppermute | solution.py:15
  19.4 11.3 %collective-permute-start.1 = (bf16[96,1,256]{2,1,0:T(2,128)(2,1)S(1)}, bf16[96,1,256]{2,1,0:T(2,128)(2,1)S(1)}, u32[]{:S(2)}, u32[]{:S(2)}) collective-permute-start(bf16[96,1,256]{2,1,0:T(2,128)(2,1)S(1)} %get-tuple-element.48), channel_id=1, source_target_pairs={{8,0},{16,8},{24,16},{32,24},{40,32},{48,40},{56,48},{64,56},{72,6... | collective-permute-start | bytes 147464 | tf_op jit(solution)/shard_map/ppermute | solution.py:17
  21.8 1.0 copy-start
  23.5 15.1 %collective-permute-start.6 = (bf16[96,10,1]{2,1,0:T(8,128)(2,1)S(1)}, bf16[96,10,1]{2,1,0:T(8,128)(2,1)S(1)}, u32[]{:S(2)}, u32[]{:S(2)}) collective-permute-start(bf16[96,10,1]{2,1,0:T(8,128)(2,1)S(1)} %get-tuple-element.17), channel_id=1, source_target_pairs={{0,1},{1,2},{2,3},{3,4},{4,5},{5,6},{6,7},{8,9},{9,10},{10,11},{11... | collective-permute-start | bytes 5768 | tf_op jit(solution)/shard_map/ppermute | solution.py:15
  28.0 10.5 %collective-permute-start.7 = (bf16[96,10,1]{2,1,0:T(8,128)(2,1)S(1)}, bf16[96,10,1]{2,1,0:T(8,128)(2,1)S(1)}, u32[]{:S(2)}, u32[]{:S(2)}) collective-permute-start(bf16[96,10,1]{2,1,0:T(8,128)(2,1)S(1)} %get-tuple-element.18), channel_id=1, source_target_pairs={{1,0},{2,1},{3,2},{4,3},{5,4},{6,5},{7,6},{9,8},{10,9},{11,10},{12... | collective-permute-start | bytes 5768 | tf_op jit(solution)/shard_map/ppermute | solution.py:17
  30.7 0.9 copy-start.4
  32.7 10.2 %collective-permute-start.2 = (bf16[96,10,1]{2,1,0:T(8,128)(2,1)S(1)}, bf16[96,10,1]{2,1,0:T(8,128)(2,1)S(1)}, u32[]{:S(2)}, u32[]{:S(2)}) collective-permute-start(bf16[96,10,1]{2,1,0:T(8,128)(2,1)S(1)} %get-tuple-element.19), channel_id=1, source_target_pairs={{1,0},{2,1},{3,2},{4,3},{5,4},{6,5},{7,6},{9,8},{10,9},{11,10},{12... | collective-permute-start | bytes 5768 | tf_op jit(solution)/shard_map/ppermute | solution.py:17
  34.6 8.3 %collective-permute-start.3 = (bf16[96,10,1]{2,1,0:T(8,128)(2,1)S(1)}, bf16[96,10,1]{2,1,0:T(8,128)(2,1)S(1)}, u32[]{:S(2)}, u32[]{:S(2)}) collective-permute-start(bf16[96,10,1]{2,1,0:T(8,128)(2,1)S(1)} %get-tuple-element.20), channel_id=1, source_target_pairs={{0,1},{1,2},{2,3},{3,4},{4,5},{5,6},{6,7},{8,9},{9,10},{10,11},{11... | collective-permute-start | bytes 5768 | tf_op jit(solution)/shard_map/ppermute | solution.py:15
  46.9 0.7 copy-start.5
  53.4 6.8 %collective-permute-start.8 = (bf16[96,1,256]{2,0,1:T(8,128)(2,1)S(1)}, bf16[96,1,256]{2,0,1:T(8,128)(2,1)S(1)}, u32[]{:S(2)}, u32[]{:S(2)}) collective-permute-start(bf16[96,1,256]{2,0,1:T(8,128)(2,1)S(1)} %get-tuple-element.40), channel_id=1, source_target_pairs={{0,8},{8,16},{16,24},{24,32},{32,40},{40,48},{48,56},{56,64},{64,7... | collective-permute-start | bytes 147464 | tf_op jit(solution)/shard_map/ppermute | solution.py:15
  58.9 4.8 %collective-permute-start.9 = (bf16[96,1,256]{2,0,1:T(8,128)(2,1)S(1)}, bf16[96,1,256]{2,0,1:T(8,128)(2,1)S(1)}, u32[]{:S(2)}, u32[]{:S(2)}) collective-permute-start(bf16[96,1,256]{2,0,1:T(8,128)(2,1)S(1)} %get-tuple-element.39), channel_id=1, source_target_pairs={{8,0},{16,8},{24,16},{32,24},{40,32},{48,40},{56,48},{64,56},{72,6... | collective-permute-start | bytes 147464 | tf_op jit(solution)/shard_map/ppermute | solution.py:17
  63.9 9.7 %collective-permute-start.10 = (bf16[96,10,1]{2,0,1:T(8,128)(2,1)S(1)}, bf16[96,10,1]{2,0,1:T(8,128)(2,1)S(1)}, u32[]{:S(2)}, u32[]{:S(2)}) collective-permute-start(bf16[96,10,1]{2,0,1:T(8,128)(2,1)S(1)} %get-tuple-element.35), channel_id=1, source_target_pairs={{1,0},{2,1},{3,2},{4,3},{5,4},{6,5},{7,6},{9,8},{10,9},{11,10},{12... | collective-permute-start | bytes 5768 | tf_op jit(solution)/shard_map/ppermute | solution.py:17
  66.0 8.8 %collective-permute-start.11 = (bf16[96,10,1]{2,0,1:T(8,128)(2,1)S(1)}, bf16[96,10,1]{2,0,1:T(8,128)(2,1)S(1)}, u32[]{:S(2)}, u32[]{:S(2)}) collective-permute-start(bf16[96,10,1]{2,0,1:T(8,128)(2,1)S(1)} %get-tuple-element.34), channel_id=1, source_target_pairs={{0,1},{1,2},{2,3},{3,4},{4,5},{5,6},{6,7},{8,9},{9,10},{10,11},{11... | collective-permute-start | bytes 5768 | tf_op jit(solution)/shard_map/ppermute | solution.py:15
  74.8 2.0 copy-start.3
Sparse Core Ops, SparseCore 0:
  82.3 267.0 all-reduce.4
where the time goes:
time: 360 us; the launch traced here: 359 us
  waiting for transfers between devices  271 us (75%)
  starting transfers between devices  36.4 us (10%)
  local copies, waits for them, and re-layouts  15.1 us (4%)
  between operations  14.9 us (4%)
  matrix products  13.7 us (4%)
  other arithmetic  7.86 us (2%)
    unnamed x2, waiting for transfers between devices  265 us
    ppermute x6, starting transfers between devices, padded_2(): lax.ppermute(tail, axis, [(i, (i + 1) % count) for i in range(ends)])  26.5 us
    ppermute x6, starting transfers between devices, padded_2(): lax.ppermute(head, axis, [((i + 1) % count, i) for i in range(ends)])  9.92 us
    unnamed x36, local copies, waits for them, and re-layouts  7.41 us
  transfers between devices with their start and end apart: 13, of which 5 were waited for; matrix products, arithmetic and copies ran while one was open for 4% of the time, Pallas kernels for 0%

commit v1 on v0

--- a/solution.py
+++ b/solution.py
@@ -51,10 +51,11 @@
 
 
 def reduce_weights(grads):
-    return (
-        lax.psum_scatter(grads[0], ("row", "col"), scatter_dimension=0, tiled=True),
-        lax.psum_scatter(grads[1], ("row", "col"), scatter_dimension=0, tiled=True),
-    )
+    shards = lax.axis_size("row") * lax.axis_size("col")
+    stacked = jnp.stack(grads).reshape(len(grads), shards, -1)
+    spread = lax.all_to_all(stacked, ("row", "col"), 1, 1, tiled=True)
+    summed = spread.sum(axis=1)
+    return (summed[0], summed[1])
 
 
 def local(features, cotangent, weight_one, bias_one, weight_two):

time: 360 us -> 120 us (0.33)
  waiting for transfers between devices: 271 us -> 24 us
  starting transfers between devices: 36.4 us -> 58.5 us
  between operations: 14.9 us -> 1.53 us
    unnamed x2 -> x0, waiting for transfers between devices: 265 us -> none
    all_to_all x0 -> x1, starting transfers between devices: none -> 24.1 us  [reduce_weights(): spread = lax.all_to_all(stacked, ('row', 'col'), 1, 1, tiled=True)]
    all_to_all x0 -> x1, waiting for transfers between devices: none -> 19.6 us  [reduce_weights(): spread = lax.all_to_all(stacked, ('row', 'col'), 1, 1, tiled=True)]
    unnamed x36 -> x42, local copies, waits for them, and re-layouts: 7.41 us -> 5.19 us
  transfers between devices with their start and end apart: 13 -> 13, of which waited for: 5 -> 5; matrix products, arithmetic and copies ran while one was open for 4% -> 16% of each run, Pallas kernels for 0% -> 0%
where the time goes in v1:
time: 120 us; the launch traced here: 119 us
  starting transfers between devices  58.5 us (49%)
  waiting for transfers between devices  24 us (20%)
  local copies, waits for them, and re-layouts  14.6 us (12%)
  matrix products  13.7 us (11%)
  other arithmetic  7.03 us (6%)
  between operations  1.53 us (1%)
    ppermute x6, starting transfers between devices, padded_2(): lax.ppermute(tail, axis, [(i, (i + 1) % count) for i in range(ends)])  24.2 us
    all_to_all x1, starting transfers between devices, reduce_weights(): spread = lax.all_to_all(stacked, ('row', 'col'), 1, 1, tiled=True)  24.1 us
    all_to_all x1, waiting for transfers between devices, reduce_weights(): spread = lax.all_to_all(stacked, ('row', 'col'), 1, 1, tiled=True)  19.6 us
    ppermute x6, starting transfers between devices, padded_2(): lax.ppermute(head, axis, [((i + 1) % count, i) for i in range(ends)])  10.2 us
    dot_general x18, matrix products, backward_taps(): lax.dot_general(kernel[offset_y, offset_x], patch, (((0,), (0,)), ((), ()...  5.88 us
    concatenate x6, other arithmetic, padded_2(): jnp.concatenate([lax.ppermute(tail, axis, [(i, (i + 1) % count) for i in...  5.72 us
    dot_general x18, matrix products, backward_taps(): lax.dot_general(patch, other, (((1,), (1,)), ((), ())), preferred_element...  5.37 us
    unnamed x42, local copies, waits for them, and re-layouts  5.19 us
  transfers between devices with their start and end apart: 13, of which 5 were waited for; matrix products, arithmetic and copies ran while one was open for 16% of the time, Pallas kernels for 0%

profile of v1, /device:TPU:1, one launch (start us, length us, event | category | flops | bytes accessed | tf_op | source)
XLA Modules:
  0.0 119.3 jit_solution(16035210917313546128)
XLA Ops:
  0.6 1.3 %fusion.126 = (bf16[96,1,256]{2,1,0:T(2,128)(2,1)S(1)}, bf16[96,1,256]{2,1,0:T(2,128)(2,1)S(1)}) fusion(bf16[96,8,256]{2,1,0:T(8,128)(2,1)} %param.5), kind=kLoop, calls=%fused_computation.200 | loop fusion | bytes 196608 | tf_op jit(solution)/shard_map/slice | solution.py:12
  2.0 4.0 %collective-permute-start.4 = (bf16[96,1,256]{2,1,0:T(2,128)(2,1)S(1)}, bf16[96,1,256]{2,1,0:T(2,128)(2,1)S(1)}, u32[]{:S(2)}, u32[]{:S(2)}) collective-permute-start(bf16[96,1,256]{2,1,0:T(2,128)(2,1)S(1)} %get-tuple-element.43), channel_id=1, source_target_pairs={{0,8},{8,16},{16,24},{24,32},{32,40},{40,48},{48,56},{56,64},{64,7... | collective-permute-start | bytes 147464 | tf_op jit(solution)/shard_map/ppermute | solution.py:15
  6.0 1.4 %collective-permute-start.5 = (bf16[96,1,256]{2,1,0:T(2,128)(2,1)S(1)}, bf16[96,1,256]{2,1,0:T(2,128)(2,1)S(1)}, u32[]{:S(2)}, u32[]{:S(2)}) collective-permute-start(bf16[96,1,256]{2,1,0:T(2,128)(2,1)S(1)} %get-tuple-element.44), channel_id=1, source_target_pairs={{8,0},{16,8},{24,16},{32,24},{40,32},{48,40},{56,48},{64,56},{72,6... | collective-permute-start | bytes 147464 | tf_op jit(solution)/shard_map/ppermute | solution.py:17
  7.4 1.4 %fusion.127 = (bf16[96,1,256]{2,1,0:T(2,128)(2,1)S(1)}, bf16[96,1,256]{2,1,0:T(2,128)(2,1)S(1)}) fusion(bf16[96,8,256]{2,1,0:T(8,128)(2,1)} %param.6), kind=kLoop, calls=%fused_computation.201 | loop fusion | bytes 196608 | tf_op jit(solution)/shard_map/slice | solution.py:12
  8.8 4.0 %collective-permute-start = (bf16[96,1,256]{2,1,0:T(2,128)(2,1)S(1)}, bf16[96,1,256]{2,1,0:T(2,128)(2,1)S(1)}, u32[]{:S(2)}, u32[]{:S(2)}) collective-permute-start(bf16[96,1,256]{2,1,0:T(2,128)(2,1)S(1)} %get-tuple-element.47), channel_id=1, source_target_pairs={{0,8},{8,16},{16,24},{24,32},{32,40},{40,48},{48,56},{56,64},{64,7... | collective-permute-start | bytes 147464 | tf_op jit(solution)/shard_map/ppermute | solution.py:15
  12.8 1.3 %collective-permute-start.1 = (bf16[96,1,256]{2,1,0:T(2,128)(2,1)S(1)}, bf16[96,1,256]{2,1,0:T(2,128)(2,1)S(1)}, u32[]{:S(2)}, u32[]{:S(2)}) collective-permute-start(bf16[96,1,256]{2,1,0:T(2,128)(2,1)S(1)} %get-tuple-element.48), channel_id=1, source_target_pairs={{8,0},{16,8},{24,16},{32,24},{40,32},{48,40},{56,48},{64,56},{72,6... | collective-permute-start | bytes 147464 | tf_op jit(solution)/shard_map/ppermute | solution.py:17
  14.1 1.1 copy.90
  15.6 0.6 copy-done
  16.9 4.5 %collective-permute-start.6 = (bf16[96,10,1]{2,1,0:T(8,128)(2,1)S(1)}, bf16[96,10,1]{2,1,0:T(8,128)(2,1)S(1)}, u32[]{:S(2)}, u32[]{:S(2)}) collective-permute-start(bf16[96,10,1]{2,1,0:T(8,128)(2,1)S(1)} %get-tuple-element.17), channel_id=1, source_target_pairs={{0,1},{1,2},{2,3},{3,4},{4,5},{5,6},{6,7},{8,9},{9,10},{10,11},{11... | collective-permute-start | bytes 5768 | tf_op jit(solution)/shard_map/ppermute | solution.py:15
  21.4 1.9 %collective-permute-start.7 = (bf16[96,10,1]{2,1,0:T(8,128)(2,1)S(1)}, bf16[96,10,1]{2,1,0:T(8,128)(2,1)S(1)}, u32[]{:S(2)}, u32[]{:S(2)}) collective-permute-start(bf16[96,10,1]{2,1,0:T(8,128)(2,1)S(1)} %get-tuple-element.18), channel_id=1, source_target_pairs={{1,0},{2,1},{3,2},{4,3},{5,4},{6,5},{7,6},{9,8},{10,9},{11,10},{12... | collective-permute-start | bytes 5768 | tf_op jit(solution)/shard_map/ppermute | solution.py:17
  24.8 3.8 %collective-permute-start.3 = (bf16[96,10,1]{2,1,0:T(8,128)(2,1)S(1)}, bf16[96,10,1]{2,1,0:T(8,128)(2,1)S(1)}, u32[]{:S(2)}, u32[]{:S(2)}) collective-permute-start(bf16[96,10,1]{2,1,0:T(8,128)(2,1)S(1)} %get-tuple-element.20), channel_id=1, source_target_pairs={{0,1},{1,2},{2,3},{3,4},{4,5},{5,6},{6,7},{8,9},{9,10},{10,11},{11... | collective-permute-start | bytes 5768 | tf_op jit(solution)/shard_map/ppermute | solution.py:15
  29.4 2.1 %collective-permute-start.2 = (bf16[96,10,1]{2,1,0:T(8,128)(2,1)S(1)}, bf16[96,10,1]{2,1,0:T(8,128)(2,1)S(1)}, u32[]{:S(2)}, u32[]{:S(2)}) collective-permute-start(bf16[96,10,1]{2,1,0:T(8,128)(2,1)S(1)} %get-tuple-element.19), channel_id=1, source_target_pairs={{1,0},{2,1},{3,2},{4,3},{5,4},{6,5},{7,6},{9,8},{10,9},{11,10},{12... | collective-permute-start | bytes 5768 | tf_op jit(solution)/shard_map/ppermute | solution.py:17
  31.6 2.0 %maximum_maximum_fusion.1 = (bf16[96,10,257]{2,1,0:T(8,128)(2,1)S(1)}, bf16[96,10,257]{2,1,0:T(8,128)(2,1)S(1)}) fusion(bf16[96,1,256]{2,1,0:T(2,128)(2,1)S(1)} %collective-permute-done.5, bf16[96,8,256]{2,1,0:T(8,128)(2,1)S(1)} %copy-done, bf16[96,1,256]{2,1,0:T(2,128)(2,1)S(1)} %collective-permute-done.4, ...), kind=kLoop, calls=%fused_computation.43 | loop fusion | flops 3947520 | bytes 1482240 | tf_op jit(solution)/shard_map/concatenate | solution.py:13
  33.6 1.0 fusion.118
  36.0 2.6 %collective-permute-done.2 = bf16[96,10,1]{2,1,0:T(8,128)(2,1)S(1)} collective-permute-done((bf16[96,10,1]{2,1,0:T(8,128)(2,1)S(1)}, bf16[96,10,1]{2,1,0:T(8,128)(2,1)S(1)}, u32[]{:S(2)}, u32[]{:S(2)}) %collective-permute-start.2) | collective-permute-done | bytes 1952 | tf_op jit(solution)/shard_map/ppermute | solution.py:17
  38.5 2.0 %pad_maximum_fusion = (bf16[96,10,257]{2,1,0:T(8,128)(2,1)S(1)}, bf16[96,10,257]{2,1,0:T(8,128)(2,1)S(1)}) fusion(bf16[96,10,1]{2,1,0:T(8,128)(2,1)S(1)} %collective-permute-done.2, bf16[96,1,256]{2,1,0:T(2,128)(2,1)S(1)} %collective-permute-done.1, bf16[96,8,256]{2,1,0:T(8,128)(2,1)S(1)} %copy-done.1, bf16[96,1,256]{2,1,0:T(2,128)(2,1)S(1)} %collective-permute-done, ...), kind=kLoop, calls=%fused_computation.41 | loop fusion | flops 3947520 | bytes 1482240 | tf_op jit(solution)/shard_map/concatenate | solution.py:13
  40.5 1.0 fusion.120
  45.9 0.6 fusion.16
  46.6 4.3 %collective-permute-start.8 = (bf16[96,1,256]{2,0,1:T(8,128)(2,1)S(1)}, bf16[96,1,256]{2,0,1:T(8,128)(2,1)S(1)}, u32[]{:S(2)}, u32[]{:S(2)}) collective-permute-start(bf16[96,1,256]{2,0,1:T(8,128)(2,1)S(1)} %get-tuple-element.40), channel_id=1, source_target_pairs={{0,8},{8,16},{16,24},{24,32},{32,40},{40,48},{48,56},{56,64},{64,7... | collective-permute-start | bytes 147464 | tf_op jit(solution)/shard_map/ppermute | solution.py:15
  50.8 1.5 %collective-permute-start.9 = (bf16[96,1,256]{2,0,1:T(8,128)(2,1)S(1)}, bf16[96,1,256]{2,0,1:T(8,128)(2,1)S(1)}, u32[]{:S(2)}, u32[]{:S(2)}) collective-permute-start(bf16[96,1,256]{2,0,1:T(8,128)(2,1)S(1)} %get-tuple-element.39), channel_id=1, source_target_pairs={{8,0},{16,8},{24,16},{32,24},{40,32},{48,40},{56,48},{64,56},{72,6... | collective-permute-start | bytes 147464 | tf_op jit(solution)/shard_map/ppermute | solution.py:17
  55.8 1.9 %collective-permute-start.10 = (bf16[96,10,1]{2,0,1:T(8,128)(2,1)S(1)}, bf16[96,10,1]{2,0,1:T(8,128)(2,1)S(1)}, u32[]{:S(2)}, u32[]{:S(2)}) collective-permute-start(bf16[96,10,1]{2,0,1:T(8,128)(2,1)S(1)} %get-tuple-element.35), channel_id=1, source_target_pairs={{1,0},{2,1},{3,2},{4,3},{5,4},{6,5},{7,6},{9,8},{10,9},{11,10},{12... | collective-permute-start | bytes 5768 | tf_op jit(solution)/shard_map/ppermute | solution.py:17
  57.8 3.6 %collective-permute-start.11 = (bf16[96,10,1]{2,0,1:T(8,128)(2,1)S(1)}, bf16[96,10,1]{2,0,1:T(8,128)(2,1)S(1)}, u32[]{:S(2)}, u32[]{:S(2)}) collective-permute-start(bf16[96,10,1]{2,0,1:T(8,128)(2,1)S(1)} %get-tuple-element.34), channel_id=1, source_target_pairs={{0,1},{1,2},{2,3},{3,4},{4,5},{5,6},{6,7},{8,9},{9,10},{10,11},{11... | collective-permute-start | bytes 5768 | tf_op jit(solution)/shard_map/ppermute | solution.py:15
  61.5 0.8 copy.70
  62.3 1.1 collective-permute-done.10
  64.0 0.5 collective-permute-done.11
  67.5 1.5 %copy.66 = f32[2,256,324]{2,0,1:T(2,128)} copy(f32[2,256,324]{2,1,0:T(8,128)S(1)} %pad_maximum_fusion.4) | data formatting | bytes 1327104 | tf_op jit(solution)/shard_map/stack | solution.py:55
  69.0 24.1 %all-to-all-start = ((f32[2,256,324]{2,0,1:T(2,128)}), f32[2,256,324]{2,0,1:T(2,128)S(1)}, u32[]{:S(2)}, u32[]{:S(2)}) async-start(f32[2,256,324]{2,0,1:T(2,128)} %copy.66), calls=%async_computation | async-start | bytes 1572864 | tf_op jit(solution)/shard_map/all_to_all | solution.py:56
  93.1 0.9 fusion.41
  94.5 0.9 copy-done.2
  98.0 0.8 copy.95
  98.8 19.6 %all-to-all-done = f32[2,256,324]{2,0,1:T(2,128)S(1)} async-done(((f32[2,256,324]{2,0,1:T(2,128)}), f32[2,256,324]{2,0,1:T(2,128)S(1)}, u32[]{:S(2)}, u32[]{:S(2)}) %all-to-all-start) | async-done | bytes 663584 | tf_op jit(solution)/shard_map/all_to_all | solution.py:56
  118.7 0.6 slice_reduce_fusion
  (115 shorter events, 19.1 us)
Async XLA Ops:
  0.6 14.6 %copy-start.3 = (bf16[3,3,96,96]{3,2,1,0:T(8,128)(2,1)S(1)}, bf16[3,3,96,96]{3,2,1,0:T(8,128)(2,1)}, u32[]{:S(2)}) copy-start(bf16[3,3,96,96]{3,2,1,0:T(8,128)(2,1)} %param.7) | copy-start | bytes 497668
  2.0 13.6 %collective-permute-start.4 = (bf16[96,1,256]{2,1,0:T(2,128)(2,1)S(1)}, bf16[96,1,256]{2,1,0:T(2,128)(2,1)S(1)}, u32[]{:S(2)}, u32[]{:S(2)}) collective-permute-start(bf16[96,1,256]{2,1,0:T(2,128)(2,1)S(1)} %get-tuple-element.43), channel_id=1, source_target_pairs={{0,8},{8,16},{16,24},{24,32},{32,40},{40,48},{48,56},{56,64},{64,7... | collective-permute-start | bytes 147464 | tf_op jit(solution)/shard_map/ppermute | solution.py:15
  6.0 9.5 %copy-start.1 = (bf16[96,8,256]{2,1,0:T(8,128)(2,1)S(1)}, bf16[96,8,256]{2,1,0:T(8,128)(2,1)}, u32[]{:S(2)}) copy-start(bf16[96,8,256]{2,1,0:T(8,128)(2,1)} %param.6) | copy-start | bytes 1179652
  6.0 9.6 %collective-permute-start.5 = (bf16[96,1,256]{2,1,0:T(2,128)(2,1)S(1)}, bf16[96,1,256]{2,1,0:T(2,128)(2,1)S(1)}, u32[]{:S(2)}, u32[]{:S(2)}) collective-permute-start(bf16[96,1,256]{2,1,0:T(2,128)(2,1)S(1)} %get-tuple-element.44), channel_id=1, source_target_pairs={{8,0},{16,8},{24,16},{32,24},{40,32},{48,40},{56,48},{64,56},{72,6... | collective-permute-start | bytes 147464 | tf_op jit(solution)/shard_map/ppermute | solution.py:17
  8.8 15.2 %collective-permute-start = (bf16[96,1,256]{2,1,0:T(2,128)(2,1)S(1)}, bf16[96,1,256]{2,1,0:T(2,128)(2,1)S(1)}, u32[]{:S(2)}, u32[]{:S(2)}) collective-permute-start(bf16[96,1,256]{2,1,0:T(2,128)(2,1)S(1)} %get-tuple-element.47), channel_id=1, source_target_pairs={{0,8},{8,16},{16,24},{24,32},{32,40},{40,48},{48,56},{56,64},{64,7... | collective-permute-start | bytes 147464 | tf_op jit(solution)/shard_map/ppermute | solution.py:15
  12.8 11.3 %collective-permute-start.1 = (bf16[96,1,256]{2,1,0:T(2,128)(2,1)S(1)}, bf16[96,1,256]{2,1,0:T(2,128)(2,1)S(1)}, u32[]{:S(2)}, u32[]{:S(2)}) collective-permute-start(bf16[96,1,256]{2,1,0:T(2,128)(2,1)S(1)} %get-tuple-element.48), channel_id=1, source_target_pairs={{8,0},{16,8},{24,16},{32,24},{40,32},{48,40},{56,48},{64,56},{72,6... | collective-permute-start | bytes 147464 | tf_op jit(solution)/shard_map/ppermute | solution.py:17
  15.2 1.0 copy-start
  16.9 14.8 %collective-permute-start.6 = (bf16[96,10,1]{2,1,0:T(8,128)(2,1)S(1)}, bf16[96,10,1]{2,1,0:T(8,128)(2,1)S(1)}, u32[]{:S(2)}, u32[]{:S(2)}) collective-permute-start(bf16[96,10,1]{2,1,0:T(8,128)(2,1)S(1)} %get-tuple-element.17), channel_id=1, source_target_pairs={{0,1},{1,2},{2,3},{3,4},{4,5},{5,6},{6,7},{8,9},{9,10},{10,11},{11... | collective-permute-start | bytes 5768 | tf_op jit(solution)/shard_map/ppermute | solution.py:15
  21.4 10.2 %collective-permute-start.7 = (bf16[96,10,1]{2,1,0:T(8,128)(2,1)S(1)}, bf16[96,10,1]{2,1,0:T(8,128)(2,1)S(1)}, u32[]{:S(2)}, u32[]{:S(2)}) collective-permute-start(bf16[96,10,1]{2,1,0:T(8,128)(2,1)S(1)} %get-tuple-element.18), channel_id=1, source_target_pairs={{1,0},{2,1},{3,2},{4,3},{5,4},{6,5},{7,6},{9,8},{10,9},{11,10},{12... | collective-permute-start | bytes 5768 | tf_op jit(solution)/shard_map/ppermute | solution.py:17
  24.7 4.3 %copy-start.8 = (bf16[3,3,96,96]{3,2,1,0:T(8,128)(2,1)S(1)}, bf16[3,3,96,96]{3,2,1,0:T(8,128)(2,1)}, u32[]{:S(2)}) copy-start(bf16[3,3,96,96]{3,2,1,0:T(8,128)(2,1)} %param.9) | copy-start | bytes 497668
  24.8 13.8 %collective-permute-start.3 = (bf16[96,10,1]{2,1,0:T(8,128)(2,1)S(1)}, bf16[96,10,1]{2,1,0:T(8,128)(2,1)S(1)}, u32[]{:S(2)}, u32[]{:S(2)}) collective-permute-start(bf16[96,10,1]{2,1,0:T(8,128)(2,1)S(1)} %get-tuple-element.20), channel_id=1, source_target_pairs={{0,1},{1,2},{2,3},{3,4},{4,5},{5,6},{6,7},{8,9},{9,10},{10,11},{11... | collective-permute-start | bytes 5768 | tf_op jit(solution)/shard_map/ppermute | solution.py:15
  29.4 9.1 %collective-permute-start.2 = (bf16[96,10,1]{2,1,0:T(8,128)(2,1)S(1)}, bf16[96,10,1]{2,1,0:T(8,128)(2,1)S(1)}, u32[]{:S(2)}, u32[]{:S(2)}) collective-permute-start(bf16[96,10,1]{2,1,0:T(8,128)(2,1)S(1)} %get-tuple-element.19), channel_id=1, source_target_pairs={{1,0},{2,1},{3,2},{4,3},{5,4},{6,5},{7,6},{9,8},{10,9},{11,10},{12... | collective-permute-start | bytes 5768 | tf_op jit(solution)/shard_map/ppermute | solution.py:17
  44.8 0.7 copy-start.9
  46.6 8.7 %collective-permute-start.8 = (bf16[96,1,256]{2,0,1:T(8,128)(2,1)S(1)}, bf16[96,1,256]{2,0,1:T(8,128)(2,1)S(1)}, u32[]{:S(2)}, u32[]{:S(2)}) collective-permute-start(bf16[96,1,256]{2,0,1:T(8,128)(2,1)S(1)} %get-tuple-element.40), channel_id=1, source_target_pairs={{0,8},{8,16},{16,24},{24,32},{32,40},{40,48},{48,56},{56,64},{64,7... | collective-permute-start | bytes 147464 | tf_op jit(solution)/shard_map/ppermute | solution.py:15
  50.8 4.8 %collective-permute-start.9 = (bf16[96,1,256]{2,0,1:T(8,128)(2,1)S(1)}, bf16[96,1,256]{2,0,1:T(8,128)(2,1)S(1)}, u32[]{:S(2)}, u32[]{:S(2)}) collective-permute-start(bf16[96,1,256]{2,0,1:T(8,128)(2,1)S(1)} %get-tuple-element.39), channel_id=1, source_target_pairs={{8,0},{16,8},{24,16},{32,24},{40,32},{48,40},{56,48},{64,56},{72,6... | collective-permute-start | bytes 147464 | tf_op jit(solution)/shard_map/ppermute | solution.py:17
  55.8 7.5 %collective-permute-start.10 = (bf16[96,10,1]{2,0,1:T(8,128)(2,1)S(1)}, bf16[96,10,1]{2,0,1:T(8,128)(2,1)S(1)}, u32[]{:S(2)}, u32[]{:S(2)}) collective-permute-start(bf16[96,10,1]{2,0,1:T(8,128)(2,1)S(1)} %get-tuple-element.35), channel_id=1, source_target_pairs={{1,0},{2,1},{3,2},{4,3},{5,4},{6,5},{7,6},{9,8},{10,9},{11,10},{12... | collective-permute-start | bytes 5768 | tf_op jit(solution)/shard_map/ppermute | solution.py:17
  57.8 6.8 %collective-permute-start.11 = (bf16[96,10,1]{2,0,1:T(8,128)(2,1)S(1)}, bf16[96,10,1]{2,0,1:T(8,128)(2,1)S(1)}, u32[]{:S(2)}, u32[]{:S(2)}) collective-permute-start(bf16[96,10,1]{2,0,1:T(8,128)(2,1)S(1)} %get-tuple-element.34), channel_id=1, source_target_pairs={{0,1},{1,2},{2,3},{3,4},{4,5},{5,6},{6,7},{8,9},{9,10},{10,11},{11... | collective-permute-start | bytes 5768 | tf_op jit(solution)/shard_map/ppermute | solution.py:15
  63.3 2.5 %copy-start.4 = (bf16[96,10,1]{2,0,1:T(8,128)(2,1)}, bf16[96,10,1]{2,0,1:T(8,128)(2,1)S(1)}, u32[]{:S(2)}) copy-start(bf16[96,10,1]{2,0,1:T(8,128)(2,1)S(1)} %collective-permute-done.10) | copy-start | bytes 5764
  64.5 2.0 %copy-start.6 = (bf16[96,10,1]{2,0,1:T(8,128)(2,1)}, bf16[96,10,1]{2,0,1:T(8,128)(2,1)S(1)}, u32[]{:S(2)}) copy-start(bf16[96,10,1]{2,0,1:T(8,128)(2,1)S(1)} %collective-permute-done.11) | copy-start | bytes 5764
  69.0 24.1 %copy-start.5 = (bf16[96,10,1]{2,0,1:T(8,128)(2,1)S(1)}, bf16[96,10,1]{2,0,1:T(8,128)(2,1)}, u32[]{:S(2)}) copy-start(bf16[96,10,1]{2,0,1:T(8,128)(2,1)} %copy-done.4) | copy-start | bytes 5764
  69.0 24.1 %copy-start.7 = (bf16[96,10,1]{2,0,1:T(8,128)(2,1)S(1)}, bf16[96,10,1]{2,0,1:T(8,128)(2,1)}, u32[]{:S(2)}) copy-start(bf16[96,10,1]{2,0,1:T(8,128)(2,1)} %copy-done.6) | copy-start | bytes 5764
  69.0 49.4 %all-to-all-start = ((f32[2,256,324]{2,0,1:T(2,128)}), f32[2,256,324]{2,0,1:T(2,128)S(1)}, u32[]{:S(2)}, u32[]{:S(2)}) async-start(f32[2,256,324]{2,0,1:T(2,128)} %copy.66), calls=%async_computation | async-start | bytes 1572864 | tf_op jit(solution)/shard_map/all_to_all | solution.py:56
  94.4 1.0 copy-start.2

commit v2 on v1

v2 whole, which is shorter than its diff:
```python
import jax
import jax.numpy as jnp
from jax import lax
from jax.sharding import PartitionSpec as P


def padded_2(cells, sides, width):
    for axis, dim in sides:
        count = lax.axis_size(axis)
        ends = count - 1
        head = lax.slice_in_dim(cells, 0, width, axis=dim)
        tail = lax.slice_in_dim(cells, cells.shape[dim] - width, cells.shape[dim], axis=dim)
        cells = jnp.concatenate(
            [
                lax.ppermute(tail, axis, [(i, (i + 1) % count) for i in range(ends)]),
                cells,
                lax.ppermute(head, axis, [((i + 1) % count, i) for i in range(ends)]),
            ],
            axis=dim,
        )
    return cells


def window(padded, start_y, start_x, tile_rows, tile_cols):
    channels = padded.shape[0]
    piece = lax.slice(
        padded, (0, start_y, start_x), (channels, start_y + tile_rows, start_x + tile_cols)
    )
    return piece.reshape(channels, tile_rows * tile_cols)


def conv_valid(cells, taps):
    return lax.conv_general_dilated(
        cells[None], taps, (1, 1), "VALID", preferred_element_type=jnp.float32
    )[0]


def forward_taps(kernel):
    return jnp.transpose(kernel, (2, 3, 0, 1))


def backward_taps(kernel):
    return jnp.transpose(kernel[::-1, ::-1], (3, 2, 0, 1))


def kernel_grads(upper, padded, start, tile_rows, tile_cols):
    grads = []
    for offset_y in range(3):
        for offset_x in range(3):
            patch = window(padded, start + offset_y, start + offset_x, tile_rows, tile_cols)
            grads.append(
                lax.dot_general(
                    upper, patch, (((1,), (1,)), ((), ())), preferred_element_type=jnp.float32
                )
            )
    return jnp.stack(grads).reshape(-1)


def reduce_weights(grads):
    shards = lax.axis_size("row") * lax.axis_size("col")
    stacked = jnp.stack(grads).reshape(len(grads), shards, -1)
    spread = lax.all_to_all(stacked, ("row", "col"), 1, 1, tiled=True)
    summed = spread.sum(axis=1)
    return (summed[0], summed[1])


def local(features, cotangent, weight_one, bias_one, weight_two):
    channels, tile_rows, tile_cols = features.shape
    row_count, col_count = lax.axis_size("row"), lax.axis_size("col")
    scale = float(tile_rows * tile_cols * row_count * col_count) ** (-0.5)
    both = padded_2(
        jnp.concatenate([features, cotangent], axis=0), (("row", 1), ("col", 2)), 2
    )
    padded_input, padded_cot = both[:channels], both[channels:]
    grid_row = (
        lax.axis_index("row") * tile_rows - 1
        + lax.broadcasted_iota(jnp.int32, (tile_rows + 2, 1), 0)
    )
    grid_col = (
        lax.axis_index("col") * tile_cols - 1
        + lax.broadcasted_iota(jnp.int32, (1, tile_cols + 2), 1)
    )
    inside = (
        (grid_row >= 0)
        & (grid_row < row_count * tile_rows)
        & (grid_col >= 0)
        & (grid_col < col_count * tile_cols)
    )
    hidden = conv_valid(padded_input, forward_taps(weight_one)) + bias_one[:, None, None]
    act = jnp.where(inside, jax.nn.silu(hidden), 0.0).astype(jnp.bfloat16)
    act_grad = conv_valid(padded_cot, backward_taps(weight_two))
    sig = jax.nn.sigmoid(hidden)
    hidden_grad = jnp.where(
        inside, act_grad * sig * (1.0 + hidden * (1.0 - sig)), 0.0
    ).astype(jnp.bfloat16)
    back_input = conv_valid(hidden_grad, backward_taps(weight_one))
    input_grad = (cotangent.astype(jnp.float32) + back_input).astype(jnp.bfloat16)
    grad_two = kernel_grads(
        cotangent.reshape(channels, -1), act, 0, tile_rows, tile_cols
    ) * scale
    inner_grad = hidden_grad[:, 1 : 1 + tile_rows, 1 : 1 + tile_cols].reshape(channels, -1)
    grad_one = kernel_grads(inner_grad, padded_input, 1, tile_rows, tile_cols) * scale
    summed_one, summed_two = reduce_weights((grad_one, grad_two))
    return (input_grad, summed_one, summed_two)


def solution(mesh):
    placed = (P(None, "row", "col"), P(None, "row", "col"), P(), P(), P())
    return jax.shard_map(
        local,
        mesh=mesh,
        in_specs=placed,
        out_specs=(P(None, "row", "col"), P(("row", "col")), P(("row", "col"))),
        check_vma=False,
    )
```

time: 120 us -> 117 us (0.975)
  starting transfers between devices: 58.5 us -> 27.8 us
  local copies, waits for them, and re-layouts: 14.6 us -> 42.3 us
  waiting for transfers between devices: 24 us -> 27.4 us
  matrix products: 13.7 us -> 11.8 us
  other arithmetic: 7.03 us -> 5.48 us
    ppermute x6 -> x2, starting transfers between devices: 24.2 us -> 8.84 us  [padded_2(): lax.ppermute(tail, axis, [(i, (i + 1) % count) for i in range(ends)])]
    conv_general_dilated x0 -> x14, local copies, waits for them, and re-layouts: none -> 14.5 us  [conv_valid(): lax.conv_general_dilated(cells[None], taps, (1, 1), 'VALID', preferred_el...]
    unnamed x42 -> x29, local copies, waits for them, and re-layouts: 5.19 us -> 15.6 us
    all_to_all x1, starting transfers between devices: 24.1 us -> 15.8 us  [reduce_weights(): spread = lax.all_to_all(stacked, ('row', 'col'), 1, 1, tiled=True)]
    dot_general x45 -> x18, matrix products: 13.7 us -> 5.98 us  [kernel_grads(): lax.dot_general(upper, patch, (((1,), (1,)), ((), ())), preferred_element...]
    ppermute x6 -> x2, starting transfers between devices: 10.2 us -> 3.21 us  [padded_2(): lax.ppermute(head, axis, [((i + 1) % count, i) for i in range(ends)])]
    conv_general_dilated x0 -> x3, matrix products: none -> 5.86 us  [conv_valid(): lax.conv_general_dilated(cells[None], taps, (1, 1), 'VALID', preferred_el...]
    broadcast_in_dim x0 -> x3, local copies, waits for them, and re-layouts: none -> 4.6 us  [conv_valid(): cells[None]]
  transfers between devices with their start and end apart: 13 -> 5, of which waited for: 5 -> 4; matrix products, arithmetic and copies ran while one was open for 16% -> 6% of each run, Pallas kernels for 0% -> 0%
where the time goes in v2:
time: 117 us; the launch traced here: 116 us
  local copies, waits for them, and re-layouts  42.3 us (36%)
  starting transfers between devices  27.8 us (24%)
  waiting for transfers between devices  27.4 us (23%)
  matrix products  11.8 us (10%)
  other arithmetic  5.48 us (5%)
    all_to_all x1, waiting for transfers between devices, reduce_weights(): spread = lax.all_to_all(stacked, ('row', 'col'), 1, 1, tiled=True)  18.8 us
    all_to_all x1, starting transfers between devices, reduce_weights(): spread = lax.all_to_all(stacked, ('row', 'col'), 1, 1, tiled=True)  15.8 us
    unnamed x29, local copies, waits for them, and re-layouts  15.6 us
    conv_general_dilated x14, local copies, waits for them, and re-layouts, conv_valid(): lax.conv_general_dilated(cells[None], taps, (1, 1), 'VALID', preferred_el...  14.5 us
    ppermute x2, starting transfers between devices, padded_2(): lax.ppermute(tail, axis, [(i, (i + 1) % count) for i in range(ends)])  8.84 us
    ppermute x2, waiting for transfers between devices, padded_2(): lax.ppermute(head, axis, [((i + 1) % count, i) for i in range(ends)])  6.36 us
    dot_general x18, matrix products, kernel_grads(): lax.dot_general(upper, patch, (((1,), (1,)), ((), ())), preferred_element...  5.98 us
    conv_general_dilated x3, matrix products, conv_valid(): lax.conv_general_dilated(cells[None], taps, (1, 1), 'VALID', preferred_el...  5.86 us
  transfers between devices with their start and end apart: 5, of which 4 were waited for; matrix products, arithmetic and copies ran while one was open for 6% of the time, Pallas kernels for 0%

profile of v2, /device:TPU:1, one launch (start us, length us, event | category | flops | bytes accessed | tf_op | source)
XLA Modules:
  0.0 115.9 jit_solution(6633089567317741151)
XLA Ops:
  0.6 1.1 copy_dynamic-update-slice_fusion
  2.9 4.0 %collective-permute-start = (bf16[192,2,256]{2,0,1:T(8,128)(2,1)S(1)}, bf16[192,2,256]{2,0,1:T(8,128)(2,1)S(1)}, u32[]{:S(2)}, u32[]{:S(2)}) collective-permute-start(bf16[192,2,256]{2,0,1:T(8,128)(2,1)S(1)} %get-tuple-element.17), channel_id=1, source_target_pairs={{0,8},{8,16},{16,24},{24,32},{32,40},{40,48},{48,56},{56,64},{64,7... | collective-permute-start | bytes 589832 | tf_op jit(solution)/shard_map/ppermute | solution.py:15
  6.9 1.3 %collective-permute-start.1 = (bf16[192,2,256]{2,0,1:T(8,128)(2,1)S(1)}, bf16[192,2,256]{2,0,1:T(8,128)(2,1)S(1)}, u32[]{:S(2)}, u32[]{:S(2)}) collective-permute-start(bf16[192,2,256]{2,0,1:T(8,128)(2,1)S(1)} %get-tuple-element.18), channel_id=1, source_target_pairs={{8,0},{16,8},{24,16},{32,24},{40,32},{48,40},{56,48},{64,56},{72,6... | collective-permute-start | bytes 589832 | tf_op jit(solution)/shard_map/ppermute | solution.py:17
  8.2 2.2 %collective-permute-done = bf16[192,2,256]{2,0,1:T(8,128)(2,1)S(1)} collective-permute-done((bf16[192,2,256]{2,0,1:T(8,128)(2,1)S(1)}, bf16[192,2,256]{2,0,1:T(8,128)(2,1)S(1)}, u32[]{:S(2)}, u32[]{:S(2)}) %collective-permute-start) | collective-permute-done | bytes 196640 | tf_op jit(solution)/shard_map/ppermute | solution.py:15
  10.5 3.8 %collective-permute-done.1 = bf16[192,2,256]{2,0,1:T(8,128)(2,1)S(1)} collective-permute-done((bf16[192,2,256]{2,0,1:T(8,128)(2,1)S(1)}, bf16[192,2,256]{2,0,1:T(8,128)(2,1)S(1)}, u32[]{:S(2)}, u32[]{:S(2)}) %collective-permute-start.1) | collective-permute-done | bytes 196640 | tf_op jit(solution)/shard_map/ppermute | solution.py:17
  15.1 4.8 %collective-permute-start.2 = (bf16[192,12,2]{0,2,1:T(2,128)(2,1)S(1)}, bf16[192,12,2]{0,2,1:T(2,128)(2,1)S(1)}, u32[]{:S(2)}, u32[]{:S(2)}) collective-permute-start(bf16[192,12,2]{0,2,1:T(2,128)(2,1)S(1)} %copy.69), channel_id=1, source_target_pairs={{0,1},{1,2},{2,3},{3,4},{4,5},{5,6},{6,7},{8,9},{9,10},{10,11},{11... | collective-permute-start | bytes 27656 | tf_op jit(solution)/shard_map/ppermute | solution.py:15
  20.2 1.9 %collective-permute-start.3 = (bf16[192,12,2]{0,2,1:T(2,128)(2,1)S(1)}, bf16[192,12,2]{0,2,1:T(2,128)(2,1)S(1)}, u32[]{:S(2)}, u32[]{:S(2)}) collective-permute-start(bf16[192,12,2]{0,2,1:T(2,128)(2,1)S(1)} %copy.70), channel_id=1, source_target_pairs={{1,0},{2,1},{3,2},{4,3},{5,4},{6,5},{7,6},{9,8},{10,9},{11,10},{12... | collective-permute-start | bytes 27656 | tf_op jit(solution)/shard_map/ppermute | solution.py:17
  22.7 2.5 %collective-permute-done.3 = bf16[192,12,2]{0,2,1:T(2,128)(2,1)S(1)} collective-permute-done((bf16[192,12,2]{0,2,1:T(2,128)(2,1)S(1)}, bf16[192,12,2]{0,2,1:T(2,128)(2,1)S(1)}, u32[]{:S(2)}, u32[]{:S(2)}) %collective-permute-start.3) | collective-permute-done | bytes 9248 | tf_op jit(solution)/shard_map/ppermute | solution.py:17
  25.6 1.1 pad_maximum_fusion
  27.9 2.2 %copy.131 = bf16[96,12,1,260]{0,3,1,2:T(8,128)(2,1)} copy(bf16[96,12,1,260]{3,0,1,2:T(8,128)(2,1)} %get-tuple-element.13) | data formatting | bytes 1198080
  30.1 2.2 %pad.2.clone = bf16[96,12,1,264]{0,3,1,2:T(8,128)(2,1)} pad(bf16[96,12,1,260]{0,3,1,2:T(8,128)(2,1)} %copy.131, bf16[]{:T(256)} %constant.33), padding=0_0x0_0x0_0x0_4 | pad | bytes 1207298 | tf_op jit(solution)/shard_map/broadcast_in_dim | solution.py:34
  32.3 2.2 %reshape.88 = bf16[96,12,1,8,33]{0,4,3,1,2:T(8,128)(2,1)} reshape(bf16[96,12,1,264]{0,3,1,2:T(8,128)(2,1)} %pad.2.clone) | data formatting | bytes 1216512 | tf_op jit(solution)/shard_map/conv_general_dilated | solution.py:33
  34.5 1.3 %copy.78 = bf16[96,12,1,8,33]{0,3,4,1,2:T(8,128)(2,1)S(1)} copy(bf16[96,12,1,8,33]{0,4,3,1,2:T(8,128)(2,1)} %reshape.88) | data formatting | bytes 1216512 | tf_op jit(solution)/shard_map/conv_general_dilated | solution.py:33
  36.8 1.3 %copy.130 = bf16[96,12,1,260]{0,3,1,2:T(8,128)(2,1)} copy(bf16[96,12,1,260]{3,0,1,2:T(8,128)(2,1)S(1)} %get-tuple-element.14) | data formatting | bytes 1198080
  38.1 1.3 %pad.clone = bf16[96,12,1,264]{0,3,1,2:T(8,128)(2,1)S(1)} pad(bf16[96,12,1,260]{0,3,1,2:T(8,128)(2,1)} %copy.130, bf16[]{:T(256)} %constant.33), padding=0_0x0_0x0_0x0_4 | pad | bytes 1207298 | tf_op jit(solution)/shard_map/broadcast_in_dim | solution.py:34
  39.4 1.2 %reshape.81 = bf16[96,12,1,8,33]{0,4,3,1,2:T(8,128)(2,1)} reshape(bf16[96,12,1,264]{0,3,1,2:T(8,128)(2,1)S(1)} %pad.clone) | data formatting | bytes 1216512 | tf_op jit(solution)/shard_map/conv_general_dilated | solution.py:33
  40.6 1.4 %copy.75 = bf16[96,12,1,8,33]{0,3,4,1,2:T(8,128)(2,1)S(1)} copy(bf16[96,12,1,8,33]{0,4,3,1,2:T(8,128)(2,1)} %reshape.81) | data formatting | bytes 1216512 | tf_op jit(solution)/shard_map/conv_general_dilated | solution.py:33
  42.1 1.8 %convolution_select_fusion = f32[10,8,33,96]{3,1,2,0:T(8,128)S(1)} fusion(bf16[3,3,96,96]{3,2,1,0:T(8,128)(2,1)S(1)} %copy-done.7, bf16[96,12,1,7,2]{0,3,4,1,2:T(8,128)(2,1)S(1)} %slice.140, bf16[96,12,1,8,33]{0,3,4,1,2:T(8,128)(2,1)S(1)} %copy-done.4, pred[8,33]{0,1:T(8,128)(4,1)S(1)} %copy-done.10), kind=kOutput, calls=%fused_computation.7 | convolution fusion | flops 440133120 | bytes 1820424 | tf_op jit(solution)/shard_map/conv_general_dilated | solution.py:33
  43.9 1.5 %copy.85 = f32[10,8,33,96]{3,2,1,0:T(8,128)} copy(f32[10,8,33,96]{3,1,2,0:T(8,128)S(1)} %convolution_select_fusion) | data formatting | bytes 2027520 | tf_op jit(solution)/shard_map/conv_general_dilated | solution.py:33
  45.4 2.8 %add_multiply_fusion = (bf16[10,8,33,96]{3,1,2,0:T(8,128)(2,1)}, f32[10,8,33,96]{3,1,2,0:T(8,128)S(1)}) fusion(f32[10,8,33,96]{3,1,2,0:T(8,128)S(1)} %convolution_select_fusion, f32[96]{0:T(128)S(1)} %copy-done.6, bf16[3,3,96,96]{3,2,1,0:T(8,128)(2,1)S(1)} %copy-done, bf16[96,12,1,7,2]{0,3,4,1,2:T(8,128)(2,1)S(1)} %slice.138, ...), kind=kOutput, calls=%fused_computation.14 | convolution fusion | flops 442667520 | bytes 3341448 | tf_op jit(solution)/shard_map/conv_general_dilated | solution.py:33
  48.1 1.4 %copy.83 = f32[10,8,33,96]{3,2,1,0:T(8,128)} copy(f32[10,8,33,96]{3,1,2,0:T(8,128)S(1)} %get-tuple-element.20) | data formatting | bytes 2027520 | tf_op jit(solution)/shard_map/conv_general_dilated | solution.py:33
  49.6 2.5 %reshape.85 = f32[10,1,264,96]{3,2,0,1:T(8,128)} reshape(f32[10,8,33,96]{3,2,1,0:T(8,128)} %copy.83) | data formatting | bytes 2027520 | tf_op jit(solution)/shard_map/conv_general_dilated | solution.py:33
  52.1 3.0 %copy.128 = f32[10,1,258,96]{2,3,0,1:T(8,128)} copy(f32[10,1,258,96]{3,2,0,1:T(8,128)} %bitcast.179) | data formatting | bytes 1981440
  55.1 2.5 %reshape.92 = f32[10,1,264,96]{3,2,0,1:T(8,128)} reshape(f32[10,8,33,96]{3,2,1,0:T(8,128)} %copy.85) | data formatting | bytes 2027520 | tf_op jit(solution)/shard_map/conv_general_dilated | solution.py:33
  57.6 3.0 %copy.129 = f32[10,1,258,96]{2,3,0,1:T(8,128)} copy(f32[10,1,258,96]{3,2,0,1:T(8,128)} %bitcast.180) | data formatting | bytes 1981440
  60.6 1.9 %add_divide_fusion = (f32[96,10,258]{2,0,1:T(8,128)S(1)}, f32[96,10,258]{2,0,1:T(8,128)S(1)}) fusion(f32[96]{0:T(128)S(1)} %copy-done.6, f32[10,1,258,96]{2,3,0,1:T(8,128)} %copy.129), kind=kLoop, calls=%fused_computation.6 | loop fusion | flops 990720 | bytes 2972544 | tf_op jit(solution)/shard_map/div | solution.py:92
  72.4 1.5 %copy.108 = f32[2,256,324]{2,0,1:T(2,128)} copy(f32[2,256,324]{2,1,0:T(8,128)S(1)} %pad_maximum_fusion.2) | data formatting | bytes 1327104 | tf_op jit(solution)/shard_map/stack | solution.py:61
  73.9 15.8 %all-to-all-start = ((f32[2,256,324]{2,0,1:T(2,128)}), f32[2,256,324]{2,0,1:T(2,128)S(1)}, u32[]{:S(2)}, u32[]{:S(2)}) async-start(f32[2,256,324]{2,0,1:T(2,128)} %copy.108), calls=%async_computation | async-start | bytes 1572864 | tf_op jit(solution)/shard_map/all_to_all | solution.py:62
  90.1 1.2 %copy.79 = bf16[10,8,33,96]{3,2,1,0:T(8,128)(2,1)S(1)} copy(bf16[10,8,33,96]{3,1,2,0:T(8,128)(2,1)} %get-tuple-element.19) | data formatting | bytes 1013760 | tf_op jit(solution)/shard_map/mul | solution.py:94
  93.3 1.3 %convolution_select_fusion.2 = f32[8,8,33,96]{3,1,2,0:T(8,128)S(1)} fusion(bf16[3,3,96,96]{3,2,1,0:T(8,128)(2,1)S(1)} %copy-done.8, bf16[96,10,1,7,2]{0,3,4,1,2:T(8,128)(2,1)S(1)} %slice.142, bf16[96,10,1,8,33]{0,3,4,1,2:T(8,128)(2,1)S(1)} %copy.81, pred[8,33]{0,1:T(8,128)(4,1)S(1)} %copy-done.9), kind=kOutput, calls=%fused_computation.11 | convolution fusion | flops 352171008 | bytes 1510920 | tf_op jit(solution)/shard_map/conv_general_dilated | solution.py:33
  95.0 1.3 %copy.109 = bf16[96,8,256]{2,1,0:T(8,128)(2,1)} copy(bf16[96,8,256]{0,1,2:T(8,128)(2,1)S(1)} %fusion.23) | data formatting | bytes 786432
  96.2 18.8 %all-to-all-done = f32[2,256,324]{2,0,1:T(2,128)S(1)} async-done(((f32[2,256,324]{2,0,1:T(2,128)}), f32[2,256,324]{2,0,1:T(2,128)S(1)}, u32[]{:S(2)}, u32[]{:S(2)}) %all-to-all-start) | async-done | bytes 663584 | tf_op jit(solution)/shard_map/all_to_all | solution.py:62
  (74 shorter events, 18.6 us)
Async XLA Ops:
  0.6 44.7 %copy-start = (bf16[3,3,96,96]{3,2,1,0:T(8,128)(2,1)S(1)}, bf16[3,3,96,96]{3,2,1,0:T(8,128)(2,1)}, u32[]{:S(2)}) copy-start(bf16[3,3,96,96]{3,2,1,0:T(8,128)(2,1)} %param.9) | copy-start | bytes 497668
  2.9 7.6 %collective-permute-start = (bf16[192,2,256]{2,0,1:T(8,128)(2,1)S(1)}, bf16[192,2,256]{2,0,1:T(8,128)(2,1)S(1)}, u32[]{:S(2)}, u32[]{:S(2)}) collective-permute-start(bf16[192,2,256]{2,0,1:T(8,128)(2,1)S(1)} %get-tuple-element.17), channel_id=1, source_target_pairs={{0,8},{8,16},{16,24},{24,32},{32,40},{40,48},{48,56},{56,64},{64,7... | collective-permute-start | bytes 589832 | tf_op jit(solution)/shard_map/ppermute | solution.py:15
  6.9 7.4 %collective-permute-start.1 = (bf16[192,2,256]{2,0,1:T(8,128)(2,1)S(1)}, bf16[192,2,256]{2,0,1:T(8,128)(2,1)S(1)}, u32[]{:S(2)}, u32[]{:S(2)}) collective-permute-start(bf16[192,2,256]{2,0,1:T(8,128)(2,1)S(1)} %get-tuple-element.18), channel_id=1, source_target_pairs={{8,0},{16,8},{24,16},{32,24},{40,32},{48,40},{56,48},{64,56},{72,6... | collective-permute-start | bytes 589832 | tf_op jit(solution)/shard_map/ppermute | solution.py:17
  15.1 7.2 %collective-permute-start.2 = (bf16[192,12,2]{0,2,1:T(2,128)(2,1)S(1)}, bf16[192,12,2]{0,2,1:T(2,128)(2,1)S(1)}, u32[]{:S(2)}, u32[]{:S(2)}) collective-permute-start(bf16[192,12,2]{0,2,1:T(2,128)(2,1)S(1)} %copy.69), channel_id=1, source_target_pairs={{0,1},{1,2},{2,3},{3,4},{4,5},{5,6},{6,7},{8,9},{9,10},{10,11},{11... | collective-permute-start | bytes 27656 | tf_op jit(solution)/shard_map/ppermute | solution.py:15
  20.2 5.0 %collective-permute-start.3 = (bf16[192,12,2]{0,2,1:T(2,128)(2,1)S(1)}, bf16[192,12,2]{0,2,1:T(2,128)(2,1)S(1)}, u32[]{:S(2)}, u32[]{:S(2)}) collective-permute-start(bf16[192,12,2]{0,2,1:T(2,128)(2,1)S(1)} %copy.70), channel_id=1, source_target_pairs={{1,0},{2,1},{3,2},{4,3},{5,4},{6,5},{7,6},{9,8},{10,9},{11,10},{12... | collective-permute-start | bytes 27656 | tf_op jit(solution)/shard_map/ppermute | solution.py:17
  35.8 0.9 copy-start.3
  39.4 2.6 %copy-start.10 = (pred[8,33]{0,1:T(8,128)(4,1)S(1)}, pred[8,33]{0,1:T(8,128)(4,1)}, u32[]{:S(2)}) copy-start(pred[8,33]{0,1:T(8,128)(4,1)} %constant.46) | copy-start | bytes 796
  40.6 1.4 %copy-start.4 = (bf16[96,12,1,8,33]{0,3,4,1,2:T(8,128)(2,1)S(1)}, bf16[96,12,1,8,33]{0,3,4,1,2:T(8,128)(2,1)}, u32[]{:S(2)}) copy-start(bf16[96,12,1,8,33]{0,3,4,1,2:T(8,128)(2,1)} %copy-done.3) | copy-start | bytes 1824772
  40.6 1.5 %copy-start.7 = (bf16[3,3,96,96]{3,2,1,0:T(8,128)(2,1)S(1)}, bf16[3,3,96,96]{3,2,1,0:T(8,128)(2,1)}, u32[]{:S(2)}) copy-start(bf16[3,3,96,96]{3,2,1,0:T(8,128)(2,1)} %param.7) | copy-start | bytes 497668
  43.9 1.5 %copy-start.6 = (f32[96]{0:T(128)S(1)}, f32[96]{0:T(128)}, u32[]{:S(2)}) copy-start(f32[96]{0:T(128)} %param.8) | copy-start | bytes 1156
  62.4 1.4 %copy-start.1 = (f32[10,1,258,96]{2,3,0,1:T(8,128)S(1)}, f32[10,1,258,96]{2,3,0,1:T(8,128)}, u32[]{:S(2)}) copy-start(f32[10,1,258,96]{2,3,0,1:T(8,128)} %copy.128) | copy-start | bytes 2972164
  65.6 1.0 copy-start.5
  68.0 1.0 copy-start.2
  73.9 41.1 %all-to-all-start = ((f32[2,256,324]{2,0,1:T(2,128)}), f32[2,256,324]{2,0,1:T(2,128)S(1)}, u32[]{:S(2)}, u32[]{:S(2)}) async-start(f32[2,256,324]{2,0,1:T(2,128)} %copy.108), calls=%async_computation | async-start | bytes 1572864 | tf_op jit(solution)/shard_map/all_to_all | solution.py:62
  92.4 0.9 copy-start.8
  92.4 0.9 copy-start.9

commit v3 on v2

--- a/solution.py
+++ b/solution.py
@@ -29,18 +29,21 @@
     return piece.reshape(channels, tile_rows * tile_cols)
 
 
-def conv_valid(cells, taps):
-    return lax.conv_general_dilated(
-        cells[None], taps, (1, 1), "VALID", preferred_element_type=jnp.float32
-    )[0]
-
-
-def forward_taps(kernel):
-    return jnp.transpose(kernel, (2, 3, 0, 1))
-
-
-def backward_taps(kernel):
-    return jnp.transpose(kernel[::-1, ::-1], (3, 2, 0, 1))
+def conv_taps(padded, kernel, flip, rows, cols):
+    channels = padded.shape[0]
+    total = jnp.zeros((kernel.shape[2], rows * cols), jnp.float32)
+    for offset_y in range(3):
+        for offset_x in range(3):
+            if flip:
+                patch = window(padded, 2 - offset_y, 2 - offset_x, rows, cols)
+                taps, contract = kernel[offset_y, offset_x], 0
+            else:
+                patch = window(padded, offset_y, offset_x, rows, cols)
+                taps, contract = kernel[offset_y, offset_x], 1
+            total = total + lax.dot_general(
+                taps, patch, (((contract,), (0,)), ((), ())), preferred_element_type=jnp.float32
+            )
+    return total
 
 
 def kernel_grads(upper, padded, start, tile_rows, tile_cols):
@@ -86,19 +89,25 @@
         & (grid_col >= 0)
         & (grid_col < col_count * tile_cols)
     )
-    hidden = conv_valid(padded_input, forward_taps(weight_one)) + bias_one[:, None, None]
+    ext_rows, ext_cols = tile_rows + 2, tile_cols + 2
+    inside = inside.reshape(1, ext_rows * ext_cols)
+    hidden = conv_taps(padded_input, weight_one, False, ext_rows, ext_cols) + bias_one[:, None]
     act = jnp.where(inside, jax.nn.silu(hidden), 0.0).astype(jnp.bfloat16)
-    act_grad = conv_valid(padded_cot, backward_taps(weight_two))
+    act_grad = conv_taps(padded_cot, weight_two, True, ext_rows, ext_cols)
     sig = jax.nn.sigmoid(hidden)
     hidden_grad = jnp.where(
         inside, act_grad * sig * (1.0 + hidden * (1.0 - sig)), 0.0
     ).astype(jnp.bfloat16)
-    back_input = conv_valid(hidden_grad, backward_taps(weight_one))
-    input_grad = (cotangent.astype(jnp.float32) + back_input).astype(jnp.bfloat16)
+    act = act.reshape(channels, ext_rows, ext_cols)
+    hidden_grad = hidden_grad.reshape(channels, ext_rows, ext_cols)
+    back_input = conv_taps(hidden_grad, weight_one, True, tile_rows, tile_cols)
+    input_grad = (cotangent.reshape(channels, -1).astype(jnp.float32) + back_input).astype(
+        jnp.bfloat16
+    ).reshape(channels, tile_rows, tile_cols)
     grad_two = kernel_grads(
         cotangent.reshape(channels, -1), act, 0, tile_rows, tile_cols
     ) * scale
-    inner_grad = hidden_grad[:, 1 : 1 + tile_rows, 1 : 1 + tile_cols].reshape(channels, -1)
+    inner_grad = window(hidden_grad, 1, 1, tile_rows, tile_cols)
     grad_one = kernel_grads(inner_grad, padded_input, 1, tile_rows, tile_cols) * scale
     summed_one, summed_two = reduce_weights((grad_one, grad_two))
     return (input_grad, summed_one, summed_two)

time: 117 us -> 192 us (1.64)
  local copies, waits for them, and re-layouts: 42.3 us -> 108 us
  matrix products: 11.8 us -> 22.4 us
    slice x1 -> x22, local copies, waits for them, and re-layouts: 0.08 us -> 46.3 us  [window(): lax.slice(padded, (0, start_y, start_x), (channels, start_y + tile_rows,...]
    reshape x0 -> x20, local copies, waits for them, and re-layouts: none -> 39.5 us  [the longest x18 37.1 us: window(): return piece.reshape(channels, tile_rows * tile_cols)]
    conv_general_dilated x14 -> x0, local copies, waits for them, and re-layouts: 14.5 us -> none  [conv_valid(): lax.conv_general_dilated(cells[None], taps, (1, 1), 'VALID', preferred_el...]
    dot_general x0 -> x27, matrix products: none -> 12.9 us  [conv_taps(): lax.dot_general(taps, patch, (((contract,), (0,)), ((), ())), preferred_e...]
    conv_general_dilated x3 -> x0, matrix products: 5.86 us -> none  [conv_valid(): lax.conv_general_dilated(cells[None], taps, (1, 1), 'VALID', preferred_el...]
    broadcast_in_dim x3 -> x0, local copies, waits for them, and re-layouts: 4.6 us -> none  [conv_valid(): cells[None]]
    dot_general x18, matrix products: 5.98 us -> 9.46 us  [kernel_grads(): lax.dot_general(upper, patch, (((1,), (1,)), ((), ())), preferred_element...]
    ppermute x2, waiting for transfers between devices: 6.36 us -> 3.84 us  [padded_2(): lax.ppermute(head, axis, [((i + 1) % count, i) for i in range(ends)])]
  transfers between devices with their start and end apart: 5 -> 5, of which waited for: 4 -> 3; matrix products, arithmetic and copies ran while one was open for 6% -> 3% of each run, Pallas kernels for 0% -> 0%
where the time goes in v3:
time: 192 us; the launch traced here: 190 us
  local copies, waits for them, and re-layouts  108 us (56%)
  starting transfers between devices  28.8 us (15%)
  waiting for transfers between devices  25.7 us (13%)
  matrix products  22.4 us (12%)
  other arithmetic  4.28 us (2%)
    slice x22, local copies, waits for them, and re-layouts, window(): lax.slice(padded, (0, start_y, start_x), (channels, start_y + tile_rows,...  46.3 us
    reshape x18, local copies, waits for them, and re-layouts, window(): return piece.reshape(channels, tile_rows * tile_cols)  37.1 us
    all_to_all x1, waiting for transfers between devices, reduce_weights(): spread = lax.all_to_all(stacked, ('row', 'col'), 1, 1, tiled=True)  19.6 us
    all_to_all x1, starting transfers between devices, reduce_weights(): spread = lax.all_to_all(stacked, ('row', 'col'), 1, 1, tiled=True)  16.8 us
    unnamed x85, local copies, waits for them, and re-layouts  14.7 us
    dot_general x27, matrix products, conv_taps(): lax.dot_general(taps, patch, (((contract,), (0,)), ((), ())), preferred_e...  12.9 us
    dot_general x18, matrix products, kernel_grads(): lax.dot_general(upper, patch, (((1,), (1,)), ((), ())), preferred_element...  9.46 us
    ppermute x2, starting transfers between devices, padded_2(): lax.ppermute(tail, axis, [(i, (i + 1) % count) for i in range(ends)])  7.05 us
  transfers between devices with their start and end apart: 5, of which 3 were waited for; matrix products, arithmetic and copies ran while one was open for 3% of the time, Pallas kernels for 0%

profile of v3, /device:TPU:1, one launch (start us, length us, event | category | flops | bytes accessed | tf_op | source)
XLA Modules:
  0.0 190.0 jit_solution(1191015780589509175)
XLA Ops:
  2.8 4.0 %collective-permute-start = (bf16[192,2,256]{2,0,1:T(8,128)(2,1)S(1)}, bf16[192,2,256]{2,0,1:T(8,128)(2,1)S(1)}, u32[]{:S(2)}, u32[]{:S(2)}) collective-permute-start(bf16[192,2,256]{2,0,1:T(8,128)(2,1)S(1)} %get-tuple-element.36), channel_id=1, source_target_pairs={{0,8},{8,16},{16,24},{24,32},{32,40},{40,48},{48,56},{56,64},{64,7... | collective-permute-start | bytes 589832 | tf_op jit(solution)/shard_map/ppermute | solution.py:15
  8.2 2.2 %collective-permute-done = bf16[192,2,256]{2,0,1:T(8,128)(2,1)S(1)} collective-permute-done((bf16[192,2,256]{2,0,1:T(8,128)(2,1)S(1)}, bf16[192,2,256]{2,0,1:T(8,128)(2,1)S(1)}, u32[]{:S(2)}, u32[]{:S(2)}) %collective-permute-start) | collective-permute-done | bytes 196640 | tf_op jit(solution)/shard_map/ppermute | solution.py:15
  10.4 3.8 %collective-permute-done.1 = bf16[192,2,256]{2,0,1:T(8,128)(2,1)S(1)} collective-permute-done((bf16[192,2,256]{2,0,1:T(8,128)(2,1)S(1)}, bf16[192,2,256]{2,0,1:T(8,128)(2,1)S(1)}, u32[]{:S(2)}, u32[]{:S(2)}) %collective-permute-start.1) | collective-permute-done | bytes 196640 | tf_op jit(solution)/shard_map/ppermute | solution.py:17
  15.3 3.7 %collective-permute-start.2 = (bf16[192,12,2]{0,2,1:T(2,128)(2,1)S(1)}, bf16[192,12,2]{0,2,1:T(2,128)(2,1)S(1)}, u32[]{:S(2)}, u32[]{:S(2)}) collective-permute-start(bf16[192,12,2]{0,2,1:T(2,128)(2,1)S(1)} %copy.93), channel_id=1, source_target_pairs={{1,0},{2,1},{3,2},{4,3},{5,4},{6,5},{7,6},{9,8},{10,9},{11,10},{12... | collective-permute-start | bytes 27656 | tf_op jit(solution)/shard_map/ppermute | solution.py:17
  19.1 3.0 %collective-permute-start.3 = (bf16[192,12,2]{0,2,1:T(2,128)(2,1)S(1)}, bf16[192,12,2]{0,2,1:T(2,128)(2,1)S(1)}, u32[]{:S(2)}, u32[]{:S(2)}) collective-permute-start(bf16[192,12,2]{0,2,1:T(2,128)(2,1)S(1)} %copy.96), channel_id=1, source_target_pairs={{0,1},{1,2},{2,3},{3,4},{4,5},{5,6},{6,7},{8,9},{9,10},{10,11},{11... | collective-permute-start | bytes 27656 | tf_op jit(solution)/shard_map/ppermute | solution.py:15
  25.2 3.3 %fusion.126 = (bf16[96,10,258]{2,0,1:T(8,128)(2,1)}, bf16[96,10,258]{2,0,1:T(8,128)(2,1)}, bf16[96,10,258]{2,0,1:T(8,128)(2,1)}, bf16[96,10,258]{2,0,1:T(8,128)(...) fusion(bf16[192,12,260]{2,0,1:T(8,128)(2,1)S(1)} %pad_maximum_fusion.1), kind=kLoop, calls=%fused_computation.186 | loop fusion | bytes 5944320 | tf_op jit(solution)/shard_map/slice | solution.py:26
  28.5 2.3 %copy.115 = bf16[96,10,258]{0,2,1:T(8,128)(2,1)} copy(bf16[96,10,258]{2,0,1:T(8,128)(2,1)} %get-tuple-element.11) | data formatting | bytes 990720 | tf_op jit(solution)/shard_map/slice | solution.py:26
  30.8 2.2 %reshape.211 = bf16[96,2580]{0,1:T(8,128)(2,1)} reshape(bf16[96,10,258]{0,2,1:T(8,128)(2,1)} %copy.115) | data formatting | bytes 990720 | tf_op jit(solution)/shard_map/reshape | solution.py:29
  33.0 2.3 %copy.112 = bf16[96,10,258]{0,2,1:T(8,128)(2,1)} copy(bf16[96,10,258]{2,0,1:T(8,128)(2,1)} %get-tuple-element.12) | data formatting | bytes 990720 | tf_op jit(solution)/shard_map/slice | solution.py:26
  35.3 2.2 %reshape.208 = bf16[96,2580]{0,1:T(8,128)(2,1)} reshape(bf16[96,10,258]{0,2,1:T(8,128)(2,1)} %copy.112) | data formatting | bytes 990720 | tf_op jit(solution)/shard_map/reshape | solution.py:29
  38.6 2.1 %reshape.205 = bf16[96,2580]{0,1:T(8,128)(2,1)} reshape(bf16[96,10,258]{0,2,1:T(8,128)(2,1)} %copy.109) | data formatting | bytes 990720 | tf_op jit(solution)/shard_map/reshape | solution.py:29
  40.8 2.3 %copy.106 = bf16[96,10,258]{0,2,1:T(8,128)(2,1)} copy(bf16[96,10,258]{2,0,1:T(8,128)(2,1)} %get-tuple-element.14) | data formatting | bytes 990720 | tf_op jit(solution)/shard_map/slice | solution.py:26
  49.9 2.5 %maximum_maximum_fusion = (bf16[192,12,258]{2,0,1:T(8,128)(2,1)S(1)}, bf16[192,12,258]{2,0,1:T(8,128)(2,1)S(1)}) fusion(bf16[192,2,256]{2,0,1:T(8,128)(2,1)S(1)} %collective-permute-done.1, bf16[192,8,256]{2,0,1:T(8,128)(2,1)S(1)} %constant_dynamic-update-slice_fusion, bf16[192,2,256]{2,0,1:T(8,128)(2,1)} %copy-done.29, bf16[192,12,2]{2,0,1:T(8,128)(2,1)S(1)} %copy.97, ...), kind=kLoop, calls=%fused_computation.36 | loop fusion | flops 9510912 | bytes 3575808 | tf_op jit(solution)/shard_map/concatenate | solution.py:13
  52.4 3.6 %fusion.125 = (bf16[96,10,258]{2,0,1:T(8,128)(2,1)}, bf16[96,10,258]{2,0,1:T(8,128)(2,1)}, bf16[96,10,258]{2,0,1:T(8,128)(2,1)}, bf16[96,10,258]{2,0,1:T(8,128)(...) fusion(bf16[192,12,258]{2,0,1:T(8,128)(2,1)S(1)} %get-tuple-ele, ...), kind=kLoop, calls=%fused_computation.185 | loop fusion | bytes 11888640 | tf_op jit(solution)/shard_map/slice | solution.py:26
  56.2 2.3 %copy.116 = bf16[96,10,258]{0,2,1:T(8,128)(2,1)} copy(bf16[96,10,258]{2,0,1:T(8,128)(2,1)} %get-tuple-element.5) | data formatting | bytes 990720 | tf_op jit(solution)/shard_map/slice | solution.py:26
  60.6 2.3 %copy.113 = bf16[96,10,258]{0,2,1:T(8,128)(2,1)} copy(bf16[96,10,258]{2,0,1:T(8,128)(2,1)} %get-tuple-element.6) | data formatting | bytes 990720 | tf_op jit(solution)/shard_map/slice | solution.py:26
  65.0 2.3 %copy.110 = bf16[96,10,258]{0,2,1:T(8,128)(2,1)} copy(bf16[96,10,258]{2,0,1:T(8,128)(2,1)} %get-tuple-element.7) | data formatting | bytes 990720 | tf_op jit(solution)/shard_map/slice | solution.py:26
  69.4 2.3 %copy.105 = bf16[96,10,258]{0,2,1:T(8,128)(2,1)} copy(bf16[96,10,258]{2,0,1:T(8,128)(2,1)} %get-tuple-element.8) | data formatting | bytes 990720 | tf_op jit(solution)/shard_map/slice | solution.py:26
  73.7 2.3 %copy.102 = bf16[96,10,258]{0,2,1:T(8,128)(2,1)} copy(bf16[96,10,258]{2,0,1:T(8,128)(2,1)} %get-tuple-element.9) | data formatting | bytes 990720 | tf_op jit(solution)/shard_map/slice | solution.py:26
  76.1 2.1 %reshape.198 = bf16[96,2580]{0,1:T(8,128)(2,1)} reshape(bf16[96,10,258]{0,2,1:T(8,128)(2,1)} %copy.102) | data formatting | bytes 990720 | tf_op jit(solution)/shard_map/reshape | solution.py:29
  78.2 2.3 %copy.95 = bf16[96,10,258]{0,2,1:T(8,128)(2,1)} copy(bf16[96,10,258]{2,0,1:T(8,128)(2,1)} %get-tuple-element.10) | data formatting | bytes 990720 | tf_op jit(solution)/shard_map/slice | solution.py:26
  80.5 2.1 %reshape.195 = bf16[96,2580]{0,1:T(8,128)(2,1)} reshape(bf16[96,10,258]{0,2,1:T(8,128)(2,1)} %copy.95) | data formatting | bytes 990720 | tf_op jit(solution)/shard_map/reshape | solution.py:29
  82.6 2.3 %copy.101 = bf16[96,10,258]{0,2,1:T(8,128)(2,1)} copy(bf16[96,10,258]{2,0,1:T(8,128)(2,1)} %get-tuple-element.49) | data formatting | bytes 990720 | tf_op jit(solution)/shard_map/slice | solution.py:26
  87.0 2.3 %copy.104 = bf16[96,10,258]{0,2,1:T(8,128)(2,1)} copy(bf16[96,10,258]{2,0,1:T(8,128)(2,1)} %get-tuple-element.50) | data formatting | bytes 990720 | tf_op jit(solution)/shard_map/slice | solution.py:26
  91.4 2.3 %copy.107 = bf16[96,10,258]{0,2,1:T(8,128)(2,1)} copy(bf16[96,10,258]{2,0,1:T(8,128)(2,1)} %get-tuple-element.51) | data formatting | bytes 990720 | tf_op jit(solution)/shard_map/slice | solution.py:26
  95.8 2.3 %copy.108 = bf16[96,10,258]{0,2,1:T(8,128)(2,1)} copy(bf16[96,10,258]{2,0,1:T(8,128)(2,1)} %get-tuple-element.52) | data formatting | bytes 990720 | tf_op jit(solution)/shard_map/slice | solution.py:26
  98.1 2.1 %reshape.204 = bf16[96,2580]{0,1:T(8,128)(2,1)} reshape(bf16[96,10,258]{0,2,1:T(8,128)(2,1)} %copy.108) | data formatting | bytes 990720 | tf_op jit(solution)/shard_map/reshape | solution.py:29
  100.3 2.3 %copy.111 = bf16[96,10,258]{0,2,1:T(8,128)(2,1)} copy(bf16[96,10,258]{2,0,1:T(8,128)(2,1)} %get-tuple-element.53) | data formatting | bytes 990720 | tf_op jit(solution)/shard_map/slice | solution.py:26
  105.8 2.2 %reshape.210 = bf16[96,2580]{0,1:T(8,128)(2,1)} reshape(bf16[96,10,258]{0,2,1:T(8,128)(2,1)} %copy.114) | data formatting | bytes 990720 | tf_op jit(solution)/shard_map/reshape | solution.py:29
  131.3 2.3 %fusion.131 = (bf16[96,8,256]{0,2,1:T(8,128)(2,1)}, bf16[96,8,256]{0,2,1:T(8,128)(2,1)}, bf16[96,8,256]{0,2,1:T(8,128)(2,1)}, bf16[96,8,256]{0,2,1:T(8,128)(2,1)...) fusion(bf16[96,10,258]{0,2,1:T(8,128)(2,1)S(1)} %reshape.213), kind=kLoop, calls=%fused_computation.191 | loop fusion | bytes 7077888 | tf_op jit(solution)/shard_map/slice | solution.py:26
  147.0 16.8 %all-to-all-start = ((f32[2,256,324]{2,0,1:T(2,128)}), f32[2,256,324]{2,0,1:T(2,128)S(1)}, u32[]{:S(2)}, u32[]{:S(2)}) async-start(f32[2,256,324]{2,0,1:T(2,128)} %copy.149), calls=%async_computation | async-start | bytes 1572864 | tf_op jit(solution)/shard_map/all_to_all | solution.py:65
  169.5 19.6 %all-to-all-done = f32[2,256,324]{2,0,1:T(2,128)S(1)} async-done(((f32[2,256,324]{2,0,1:T(2,128)}), f32[2,256,324]{2,0,1:T(2,128)S(1)}, u32[]{:S(2)}, u32[]{:S(2)}) %all-to-all-start) | async-done | bytes 663584 | tf_op jit(solution)/shard_map/all_to_all | solution.py:65
  (173 shorter events, 76.7 us)
Async XLA Ops:
  2.8 7.6 %collective-permute-start = (bf16[192,2,256]{2,0,1:T(8,128)(2,1)S(1)}, bf16[192,2,256]{2,0,1:T(8,128)(2,1)S(1)}, u32[]{:S(2)}, u32[]{:S(2)}) collective-permute-start(bf16[192,2,256]{2,0,1:T(8,128)(2,1)S(1)} %get-tuple-element.36), channel_id=1, source_target_pairs={{0,8},{8,16},{16,24},{24,32},{32,40},{40,48},{48,56},{56,64},{64,7... | collective-permute-start | bytes 589832 | tf_op jit(solution)/shard_map/ppermute | solution.py:15
  6.9 7.4 %collective-permute-start.1 = (bf16[192,2,256]{2,0,1:T(8,128)(2,1)S(1)}, bf16[192,2,256]{2,0,1:T(8,128)(2,1)S(1)}, u32[]{:S(2)}, u32[]{:S(2)}) collective-permute-start(bf16[192,2,256]{2,0,1:T(8,128)(2,1)S(1)} %get-tuple-element.37), channel_id=1, source_target_pairs={{8,0},{16,8},{24,16},{32,24},{40,32},{48,40},{56,48},{64,56},{72,6... | collective-permute-start | bytes 589832 | tf_op jit(solution)/shard_map/ppermute | solution.py:17
  10.4 13.7 %copy-start.29 = (bf16[192,2,256]{2,0,1:T(8,128)(2,1)}, bf16[192,2,256]{2,0,1:T(8,128)(2,1)S(1)}, u32[]{:S(2)}) copy-start(bf16[192,2,256]{2,0,1:T(8,128)(2,1)S(1)} %collective-permute-done) | copy-start | bytes 589828
  14.4 7.9 %copy-start.31 = (bf16[96,8,256]{2,1,0:T(8,128)(2,1)S(1)}, bf16[96,8,256]{2,1,0:T(8,128)(2,1)}, u32[]{:S(2)}) copy-start(bf16[96,8,256]{2,1,0:T(8,128)(2,1)} %param.6) | copy-start | bytes 1179652
  15.3 8.3 %collective-permute-start.2 = (bf16[192,12,2]{0,2,1:T(2,128)(2,1)S(1)}, bf16[192,12,2]{0,2,1:T(2,128)(2,1)S(1)}, u32[]{:S(2)}, u32[]{:S(2)}) collective-permute-start(bf16[192,12,2]{0,2,1:T(2,128)(2,1)S(1)} %copy.93), channel_id=1, source_target_pairs={{1,0},{2,1},{3,2},{4,3},{5,4},{6,5},{7,6},{9,8},{10,9},{11,10},{12... | collective-permute-start | bytes 27656 | tf_op jit(solution)/shard_map/ppermute | solution.py:17
  19.1 4.2 %collective-permute-start.3 = (bf16[192,12,2]{0,2,1:T(2,128)(2,1)S(1)}, bf16[192,12,2]{0,2,1:T(2,128)(2,1)S(1)}, u32[]{:S(2)}, u32[]{:S(2)}) collective-permute-start(bf16[192,12,2]{0,2,1:T(2,128)(2,1)S(1)} %copy.96), channel_id=1, source_target_pairs={{0,1},{1,2},{2,3},{3,4},{4,5},{5,6},{6,7},{8,9},{9,10},{10,11},{11... | collective-permute-start | bytes 27656 | tf_op jit(solution)/shard_map/ppermute | solution.py:15
  24.1 1.1 copy-start.1
  30.8 6.6 %copy-start.4 = (bf16[96,10,258]{2,0,1:T(8,128)(2,1)S(1)}, bf16[96,10,258]{2,0,1:T(8,128)(2,1)}, u32[]{:S(2)}) copy-start(bf16[96,10,258]{2,0,1:T(8,128)(2,1)} %get-tuple-element.13) | copy-start | bytes 1486084
  38.6 6.5 %copy-start.3 = (bf16[96,10,258]{2,0,1:T(8,128)(2,1)S(1)}, bf16[96,10,258]{2,0,1:T(8,128)(2,1)}, u32[]{:S(2)}) copy-start(bf16[96,10,258]{2,0,1:T(8,128)(2,1)} %get-tuple-element.15) | copy-start | bytes 1486084
  52.4 3.8 %copy-start = (bf16[192,12,258]{2,0,1:T(8,128)(2,1)}, bf16[192,12,258]{2,0,1:T(8,128)(2,1)S(1)}, u32[]{:S(2)}) copy-start(bf16[192,12,258]{2,0,1:T(8,128)(2,1)S(1)} %get-tuple-element.32) | copy-start | bytes 3566596
  105.8 3.7 %copy-start.11 = (bf16[96,2580]{0,1:T(8,128)(2,1)S(1)}, bf16[96,2580]{0,1:T(8,128)(2,1)}, u32[]{:S(2)}) copy-start(bf16[96,2580]{0,1:T(8,128)(2,1)} %reshape.196) | copy-start | bytes 1486084
  109.5 1.2 copy-start.18
  109.5 1.2 copy-start.39
  110.8 1.1 copy-start.15
  111.9 1.1 copy-start.9
  112.9 1.1 copy-start.17
  114.0 1.1 copy-start.13
  115.1 1.1 copy-start.8
  116.2 1.1 copy-start.33
  116.2 1.5 copy-start.7
  117.7 1.1 copy-start.12
  124.3 1.1 copy-start.40
  125.3 1.4 copy-start.36
  131.3 2.3 %copy-start.30 = (bf16[192,2,256]{2,0,1:T(8,128)(2,1)S(1)}, bf16[192,2,256]{2,0,1:T(8,128)(2,1)}, u32[]{:S(2)}) copy-start(bf16[192,2,256]{2,0,1:T(8,128)(2,1)} %copy-done.29) | copy-start | bytes 589828
  134.0 2.0 %copy-start.38 = (bf16[96,8,256]{2,1,0:T(8,128)(2,1)S(1)}, bf16[96,8,256]{2,1,0:T(8,128)(2,1)}, u32[]{:S(2)}) copy-start(bf16[96,8,256]{2,1,0:T(8,128)(2,1)} %param.5) | copy-start | bytes 1179652
  141.3 1.1 copy-start.32
  145.5 18.3 %copy-start.28 = (bf16[96,8,256]{0,2,1:T(8,128)(2,1)S(1)}, bf16[96,8,256]{0,2,1:T(8,128)(2,1)}, u32[]{:S(2)}) copy-start(bf16[96,8,256]{0,2,1:T(8,128)(2,1)} %get-tuple-element.46) | copy-start | bytes 1179652
  145.5 18.3 %copy-start.34 = (bf16[3,3,96,96]{3,2,1,0:T(8,128)(2,1)S(1)}, bf16[3,3,96,96]{3,2,1,0:T(8,128)(2,1)}, u32[]{:S(2)}) copy-start(bf16[3,3,96,96]{3,2,1,0:T(8,128)(2,1)} %param.7) | copy-start | bytes 497668
  147.0 17.1 %copy-start.27 = (bf16[96,8,256]{0,2,1:T(8,128)(2,1)S(1)}, bf16[96,8,256]{0,2,1:T(8,128)(2,1)}, u32[]{:S(2)}) copy-start(bf16[96,8,256]{0,2,1:T(8,128)(2,1)} %get-tuple-element.45) | copy-start | bytes 1179652
  147.0 42.1 %all-to-all-start = ((f32[2,256,324]{2,0,1:T(2,128)}), f32[2,256,324]{2,0,1:T(2,128)S(1)}, u32[]{:S(2)}, u32[]{:S(2)}) async-start(f32[2,256,324]{2,0,1:T(2,128)} %copy.149), calls=%async_computation | async-start | bytes 1572864 | tf_op jit(solution)/shard_map/all_to_all | solution.py:65
  167.0 1.2 copy-start.2
  167.0 1.3 copy-start.20
  (14 other events, 15.1 us)

commit v4 on v3

v4 whole, which is shorter than its diff:
```python
import jax
import jax.numpy as jnp
from jax import lax
from jax.sharding import PartitionSpec as P


def padded_2(cells, sides, width):
    for axis, dim in sides:
        count = lax.axis_size(axis)
        ends = count - 1
        head = lax.slice_in_dim(cells, 0, width, axis=dim)
        tail = lax.slice_in_dim(cells, cells.shape[dim] - width, cells.shape[dim], axis=dim)
        cells = jnp.concatenate(
            [
                lax.ppermute(tail, axis, [(i, (i + 1) % count) for i in range(ends)]),
                cells,
                lax.ppermute(head, axis, [((i + 1) % count, i) for i in range(ends)]),
            ],
            axis=dim,
        )
    return cells


def window(padded, start_y, start_x, tile_rows, tile_cols):
    channels = padded.shape[0]
    piece = lax.slice(
        padded, (0, start_y, start_x), (channels, start_y + tile_rows, start_x + tile_cols)
    )
    return piece.reshape(channels, tile_rows * tile_cols)


def conv_taps(padded, kernel, flip, rows, cols):
    total = jnp.zeros((kernel.shape[2], rows * cols), jnp.float32)
    for offset_y in range(3):
        for offset_x in range(3):
            if flip:
                patch = window(padded, 2 - offset_y, 2 - offset_x, rows, cols)
            else:
                patch = window(padded, offset_y, offset_x, rows, cols)
            total = total + lax.dot_general(
                kernel[offset_y, offset_x],
                patch,
                (((0 if flip else 1,), (0,)), ((), ())),
                preferred_element_type=jnp.float32,
            )
    return total


def kernel_grads(pairs):
    return jnp.stack(
        [
            lax.dot_general(
                upper, lower, (((1,), (1,)), ((), ())), preferred_element_type=jnp.float32
            )
            for upper, lower in pairs
        ]
    ).reshape(-1)


def reduce_weights(grads):
    shards = lax.axis_size("row") * lax.axis_size("col")
    stacked = jnp.stack(grads).reshape(len(grads), shards, -1)
    spread = lax.all_to_all(stacked, ("row", "col"), 1, 1, tiled=True)
    summed = spread.sum(axis=1)
    return (summed[0], summed[1])


def local(features, cotangent, weight_one, bias_one, weight_two):
    channels, tile_rows, tile_cols = features.shape
    row_count, col_count = lax.axis_size("row"), lax.axis_size("col")
    scale = float(tile_rows * tile_cols * row_count * col_count) ** (-0.5)
    ext_rows = tile_rows + 2
    both = padded_2(jnp.concatenate([features, cotangent], axis=0), (("row", 1),), 2)
    both = padded_2(both, (("col", 2),), 1)
    padded_input, padded_cot = both[:channels], both[channels:]
    grid_row = (
        lax.axis_index("row") * tile_rows
        - 1
        + lax.broadcasted_iota(jnp.int32, (1, ext_rows * tile_cols), 1) // tile_cols
    )
    inside = (grid_row >= 0) & (grid_row < row_count * tile_rows)
    inner = slice(tile_cols, tile_cols * (tile_rows + 1))
    hidden = conv_taps(padded_input, weight_one, False, ext_rows, tile_cols) + bias_one[:, None]
    act = jax.nn.silu(hidden[:, inner]).astype(jnp.bfloat16)
    act_grad = conv_taps(padded_cot, weight_two, True, ext_rows, tile_cols)
    sig = jax.nn.sigmoid(hidden)
    hidden_grad = jnp.where(
        inside, act_grad * sig * (1.0 + hidden * (1.0 - sig)), 0.0
    ).astype(jnp.bfloat16)
    padded_hid = padded_2(
        hidden_grad.reshape(channels, ext_rows, tile_cols), (("col", 2),), 1
    )
    back_input = conv_taps(padded_hid, weight_one, True, tile_rows, tile_cols)
    input_grad = (cotangent.reshape(channels, -1).astype(jnp.float32) + back_input).astype(
        jnp.bfloat16
    ).reshape(channels, tile_rows, tile_cols)
    grad_two = kernel_grads(
        [
            (window(padded_cot, 3 - offset_y, 2 - offset_x, tile_rows, tile_cols), act)
            for offset_y in range(3)
            for offset_x in range(3)
        ]
    ) * scale
    inner_grad = hidden_grad[:, inner]
    grad_one = kernel_grads(
        [
            (inner_grad, window(padded_input, offset_y + 1, offset_x, tile_rows, tile_cols))
            for offset_y in range(3)
            for offset_x in range(3)
        ]
    ) * scale
    summed_one, summed_two = reduce_weights((grad_one, grad_two))
    return (input_grad, summed_one, summed_two)


def solution(mesh):
    placed = (P(None, "row", "col"), P(None, "row", "col"), P(), P(), P())
    return jax.shard_map(
        local,
        mesh=mesh,
        in_specs=placed,
        out_specs=(P(None, "row", "col"), P(("row", "col")), P(("row", "col"))),
        check_vma=False,
    )
```

time: 192 us -> 150 us (0.78)
  local copies, waits for them, and re-layouts: 108 us -> 63.9 us
  starting transfers between devices: 28.8 us -> 33.4 us
  matrix products: 22.4 us -> 17.9 us
  other arithmetic: 4.28 us -> 7.04 us
    reshape x18 -> x16, local copies, waits for them, and re-layouts: 37.1 us -> 6.32 us  [window(): return piece.reshape(channels, tile_rows * tile_cols)]
    slice x22 -> x20, local copies, waits for them, and re-layouts: 46.3 us -> 36.6 us  [window(): lax.slice(padded, (0, start_y, start_x), (channels, start_y + tile_rows,...]
    dot_general x45, matrix products: 22.4 us -> 17.9 us  [the longest x27 10.7 us: conv_taps(): lax.dot_general(kernel[offset_y, offset_x], patch, (((0 if flip else 1,),...]
    ppermute x2 -> x3, starting transfers between devices: 7.05 us -> 10.7 us  [padded_2(): lax.ppermute(tail, axis, [(i, (i + 1) % count) for i in range(ends)])]
    reshape x2 -> x0, local copies, waits for them, and re-layouts: 2.38 us -> none  [the longest x1 1.35 us: local(): hidden_grad = hidden_grad.reshape(channels, ext_rows, ext_cols)]
    ppermute x2 -> x3, starting transfers between devices: 5.01 us -> 6.93 us  [padded_2(): lax.ppermute(head, axis, [((i + 1) % count, i) for i in range(ends)])]
    concatenate x3 -> x4, other arithmetic: 3.74 us -> 5.2 us  [padded_2(): jnp.concatenate([lax.ppermute(tail, axis, [(i, (i + 1) % count) for i in...]
    unnamed x85 -> x89, local copies, waits for them, and re-layouts: 14.7 us -> 13.3 us
  transfers between devices with their start and end apart: 5 -> 7, of which waited for: 3 -> 3; matrix products, arithmetic and copies ran while one was open for 3% -> 16% of each run, Pallas kernels for 0% -> 0%
where the time goes in v4:
time: 150 us; the launch traced here: 149 us
  local copies, waits for them, and re-layouts  63.9 us (43%)
  starting transfers between devices  33.4 us (22%)
  waiting for transfers between devices  24.9 us (17%)
  matrix products  17.9 us (12%)
  other arithmetic  7.04 us (5%)
    slice x20, local copies, waits for them, and re-layouts, window(): lax.slice(padded, (0, start_y, start_x), (channels, start_y + tile_rows,...  36.6 us
    all_to_all x1, waiting for transfers between devices, reduce_weights(): spread = lax.all_to_all(stacked, ('row', 'col'), 1, 1, tiled=True)  19.8 us
    all_to_all x1, starting transfers between devices, reduce_weights(): spread = lax.all_to_all(stacked, ('row', 'col'), 1, 1, tiled=True)  15.8 us
    unnamed x89, local copies, waits for them, and re-layouts  13.3 us
    dot_general x27, matrix products, conv_taps(): lax.dot_general(kernel[offset_y, offset_x], patch, (((0 if flip else 1,),...  10.7 us
    ppermute x3, starting transfers between devices, padded_2(): lax.ppermute(tail, axis, [(i, (i + 1) % count) for i in range(ends)])  10.7 us
    dot_general x18, matrix products, kernel_grads(): lax.dot_general(upper, lower, (((1,), (1,)), ((), ())), preferred_element...  7.21 us
    ppermute x3, starting transfers between devices, padded_2(): lax.ppermute(head, axis, [((i + 1) % count, i) for i in range(ends)])  6.93 us
  transfers between devices with their start and end apart: 7, of which 3 were waited for; matrix products, arithmetic and copies ran while one was open for 16% of the time, Pallas kernels for 0%

profile of v4, /device:TPU:1, one launch (start us, length us, event | category | flops | bytes accessed | tf_op | source)
XLA Modules:
  0.0 148.7 jit_solution(6265046398522910356)
XLA Ops:
  2.9 4.0 %collective-permute-start = (bf16[192,2,256]{2,0,1:T(8,128)(2,1)S(1)}, bf16[192,2,256]{2,0,1:T(8,128)(2,1)S(1)}, u32[]{:S(2)}, u32[]{:S(2)}) collective-permute-start(bf16[192,2,256]{2,0,1:T(8,128)(2,1)S(1)} %get-tuple-element.47), channel_id=1, source_target_pairs={{0,8},{8,16},{16,24},{24,32},{32,40},{40,48},{48,56},{56,64},{64,7... | collective-permute-start | bytes 589832 | tf_op jit(solution)/shard_map/ppermute | solution.py:15
  9.2 1.3 collective-permute-done
  10.5 3.8 %collective-permute-done.1 = bf16[192,2,256]{2,0,1:T(8,128)(2,1)S(1)} collective-permute-done((bf16[192,2,256]{2,0,1:T(8,128)(2,1)S(1)}, bf16[192,2,256]{2,0,1:T(8,128)(2,1)S(1)}, u32[]{:S(2)}, u32[]{:S(2)}) %collective-permute-start.1) | collective-permute-done | bytes 196640 | tf_op jit(solution)/shard_map/ppermute | solution.py:17
  16.2 3.7 %collective-permute-start.2 = (bf16[192,12,1]{0,1,2:T(8,128)(2,1)S(1)}, bf16[192,12,1]{0,1,2:T(8,128)(2,1)S(1)}, u32[]{:S(2)}, u32[]{:S(2)}) collective-permute-start(bf16[192,12,1]{0,1,2:T(8,128)(2,1)S(1)} %copy.58), channel_id=1, source_target_pairs={{1,0},{2,1},{3,2},{4,3},{5,4},{6,5},{7,6},{9,8},{10,9},{11,10},{12... | collective-permute-start | bytes 13832 | tf_op jit(solution)/shard_map/ppermute | solution.py:17
  20.3 3.0 %collective-permute-start.3 = (bf16[192,12,1]{0,1,2:T(8,128)(2,1)S(1)}, bf16[192,12,1]{0,1,2:T(8,128)(2,1)S(1)}, u32[]{:S(2)}, u32[]{:S(2)}) collective-permute-start(bf16[192,12,1]{0,1,2:T(8,128)(2,1)S(1)} %copy.62), channel_id=1, source_target_pairs={{0,1},{1,2},{2,3},{3,4},{4,5},{5,6},{6,7},{8,9},{9,10},{10,11},{11... | collective-permute-start | bytes 13832 | tf_op jit(solution)/shard_map/ppermute | solution.py:15
  25.5 2.1 %copy.72 = bf16[96,10,256]{0,2,1:T(8,128)(2,1)} copy(bf16[96,10,256]{2,0,1:T(8,128)(2,1)} %get-tuple-element.46) | data formatting | bytes 983040 | tf_op jit(solution)/shard_map/slice | solution.py:26
  27.6 2.1 %copy.75 = bf16[96,10,256]{0,2,1:T(8,128)(2,1)} copy(bf16[96,10,256]{2,0,1:T(8,128)(2,1)} %get-tuple-element.29) | data formatting | bytes 983040 | tf_op jit(solution)/shard_map/slice | solution.py:26
  31.9 1.4 copy.66
  33.6 1.9 %copy.101 = bf16[8,12,8,256]{3,2,0,1:T(8,128)(2,1)} copy(bf16[8,12,8,256]{3,2,1,0:T(8,128)(2,1)} %get-tuple-element.44) | data formatting | bytes 786432 | tf_op jit(solution)/shard_map/reshape | solution.py:29
  35.5 1.8 %copy.106 = bf16[8,12,8,256]{3,2,0,1:T(8,128)(2,1)} copy(bf16[8,12,8,256]{3,2,1,0:T(8,128)(2,1)} %get-tuple-element.35) | data formatting | bytes 786432 | tf_op jit(solution)/shard_map/reshape | solution.py:29
  40.3 2.6 %maximum_maximum_fusion = (bf16[192,12,257]{2,0,1:T(8,128)(2,1)S(1)}, bf16[192,12,257]{2,0,1:T(8,128)(2,1)S(1)}) fusion(bf16[192,2,256]{2,0,1:T(8,128)(2,1)S(1)} %collective-permute-done.1, bf16[192,8,256]{2,0,1:T(8,128)(2,1)S(1)} %copy_dynamic-update-slice_fusion, bf16[192,2,256]{2,0,1:T(8,128)(2,1)S(1)} %collective-permute-done, ...), kind=kLoop, calls=%fused_computation.35 | loop fusion | flops 9474048 | bytes 3557376 | tf_op jit(solution)/shard_map/concatenate | solution.py:13
  42.9 3.6 %fusion.117 = (bf16[96,10,256]{2,0,1:T(8,128)(2,1)}, bf16[96,10,256]{2,0,1:T(8,128)(2,1)}, bf16[96,10,256]{2,0,1:T(8,128)(2,1)}, bf16[96,10,256]{2,0,1:T(8,128)(...) fusion(bf16[192,12,257]{2,0,1:T(8,128)(2,1)S(1)} %get-tuple-ele, ...), kind=kLoop, calls=%fused_computation.209 | loop fusion | bytes 11796480 | tf_op jit(solution)/shard_map/slice | solution.py:26
  46.5 2.9 %slice_bitcast_fusion.6 = (bf16[8,12,8,256]{3,2,1,0:T(8,128)(2,1)}, bf16[8,12,8,256]{3,2,1,0:T(8,128)(2,1)}, bf16[8,12,8,256]{3,2,1,0:T(8,128)(2,1)}, bf16[8,12,...) fusion(bf16[192,12,257]{2,0,1:T(8,128)(2,1)S(1)} %get-tuple-ele, ...), kind=kLoop, calls=%fused_computation.119 | loop fusion | bytes 9437184
  49.4 1.4 copy.71
  50.7 2.1 %copy.73 = bf16[96,10,256]{0,2,1:T(8,128)(2,1)} copy(bf16[96,10,256]{2,0,1:T(8,128)(2,1)} %get-tuple-element.19) | data formatting | bytes 983040 | tf_op jit(solution)/shard_map/slice | solution.py:26
  52.9 2.1 %copy.74 = bf16[96,10,256]{0,2,1:T(8,128)(2,1)} copy(bf16[96,10,256]{2,0,1:T(8,128)(2,1)} %get-tuple-element.73) | data formatting | bytes 983040 | tf_op jit(solution)/shard_map/slice | solution.py:26
  55.0 2.1 %copy.76 = bf16[96,10,256]{0,2,1:T(8,128)(2,1)} copy(bf16[96,10,256]{2,0,1:T(8,128)(2,1)} %get-tuple-element.18) | data formatting | bytes 983040 | tf_op jit(solution)/shard_map/slice | solution.py:26
  57.1 2.2 %copy.77 = bf16[96,10,256]{0,2,1:T(8,128)(2,1)} copy(bf16[96,10,256]{2,0,1:T(8,128)(2,1)} %get-tuple-element.74) | data formatting | bytes 983040 | tf_op jit(solution)/shard_map/slice | solution.py:26
  59.3 2.1 %copy.79 = bf16[96,10,256]{0,2,1:T(8,128)(2,1)} copy(bf16[96,10,256]{2,0,1:T(8,128)(2,1)} %get-tuple-element.17) | data formatting | bytes 983040 | tf_op jit(solution)/shard_map/slice | solution.py:26
  61.4 2.1 %copy.60 = bf16[96,10,256]{0,2,1:T(8,128)(2,1)} copy(bf16[96,10,256]{2,0,1:T(8,128)(2,1)} %get-tuple-element.22) | data formatting | bytes 983040 | tf_op jit(solution)/shard_map/slice | solution.py:26
  63.5 2.1 %copy.64 = bf16[96,10,256]{0,2,1:T(8,128)(2,1)} copy(bf16[96,10,256]{2,0,1:T(8,128)(2,1)} %get-tuple-element.69) | data formatting | bytes 983040 | tf_op jit(solution)/shard_map/slice | solution.py:26
  65.6 2.2 %copy.65 = bf16[96,10,256]{0,2,1:T(8,128)(2,1)} copy(bf16[96,10,256]{2,0,1:T(8,128)(2,1)} %get-tuple-element.21) | data formatting | bytes 983040 | tf_op jit(solution)/shard_map/slice | solution.py:26
  67.8 2.2 %copy.67 = bf16[96,10,256]{0,2,1:T(8,128)(2,1)} copy(bf16[96,10,256]{2,0,1:T(8,128)(2,1)} %get-tuple-element.70) | data formatting | bytes 983040 | tf_op jit(solution)/shard_map/slice | solution.py:26
  71.1 2.2 %copy.70 = bf16[96,10,256]{0,2,1:T(8,128)(2,1)} copy(bf16[96,10,256]{2,0,1:T(8,128)(2,1)} %get-tuple-element.71) | data formatting | bytes 983040 | tf_op jit(solution)/shard_map/slice | solution.py:26
  91.1 1.3 fusion.21
  92.4 1.3 fusion.20
  99.5 1.9 %collective-permute-start.4 = (bf16[96,10,1]{0,2,1:T(2,128)(2,1)S(1)}, bf16[96,10,1]{0,2,1:T(2,128)(2,1)S(1)}, u32[]{:S(2)}, u32[]{:S(2)}) collective-permute-start(bf16[96,10,1]{0,2,1:T(2,128)(2,1)S(1)} %get-tuple-element.62), channel_id=1, source_target_pairs={{1,0},{2,1},{3,2},{4,3},{5,4},{6,5},{7,6},{9,8},{10,9},{11,10},{12... | collective-permute-start | bytes 5768 | tf_op jit(solution)/shard_map/ppermute | solution.py:17
  101.5 3.6 %collective-permute-start.5 = (bf16[96,10,1]{0,2,1:T(2,128)(2,1)S(1)}, bf16[96,10,1]{0,2,1:T(2,128)(2,1)S(1)}, u32[]{:S(2)}, u32[]{:S(2)}) collective-permute-start(bf16[96,10,1]{0,2,1:T(2,128)(2,1)S(1)} %get-tuple-element.61), channel_id=1, source_target_pairs={{0,1},{1,2},{2,3},{3,4},{4,5},{5,6},{6,7},{8,9},{9,10},{10,11},{11... | collective-permute-start | bytes 5768 | tf_op jit(solution)/shard_map/ppermute | solution.py:15
  105.2 1.5 %copy.98 = f32[2,256,324]{2,0,1:T(2,128)} copy(f32[2,256,324]{2,1,0:T(8,128)S(1)} %pad_maximum_fusion.2) | data formatting | bytes 1327104 | tf_op jit(solution)/shard_map/stack | solution.py:62
  106.7 15.8 %all-to-all-start = ((f32[2,256,324]{2,0,1:T(2,128)}), f32[2,256,324]{2,0,1:T(2,128)S(1)}, u32[]{:S(2)}, u32[]{:S(2)}) async-start(f32[2,256,324]{2,0,1:T(2,128)} %copy.98), calls=%async_computation | async-start | bytes 1572864 | tf_op jit(solution)/shard_map/all_to_all | solution.py:63
  122.5 1.5 %pad_maximum_fusion.3 = (bf16[96,8,256]{0,2,1:T(8,128)(2,1)S(1)}, bf16[96,8,256]{0,2,1:T(8,128)(2,1)S(1)}, bf16[96,8,256]{0,2,1:T(8,128)(2,1)S(1)}, bf16[96,8,25...) fusion(bf16[96,10,256]{0,2,1:T(8,128)(2,1)S(1)} %bitcast.301, ...), kind=kLoop, calls=%fused_computation.99 | loop fusion | flops 4718592 | bytes 5777408 | tf_op jit(solution)/shard_map/concatenate | solution.py:13
  128.0 19.8 %all-to-all-done = f32[2,256,324]{2,0,1:T(2,128)S(1)} async-done(((f32[2,256,324]{2,0,1:T(2,128)}), f32[2,256,324]{2,0,1:T(2,128)S(1)}, u32[]{:S(2)}, u32[]{:S(2)}) %all-to-all-start) | async-done | bytes 663584 | tf_op jit(solution)/shard_map/all_to_all | solution.py:63
  (176 shorter events, 43.5 us)
Async XLA Ops:
  0.6 7.6 %copy-start.25 = (bf16[96,8,256]{2,1,0:T(8,128)(2,1)S(1)}, bf16[96,8,256]{2,1,0:T(8,128)(2,1)}, u32[]{:S(2)}) copy-start(bf16[96,8,256]{2,1,0:T(8,128)(2,1)} %param.5) | copy-start | bytes 1179652
  0.6 8.5 %copy-start.26 = (bf16[96,8,256]{2,1,0:T(8,128)(2,1)S(1)}, bf16[96,8,256]{2,1,0:T(8,128)(2,1)}, u32[]{:S(2)}) copy-start(bf16[96,8,256]{2,1,0:T(8,128)(2,1)} %param.6) | copy-start | bytes 1179652
  2.9 7.6 %collective-permute-start = (bf16[192,2,256]{2,0,1:T(8,128)(2,1)S(1)}, bf16[192,2,256]{2,0,1:T(8,128)(2,1)S(1)}, u32[]{:S(2)}, u32[]{:S(2)}) collective-permute-start(bf16[192,2,256]{2,0,1:T(8,128)(2,1)S(1)} %get-tuple-element.47), channel_id=1, source_target_pairs={{0,8},{8,16},{16,24},{24,32},{32,40},{40,48},{48,56},{56,64},{64,7... | collective-permute-start | bytes 589832 | tf_op jit(solution)/shard_map/ppermute | solution.py:15
  6.9 7.4 %collective-permute-start.1 = (bf16[192,2,256]{2,0,1:T(8,128)(2,1)S(1)}, bf16[192,2,256]{2,0,1:T(8,128)(2,1)S(1)}, u32[]{:S(2)}, u32[]{:S(2)}) collective-permute-start(bf16[192,2,256]{2,0,1:T(8,128)(2,1)S(1)} %get-tuple-element.48), channel_id=1, source_target_pairs={{8,0},{16,8},{24,16},{32,24},{40,32},{48,40},{56,48},{64,56},{72,6... | collective-permute-start | bytes 589832 | tf_op jit(solution)/shard_map/ppermute | solution.py:17
  16.2 22.6 %collective-permute-start.2 = (bf16[192,12,1]{0,1,2:T(8,128)(2,1)S(1)}, bf16[192,12,1]{0,1,2:T(8,128)(2,1)S(1)}, u32[]{:S(2)}, u32[]{:S(2)}) collective-permute-start(bf16[192,12,1]{0,1,2:T(8,128)(2,1)S(1)} %copy.58), channel_id=1, source_target_pairs={{1,0},{2,1},{3,2},{4,3},{5,4},{6,5},{7,6},{9,8},{10,9},{11,10},{12... | collective-permute-start | bytes 13832 | tf_op jit(solution)/shard_map/ppermute | solution.py:17
  20.3 18.9 %collective-permute-start.3 = (bf16[192,12,1]{0,1,2:T(8,128)(2,1)S(1)}, bf16[192,12,1]{0,1,2:T(8,128)(2,1)S(1)}, u32[]{:S(2)}, u32[]{:S(2)}) collective-permute-start(bf16[192,12,1]{0,1,2:T(8,128)(2,1)S(1)} %copy.62), channel_id=1, source_target_pairs={{0,1},{1,2},{2,3},{3,4},{4,5},{5,6},{6,7},{8,9},{9,10},{10,11},{11... | collective-permute-start | bytes 13832 | tf_op jit(solution)/shard_map/ppermute | solution.py:15
  33.6 3.7 %copy-start.31 = (bf16[8,12,8,256]{3,2,1,0:T(8,128)(2,1)S(1)}, bf16[8,12,8,256]{3,2,1,0:T(8,128)(2,1)}, u32[]{:S(2)}) copy-start(bf16[8,12,8,256]{3,2,1,0:T(8,128)(2,1)} %get-tuple-element.36) | copy-start | bytes 1179652
  33.6 4.5 %copy-start.30 = (bf16[8,12,8,256]{3,2,1,0:T(8,128)(2,1)S(1)}, bf16[8,12,8,256]{3,2,1,0:T(8,128)(2,1)}, u32[]{:S(2)}) copy-start(bf16[8,12,8,256]{3,2,1,0:T(8,128)(2,1)} %get-tuple-element.43) | copy-start | bytes 1179652
  71.1 4.1 %copy-start.3 = (bf16[96,10,256]{0,2,1:T(8,128)(2,1)S(1)}, bf16[96,10,256]{0,2,1:T(8,128)(2,1)}, u32[]{:S(2)}) copy-start(bf16[96,10,256]{0,2,1:T(8,128)(2,1)} %copy.72) | copy-start | bytes 1474564
  73.2 1.9 %copy-start.32 = (bf16[3,3,96,96]{3,2,1,0:T(8,128)(2,1)S(1)}, bf16[3,3,96,96]{3,2,1,0:T(8,128)(2,1)}, u32[]{:S(2)}) copy-start(bf16[3,3,96,96]{3,2,1,0:T(8,128)(2,1)} %param.7) | copy-start | bytes 497668
  74.0 1.5 %copy-start.12 = (bf16[96,10,256]{0,2,1:T(8,128)(2,1)S(1)}, bf16[96,10,256]{0,2,1:T(8,128)(2,1)}, u32[]{:S(2)}) copy-start(bf16[96,10,256]{0,2,1:T(8,128)(2,1)} %copy.73) | copy-start | bytes 1474564
  75.9 1.1 copy-start.2
  78.9 1.1 copy-start.13
  80.4 1.2 copy-start
  82.0 1.1 copy-start.6
  87.1 3.7 %copy-start.35 = (bf16[96,2560]{1,0:T(8,128)(2,1)}, bf16[96,2560]{1,0:T(8,128)(2,1)S(1)}, u32[]{:S(2)}) copy-start(bf16[96,2560]{1,0:T(8,128)(2,1)S(1)} %fusion.6) | copy-start | bytes 1474564
  87.1 1.2 copy-start.24
  87.1 1.3 copy-start.23
  87.1 1.4 copy-start.22
  87.5 1.2 copy-start.21
  88.7 1.6 %copy-start.36 = (bf16[12,8,8,256]{3,1,2,0:T(8,128)(2,1)S(1)}, bf16[12,8,8,256]{3,1,2,0:T(8,128)(2,1)}, u32[]{:S(2)}) copy-start(bf16[12,8,8,256]{3,1,2,0:T(8,128)(2,1)} %copy.118) | copy-start | bytes 1179652
  91.1 3.9 %copy-start.19 = (bf16[8,12,8,256]{3,2,1,0:T(8,128)(2,1)S(1)}, bf16[8,12,8,256]{3,2,1,0:T(8,128)(2,1)}, u32[]{:S(2)}) copy-start(bf16[8,12,8,256]{3,2,1,0:T(8,128)(2,1)} %get-tuple-element.8) | copy-start | bytes 1179652
  92.4 2.6 %copy-start.18 = (bf16[8,12,8,256]{3,2,1,0:T(8,128)(2,1)S(1)}, bf16[8,12,8,256]{3,2,1,0:T(8,128)(2,1)}, u32[]{:S(2)}) copy-start(bf16[8,12,8,256]{3,2,1,0:T(8,128)(2,1)} %get-tuple-element.65) | copy-start | bytes 1179652
  93.7 1.4 copy-start.17
  93.8 1.3 copy-start.16
  95.1 1.5 %copy-start.28 = (bf16[8,12,8,256]{3,2,0,1:T(8,128)(2,1)S(1)}, bf16[8,12,8,256]{3,2,0,1:T(8,128)(2,1)}, u32[]{:S(2)}) copy-start(bf16[8,12,8,256]{3,2,0,1:T(8,128)(2,1)} %copy.109) | copy-start | bytes 1179652
  97.3 1.2 copy-start.27
  98.4 6.7 %copy-start.29 = (f32[1,256,324]{2,1,0:T(8,128)S(1)}, f32[1,256,324]{2,1,0:T(8,128)}, u32[]{:S(2)}) copy-start(f32[1,256,324]{2,1,0:T(8,128)} %mul.49) | copy-start | bytes 995332
  99.5 22.9 %collective-permute-start.4 = (bf16[96,10,1]{0,2,1:T(2,128)(2,1)S(1)}, bf16[96,10,1]{0,2,1:T(2,128)(2,1)S(1)}, u32[]{:S(2)}, u32[]{:S(2)}) collective-permute-start(bf16[96,10,1]{0,2,1:T(2,128)(2,1)S(1)} %get-tuple-element.62), channel_id=1, source_target_pairs={{1,0},{2,1},{3,2},{4,3},{5,4},{6,5},{7,6},{9,8},{10,9},{11,10},{12... | collective-permute-start | bytes 5768 | tf_op jit(solution)/shard_map/ppermute | solution.py:17
  101.5 21.0 %collective-permute-start.5 = (bf16[96,10,1]{0,2,1:T(2,128)(2,1)S(1)}, bf16[96,10,1]{0,2,1:T(2,128)(2,1)S(1)}, u32[]{:S(2)}, u32[]{:S(2)}) collective-permute-start(bf16[96,10,1]{0,2,1:T(2,128)(2,1)S(1)} %get-tuple-element.61), channel_id=1, source_target_pairs={{0,1},{1,2},{2,3},{3,4},{4,5},{5,6},{6,7},{8,9},{9,10},{10,11},{11... | collective-permute-start | bytes 5768 | tf_op jit(solution)/shard_map/ppermute | solution.py:15
  106.7 41.1 %all-to-all-start = ((f32[2,256,324]{2,0,1:T(2,128)}), f32[2,256,324]{2,0,1:T(2,128)S(1)}, u32[]{:S(2)}, u32[]{:S(2)}) async-start(f32[2,256,324]{2,0,1:T(2,128)} %copy.98), calls=%async_computation | async-start | bytes 1572864 | tf_op jit(solution)/shard_map/all_to_all | solution.py:63
  122.5 1.6 %copy-start.33 = (bf16[3,3,96,96]{3,2,1,0:T(8,128)(2,1)S(1)}, bf16[3,3,96,96]{3,2,1,0:T(8,128)(2,1)}, u32[]{:S(2)}) copy-start(bf16[3,3,96,96]{3,2,1,0:T(8,128)(2,1)} %param.7) | copy-start | bytes 497668
  (17 other events, 18.7 us)

commit v5 on v1

--- a/solution.py
+++ b/solution.py
@@ -51,10 +51,10 @@
 
 
 def reduce_weights(grads):
-    shards = lax.axis_size("row") * lax.axis_size("col")
-    stacked = jnp.stack(grads).reshape(len(grads), shards, -1)
-    spread = lax.all_to_all(stacked, ("row", "col"), 1, 1, tiled=True)
-    summed = spread.sum(axis=1)
+    rows, cols = lax.axis_size("row"), lax.axis_size("col")
+    stacked = jnp.stack(grads).reshape(len(grads), rows, cols, -1)
+    stacked = lax.all_to_all(stacked, "col", 2, 2, tiled=True).sum(axis=2)
+    summed = lax.all_to_all(stacked, "row", 1, 1, tiled=True).sum(axis=1)
     return (summed[0], summed[1])
 
 
@@ -62,8 +62,10 @@
     channels, tile_rows, tile_cols = features.shape
     cell_count = tile_rows * tile_cols
     scale = float(cell_count * lax.axis_size("row") * lax.axis_size("col")) ** (-0.5)
-    padded_input = padded_2(features, (("row", 1), ("col", 2)), 1)
-    padded_cot = padded_2(cotangent, (("row", 1), ("col", 2)), 1)
+    padded_both = padded_2(
+        jnp.concatenate([features, cotangent], axis=0), (("row", 1), ("col", 2)), 1
+    )
+    padded_input, padded_cot = padded_both[:channels], padded_both[channels:]
     hidden = jnp.zeros((channels, cell_count), jnp.float32)
     for offset_y in range(3):
         for offset_x in range(3):

time: 120 us -> 105 us (0.88)
  starting transfers between devices: 58.5 us -> 44 us
  waiting for transfers between devices: 24 us -> 18.4 us
  matrix products: 13.7 us -> 17.7 us
  local copies, waits for them, and re-layouts: 14.6 us -> 17 us
  other arithmetic: 7.03 us -> 5.79 us
    ppermute x6 -> x4, starting transfers between devices: 24.2 us -> 13.2 us  [padded_2(): lax.ppermute(tail, axis, [(i, (i + 1) % count) for i in range(ends)])]
    all_to_all x1 -> x2, waiting for transfers between devices: 19.6 us -> 14.6 us  [the longest x1 7.94 us: reduce_weights(): summed = lax.all_to_all(stacked, 'row', 1, 1, tiled=True).sum(axis=1)]
    all_to_all x1 -> x2, starting transfers between devices: 24.1 us -> 20.8 us  [the longest x1 14.9 us: reduce_weights(): summed = lax.all_to_all(stacked, 'row', 1, 1, tiled=True).sum(axis=1)]
    concatenate x6 -> x2, other arithmetic: 5.72 us -> 2.44 us  [padded_2(): jnp.concatenate([lax.ppermute(tail, axis, [(i, (i + 1) % count) for i in...]
    ppermute x0 -> x2, local copies, waits for them, and re-layouts: none -> 2.82 us  [the longest x1 1.76 us: padded_2(): lax.ppermute(tail, axis, [(i, (i + 1) % count) for i in range(ends)])]
    dot_general x9, matrix products: 2.49 us -> 4.83 us  [local(): jnp.dot(weight_one[offset_y, offset_x], patch, preferred_element_type=jnp...]
    slice x2 -> x0, local copies, waits for them, and re-layouts: 2.05 us -> none  [window(): lax.slice(padded, (0, start_y, start_x), (channels, start_y + tile_rows,...]
    slice x4 -> x3, local copies, waits for them, and re-layouts: 3 us -> 1.14 us  [padded_2(): lax.slice_in_dim(cells, cells.shape[dim] - width, cells.shape[dim], axis=...]
  transfers between devices with their start and end apart: 13 -> 10, of which waited for: 5 -> 6; matrix products, arithmetic and copies ran while one was open for 16% -> 18% of each run, Pallas kernels for 0% -> 0%
where the time goes in v5:
time: 105 us; the launch traced here: 104 us
  starting transfers between devices  44 us (42%)
  waiting for transfers between devices  18.4 us (18%)
  matrix products  17.7 us (17%)
  local copies, waits for them, and re-layouts  17 us (16%)
  other arithmetic  5.79 us (6%)
  between operations  1.52 us (1%)
    all_to_all x1, starting transfers between devices, reduce_weights(): summed = lax.all_to_all(stacked, 'row', 1, 1, tiled=True).sum(axis=1)  14.9 us
    ppermute x4, starting transfers between devices, padded_2(): lax.ppermute(tail, axis, [(i, (i + 1) % count) for i in range(ends)])  13.2 us
    ppermute x4, starting transfers between devices, padded_2(): lax.ppermute(head, axis, [((i + 1) % count, i) for i in range(ends)])  9.9 us
    all_to_all x1, waiting for transfers between devices, reduce_weights(): summed = lax.all_to_all(stacked, 'row', 1, 1, tiled=True).sum(axis=1)  7.94 us
    dot_general x18, matrix products, backward_taps(): lax.dot_general(kernel[offset_y, offset_x], patch, (((0,), (0,)), ((), ()...  7.52 us
    all_to_all x1, waiting for transfers between devices, reduce_weights(): stacked = lax.all_to_all(stacked, 'col', 2, 2, tiled=True).sum(axis=2)  6.68 us
    unnamed x38, local copies, waits for them, and re-layouts  6.63 us
    all_to_all x1, starting transfers between devices, reduce_weights(): stacked = lax.all_to_all(stacked, 'col', 2, 2, tiled=True).sum(axis=2)  5.9 us
  transfers between devices with their start and end apart: 10, of which 6 were waited for; matrix products, arithmetic and copies ran while one was open for 18% of the time, Pallas kernels for 0%

profile of v5, /device:TPU:1, one launch (start us, length us, event | category | flops | bytes accessed | tf_op | source)
XLA Modules:
  0.0 104.4 jit_solution(14865398300756227678)
XLA Ops:
  0.6 1.1 %constant_dynamic-update-slice_fusion = bf16[192,8,256]{2,0,1:T(8,128)(2,1)S(1)} fusion(bf16[96,8,256]{2,1,0:T(8,128)(2,1)} %param.5), kind=kLoop, calls=%fused_computation.123 | loop fusion | bytes 786432
  1.8 1.1 %copy_dynamic-update-slice_fusion = bf16[192,8,256]{2,0,1:T(8,128)(2,1)S(1)} fusion(bf16[192,8,256]{2,0,1:T(8,128)(2,1)S(1)} %constant_dynamic-update-slice_fusion, bf16[96,8,256]{2,1,0:T(8,128)(2,1)} %param.6), kind=kLoop, calls=%fused_computation.118 | loop fusion | bytes 786432 | tf_op jit(solution)/shard_map/concatenate | solution.py:66
  3.0 4.0 %collective-permute-start = (bf16[192,1,256]{2,0,1:T(8,128)(2,1)S(1)}, bf16[192,1,256]{2,0,1:T(8,128)(2,1)S(1)}, u32[]{:S(2)}, u32[]{:S(2)}) collective-permute-start(bf16[192,1,256]{2,0,1:T(8,128)(2,1)S(1)} %get-tuple-element.27), channel_id=1, source_target_pairs={{0,8},{8,16},{16,24},{24,32},{32,40},{40,48},{48,56},{56,64},{64,7... | collective-permute-start | bytes 294920 | tf_op jit(solution)/shard_map/ppermute | solution.py:15
  7.0 1.3 %collective-permute-start.1 = (bf16[192,1,256]{2,0,1:T(8,128)(2,1)S(1)}, bf16[192,1,256]{2,0,1:T(8,128)(2,1)S(1)}, u32[]{:S(2)}, u32[]{:S(2)}) collective-permute-start(bf16[192,1,256]{2,0,1:T(8,128)(2,1)S(1)} %get-tuple-element.28), channel_id=1, source_target_pairs={{8,0},{16,8},{24,16},{32,24},{40,32},{48,40},{56,48},{64,56},{72,6... | collective-permute-start | bytes 294920 | tf_op jit(solution)/shard_map/ppermute | solution.py:17
  8.4 1.9 %fusion.53 = f32[96,2048]{1,0:T(8,128)} fusion(bf16[96,2048]{1,0:T(8,128)(2,1)S(1)} %bitcast.351, bf16[3,3,96,96]{3,2,1,0:T(8,128)(2,1)} %param.7), kind=kOutput, calls=%fused_computation.140 | convolution fusion | flops 37748736 | bytes 1204224 | tf_op jit(solution)/shard_map/dot_general | solution.py:73
  10.4 2.0 %collective-permute-done.1 = bf16[192,1,256]{2,0,1:T(8,128)(2,1)S(1)} collective-permute-done((bf16[192,1,256]{2,0,1:T(8,128)(2,1)S(1)}, bf16[192,1,256]{2,0,1:T(8,128)(2,1)S(1)}, u32[]{:S(2)}, u32[]{:S(2)}) %collective-permute-start.1) | collective-permute-done | bytes 98336 | tf_op jit(solution)/shard_map/ppermute | solution.py:17
  13.1 4.0 %collective-permute-start.2 = (bf16[192,10,1]{0,1,2:T(8,128)(2,1)S(1)}, bf16[192,10,1]{0,1,2:T(8,128)(2,1)S(1)}, u32[]{:S(2)}, u32[]{:S(2)}) collective-permute-start(bf16[192,10,1]{0,1,2:T(8,128)(2,1)S(1)} %copy.122), channel_id=1, source_target_pairs={{1,0},{2,1},{3,2},{4,3},{5,4},{6,5},{7,6},{9,8},{10,9},{11,10},{12... | collective-permute-start | bytes 11528 | tf_op jit(solution)/shard_map/ppermute | solution.py:17
  17.1 1.0 copy.126
  18.1 3.0 %collective-permute-start.3 = (bf16[192,10,1]{0,1,2:T(8,128)(2,1)}, bf16[192,10,1]{0,1,2:T(8,128)(2,1)}, u32[]{:S(2)}, u32[]{:S(2)}) collective-permute-start(bf16[192,10,1]{0,1,2:T(8,128)(2,1)} %copy.126), channel_id=1, source_target_pairs={{0,1},{1,2},{2,3},{3,4},{4,5},{5,6},{6,7},{8,9},{9,10},{10,11},{11... | collective-permute-start | bytes 11528 | tf_op jit(solution)/shard_map/ppermute | solution.py:15
  21.3 1.0 convolution_bitcast_fusion.1
  22.3 2.0 %convolution_bitcast_fusion.5 = f32[96,2048]{1,0:T(8,128)} fusion(bf16[96,2048]{1,0:T(8,128)(2,1)S(1)} %bitcast.353, bf16[3,3,96,96]{3,2,1,0:T(8,128)(2,1)} %param.9), kind=kOutput, calls=%fused_computation.5 | convolution fusion | flops 37748736 | bytes 1204224 | tf_op jit(solution)/shard_map/dot_general | solution.py:39
  24.3 0.8 copy.178
  25.1 1.1 %copy.123 = bf16[192,10,1]{2,0,1:T(8,128)(2,1)} copy(bf16[192,10,1]{0,1,2:T(8,128)(2,1)S(1)} %collective-permute-done.2) | data formatting | bytes 7680 | tf_op jit(solution)/shard_map/ppermute | solution.py:17
  26.2 1.8 %copy.127 = bf16[192,10,1]{2,0,1:T(8,128)(2,1)} copy(bf16[192,10,1]{0,1,2:T(8,128)(2,1)} %collective-permute-done.3) | data formatting | bytes 7680 | tf_op jit(solution)/shard_map/ppermute | solution.py:15
  28.0 2.3 %pad_maximum_fusion = (bf16[192,10,257]{2,0,1:T(8,128)(2,1)S(1)}, bf16[192,10,257]{2,0,1:T(8,128)(2,1)S(1)}) fusion(bf16[192,10,1]{2,0,1:T(8,128)(2,1)} %copy.123, bf16[192,1,256]{2,0,1:T(8,128)(2,1)} %copy-done.8, bf16[192,8,256]{2,0,1:T(8,128)(2,1)S(1)} %copy_dynamic-update-slice_fusion, bf16[192,1,256]{2,0,1:T(8,128)(2,1)} %copy-done.7, ...), kind=kLoop, calls=%fused_computation.41 | loop fusion | flops 7895040 | bytes 2964480 | tf_op jit(solution)/shard_map/concatenate | solution.py:13
  30.3 1.1 %slice_bitcast_fusion.4 = (bf16[8,12,8,256]{3,2,1,0:T(8,128)(2,1)S(1)}, bf16[8,12,8,256]{3,2,1,0:T(8,128)(2,1)S(1)}, bf16[8,12,8,256]{3,2,1,0:T(8,128)(2,1)S(1)}...) fusion(bf16[192,10,257]{2,0,1:T(8,128)(2,1)S(1)} %get-tuple-ele, ...), kind=kLoop, calls=%fused_computation.104 | loop fusion | bytes 9437184
  36.6 0.8 copy-done.1
  38.1 0.7 copy-done.9
  39.5 3.2 %collective-permute-start.4 = (bf16[96,1,256]{2,0,1:T(8,128)(2,1)S(1)}, bf16[96,1,256]{2,0,1:T(8,128)(2,1)S(1)}, u32[]{:S(2)}, u32[]{:S(2)}) collective-permute-start(bf16[96,1,256]{2,0,1:T(8,128)(2,1)S(1)} %get-tuple-element.44), channel_id=1, source_target_pairs={{0,8},{8,16},{16,24},{24,32},{32,40},{40,48},{48,56},{56,64},{64,7... | collective-permute-start | bytes 147464 | tf_op jit(solution)/shard_map/ppermute | solution.py:15
  42.7 1.3 %collective-permute-start.5 = (bf16[96,1,256]{2,0,1:T(8,128)(2,1)S(1)}, bf16[96,1,256]{2,0,1:T(8,128)(2,1)S(1)}, u32[]{:S(2)}, u32[]{:S(2)}) collective-permute-start(bf16[96,1,256]{2,0,1:T(8,128)(2,1)S(1)} %get-tuple-element.43), channel_id=1, source_target_pairs={{8,0},{16,8},{24,16},{32,24},{40,32},{48,40},{56,48},{64,56},{72,6... | collective-permute-start | bytes 147464 | tf_op jit(solution)/shard_map/ppermute | solution.py:17
  47.7 3.3 %collective-permute-start.6 = (bf16[96,10,1]{2,0,1:T(8,128)(2,1)S(1)}, bf16[96,10,1]{2,0,1:T(8,128)(2,1)S(1)}, u32[]{:S(2)}, u32[]{:S(2)}) collective-permute-start(bf16[96,10,1]{2,0,1:T(8,128)(2,1)S(1)} %get-tuple-element.39), channel_id=1, source_target_pairs={{1,0},{2,1},{3,2},{4,3},{5,4},{6,5},{7,6},{9,8},{10,9},{11,10},{12... | collective-permute-start | bytes 5768 | tf_op jit(solution)/shard_map/ppermute | solution.py:17
  51.0 3.0 %collective-permute-start.7 = (bf16[96,10,1]{2,0,1:T(8,128)(2,1)S(1)}, bf16[96,10,1]{2,0,1:T(8,128)(2,1)S(1)}, u32[]{:S(2)}, u32[]{:S(2)}) collective-permute-start(bf16[96,10,1]{2,0,1:T(8,128)(2,1)S(1)} %get-tuple-element.38), channel_id=1, source_target_pairs={{0,1},{1,2},{2,3},{3,4},{4,5},{5,6},{6,7},{8,9},{9,10},{10,11},{11... | collective-permute-start | bytes 5768 | tf_op jit(solution)/shard_map/ppermute | solution.py:15
  54.1 0.8 copy.186
  54.9 0.9 collective-permute-done.6
  59.9 1.0 pad_maximum_fusion.2
  60.9 5.9 %all-to-all-start = ((f32[2,32,8,324]{3,1,0,2:T(8,128)}), f32[2,32,8,324]{3,1,0,2:T(8,128)S(1)}, u32[]{:S(2)}, u32[]{:S(2)}) async-start(f32[2,32,8,324]{3,1,0,2:T(8,128)} %pad_maximum_fusion.2), calls=%async_computation | async-start | bytes 1572864 | tf_op jit(solution)/shard_map/all_to_all | solution.py:56
  66.8 2.1 %fusion.43 = (bf16[8,12,8,256]{3,2,1,0:T(8,128)(2,1)S(1)}, bf16[8,12,8,256]{3,2,1,0:T(8,128)(2,1)S(1)}, bf16[8,12,8,256]{3,2,1,0:T(8,128)(2,1)S(1)}, bf16[8,12,8...) fusion(bf16[96,10,256]{2,0,1:T(8,128)(2,1)S(1)} %get-tuple-element.48, ...), kind=kLoop, calls=%fused_computation.122 | loop fusion | flops 4718592 | bytes 2854656
  72.2 6.7 %all-to-all-done = f32[2,32,8,324]{3,1,0,2:T(8,128)S(1)} async-done(((f32[2,32,8,324]{3,1,0,2:T(8,128)}), f32[2,32,8,324]{3,1,0,2:T(8,128)S(1)}, u32[]{:S(2)}, u32[]{:S(2)}) %all-to-all-start) | async-done | bytes 663584 | tf_op jit(solution)/shard_map/all_to_all | solution.py:56
  79.0 0.7 copy.166
  79.7 14.9 %all-to-all-start.1 = ((f32[2,32,324]{2,0,1:T(2,128)}), f32[2,32,324]{2,0,1:T(2,128)S(1)}, u32[]{:S(2)}, u32[]{:S(2)}) async-start(f32[2,32,324]{2,0,1:T(2,128)} %copy.166), calls=%async_computation.1 | async-start | bytes 196608 | tf_op jit(solution)/shard_map/all_to_all | solution.py:57
  94.9 0.8 copy.195
  95.8 7.9 %all-to-all-done.1 = f32[2,32,324]{2,0,1:T(2,128)S(1)} async-done(((f32[2,32,324]{2,0,1:T(2,128)}), f32[2,32,324]{2,0,1:T(2,128)S(1)}, u32[]{:S(2)}, u32[]{:S(2)}) %all-to-all-start.1) | async-done | bytes 82976 | tf_op jit(solution)/shard_map/all_to_all | solution.py:57
  (122 shorter events, 19.4 us)
Async XLA Ops:
  0.6 7.7 %copy-start = (bf16[96,8,256]{2,1,0:T(8,128)(2,1)S(1)}, bf16[96,8,256]{2,1,0:T(8,128)(2,1)}, u32[]{:S(2)}) copy-start(bf16[96,8,256]{2,1,0:T(8,128)(2,1)} %param.5) | copy-start | bytes 1179652
  1.8 8.5 %copy-start.2 = (bf16[96,8,256]{2,1,0:T(8,128)(2,1)S(1)}, bf16[96,8,256]{2,1,0:T(8,128)(2,1)}, u32[]{:S(2)}) copy-start(bf16[96,8,256]{2,1,0:T(8,128)(2,1)} %param.6) | copy-start | bytes 1179652
  3.0 7.4 %collective-permute-start = (bf16[192,1,256]{2,0,1:T(8,128)(2,1)S(1)}, bf16[192,1,256]{2,0,1:T(8,128)(2,1)S(1)}, u32[]{:S(2)}, u32[]{:S(2)}) collective-permute-start(bf16[192,1,256]{2,0,1:T(8,128)(2,1)S(1)} %get-tuple-element.27), channel_id=1, source_target_pairs={{0,8},{8,16},{16,24},{24,32},{32,40},{40,48},{48,56},{56,64},{64,7... | collective-permute-start | bytes 294920 | tf_op jit(solution)/shard_map/ppermute | solution.py:15
  7.0 5.4 %collective-permute-start.1 = (bf16[192,1,256]{2,0,1:T(8,128)(2,1)S(1)}, bf16[192,1,256]{2,0,1:T(8,128)(2,1)S(1)}, u32[]{:S(2)}, u32[]{:S(2)}) collective-permute-start(bf16[192,1,256]{2,0,1:T(8,128)(2,1)S(1)} %get-tuple-element.28), channel_id=1, source_target_pairs={{8,0},{16,8},{24,16},{32,24},{40,32},{48,40},{56,48},{64,56},{72,6... | collective-permute-start | bytes 294920 | tf_op jit(solution)/shard_map/ppermute | solution.py:17
  10.4 10.9 %copy-start.7 = (bf16[192,1,256]{2,0,1:T(8,128)(2,1)}, bf16[192,1,256]{2,0,1:T(8,128)(2,1)S(1)}, u32[]{:S(2)}) copy-start(bf16[192,1,256]{2,0,1:T(8,128)(2,1)S(1)} %collective-permute-done) | copy-start | bytes 294916
  12.3 9.0 %copy-start.8 = (bf16[192,1,256]{2,0,1:T(8,128)(2,1)}, bf16[192,1,256]{2,0,1:T(8,128)(2,1)S(1)}, u32[]{:S(2)}) copy-start(bf16[192,1,256]{2,0,1:T(8,128)(2,1)S(1)} %collective-permute-done.1) | copy-start | bytes 294916
  13.1 12.0 %collective-permute-start.2 = (bf16[192,10,1]{0,1,2:T(8,128)(2,1)S(1)}, bf16[192,10,1]{0,1,2:T(8,128)(2,1)S(1)}, u32[]{:S(2)}, u32[]{:S(2)}) collective-permute-start(bf16[192,10,1]{0,1,2:T(8,128)(2,1)S(1)} %copy.122), channel_id=1, source_target_pairs={{1,0},{2,1},{3,2},{4,3},{5,4},{6,5},{7,6},{9,8},{10,9},{11,10},{12... | collective-permute-start | bytes 11528 | tf_op jit(solution)/shard_map/ppermute | solution.py:17
  18.1 8.1 %collective-permute-start.3 = (bf16[192,10,1]{0,1,2:T(8,128)(2,1)}, bf16[192,10,1]{0,1,2:T(8,128)(2,1)}, u32[]{:S(2)}, u32[]{:S(2)}) collective-permute-start(bf16[192,10,1]{0,1,2:T(8,128)(2,1)} %copy.126), channel_id=1, source_target_pairs={{0,1},{1,2},{2,3},{3,4},{4,5},{5,6},{6,7},{8,9},{9,10},{10,11},{11... | collective-permute-start | bytes 11528 | tf_op jit(solution)/shard_map/ppermute | solution.py:15
  30.3 1.2 %copy-start.5 = (bf16[3,3,96,96]{3,2,1,0:T(8,128)(2,1)S(1)}, bf16[3,3,96,96]{3,2,1,0:T(8,128)(2,1)}, u32[]{:S(2)}) copy-start(bf16[3,3,96,96]{3,2,1,0:T(8,128)(2,1)} %param.7) | copy-start | bytes 497668
  32.1 0.9 copy-start.13
  33.8 1.0 copy-start.3
  36.3 1.1 %copy-start.1 = (f32[96,2048]{1,0:T(8,128)S(1)}, f32[96,2048]{1,0:T(8,128)}, u32[]{:S(2)}) copy-start(f32[96,2048]{1,0:T(8,128)} %fusion.53) | copy-start | bytes 2359300
  36.6 1.1 %copy-start.14 = (f32[96]{0:T(128)S(1)}, f32[96]{0:T(128)}, u32[]{:S(2)}) copy-start(f32[96]{0:T(128)} %param.8) | copy-start | bytes 1156
  37.7 1.1 %copy-start.9 = (f32[96,2048]{1,0:T(8,128)S(1)}, f32[96,2048]{1,0:T(8,128)}, u32[]{:S(2)}) copy-start(f32[96,2048]{1,0:T(8,128)} %convolution_bitcast_fusion.5) | copy-start | bytes 2359300
  39.5 7.5 %collective-permute-start.4 = (bf16[96,1,256]{2,0,1:T(8,128)(2,1)S(1)}, bf16[96,1,256]{2,0,1:T(8,128)(2,1)S(1)}, u32[]{:S(2)}, u32[]{:S(2)}) collective-permute-start(bf16[96,1,256]{2,0,1:T(8,128)(2,1)S(1)} %get-tuple-element.44), channel_id=1, source_target_pairs={{0,8},{8,16},{16,24},{24,32},{32,40},{40,48},{48,56},{56,64},{64,7... | collective-permute-start | bytes 147464 | tf_op jit(solution)/shard_map/ppermute | solution.py:15
  42.7 4.8 %collective-permute-start.5 = (bf16[96,1,256]{2,0,1:T(8,128)(2,1)S(1)}, bf16[96,1,256]{2,0,1:T(8,128)(2,1)S(1)}, u32[]{:S(2)}, u32[]{:S(2)}) collective-permute-start(bf16[96,1,256]{2,0,1:T(8,128)(2,1)S(1)} %get-tuple-element.43), channel_id=1, source_target_pairs={{8,0},{16,8},{24,16},{32,24},{40,32},{48,40},{56,48},{64,56},{72,6... | collective-permute-start | bytes 147464 | tf_op jit(solution)/shard_map/ppermute | solution.py:17
  47.7 8.1 %collective-permute-start.6 = (bf16[96,10,1]{2,0,1:T(8,128)(2,1)S(1)}, bf16[96,10,1]{2,0,1:T(8,128)(2,1)S(1)}, u32[]{:S(2)}, u32[]{:S(2)}) collective-permute-start(bf16[96,10,1]{2,0,1:T(8,128)(2,1)S(1)} %get-tuple-element.39), channel_id=1, source_target_pairs={{1,0},{2,1},{3,2},{4,3},{5,4},{6,5},{7,6},{9,8},{10,9},{11,10},{12... | collective-permute-start | bytes 5768 | tf_op jit(solution)/shard_map/ppermute | solution.py:17
  51.0 6.0 %collective-permute-start.7 = (bf16[96,10,1]{2,0,1:T(8,128)(2,1)S(1)}, bf16[96,10,1]{2,0,1:T(8,128)(2,1)S(1)}, u32[]{:S(2)}, u32[]{:S(2)}) collective-permute-start(bf16[96,10,1]{2,0,1:T(8,128)(2,1)S(1)} %get-tuple-element.38), channel_id=1, source_target_pairs={{0,1},{1,2},{2,3},{3,4},{4,5},{5,6},{6,7},{8,9},{9,10},{10,11},{11... | collective-permute-start | bytes 5768 | tf_op jit(solution)/shard_map/ppermute | solution.py:15
  55.7 2.5 %copy-start.10 = (bf16[96,10,1]{2,0,1:T(8,128)(2,1)}, bf16[96,10,1]{2,0,1:T(8,128)(2,1)S(1)}, u32[]{:S(2)}) copy-start(bf16[96,10,1]{2,0,1:T(8,128)(2,1)S(1)} %collective-permute-done.6) | copy-start | bytes 5764
  56.9 2.0 %copy-start.12 = (bf16[96,10,1]{2,0,1:T(8,128)(2,1)}, bf16[96,10,1]{2,0,1:T(8,128)(2,1)S(1)}, u32[]{:S(2)}) copy-start(bf16[96,10,1]{2,0,1:T(8,128)(2,1)S(1)} %collective-permute-done.7) | copy-start | bytes 5764
  60.9 5.9 %copy-start.11 = (bf16[96,10,1]{2,0,1:T(8,128)(2,1)S(1)}, bf16[96,10,1]{2,0,1:T(8,128)(2,1)}, u32[]{:S(2)}) copy-start(bf16[96,10,1]{2,0,1:T(8,128)(2,1)} %copy-done.10) | copy-start | bytes 5764
  60.9 18.1 %all-to-all-start = ((f32[2,32,8,324]{3,1,0,2:T(8,128)}), f32[2,32,8,324]{3,1,0,2:T(8,128)S(1)}, u32[]{:S(2)}, u32[]{:S(2)}) async-start(f32[2,32,8,324]{3,1,0,2:T(8,128)} %pad_maximum_fusion.2), calls=%async_computation | async-start | bytes 1572864 | tf_op jit(solution)/shard_map/all_to_all | solution.py:56
  66.8 2.2 %copy-start.6 = (bf16[3,3,96,96]{3,2,1,0:T(8,128)(2,1)S(1)}, bf16[3,3,96,96]{3,2,1,0:T(8,128)(2,1)}, u32[]{:S(2)}) copy-start(bf16[3,3,96,96]{3,2,1,0:T(8,128)(2,1)} %param.7) | copy-start | bytes 497668
  68.9 1.0 copy-start.4
  79.7 24.0 %all-to-all-start.1 = ((f32[2,32,324]{2,0,1:T(2,128)}), f32[2,32,324]{2,0,1:T(2,128)S(1)}, u32[]{:S(2)}, u32[]{:S(2)}) async-start(f32[2,32,324]{2,0,1:T(2,128)} %copy.166), calls=%async_computation.1 | async-start | bytes 196608 | tf_op jit(solution)/shard_map/all_to_all | solution.py:57

commit v6 on v5

--- a/solution.py
+++ b/solution.py
@@ -53,12 +53,13 @@
 def reduce_weights(grads):
     rows, cols = lax.axis_size("row"), lax.axis_size("col")
     stacked = jnp.stack(grads).reshape(len(grads), rows, cols, -1)
-    stacked = lax.all_to_all(stacked, "col", 2, 2, tiled=True).sum(axis=2)
+    stacked = lax.all_to_all(stacked, "col", 2, 2, tiled=True)
+    stacked = stacked.sum(axis=2)
     summed = lax.all_to_all(stacked, "row", 1, 1, tiled=True).sum(axis=1)
     return (summed[0], summed[1])
 
 
-def local(features, cotangent, weight_one, bias_one, weight_two):
+def block(features, cotangent, weight_one, bias_one, weight_two):
     channels, tile_rows, tile_cols = features.shape
     cell_count = tile_rows * tile_cols
     scale = float(cell_count * lax.axis_size("row") * lax.axis_size("col")) ** (-0.5)
@@ -82,10 +83,20 @@
     padded_hid = padded_2(
         hidden_grad.reshape(channels, tile_rows, tile_cols), (("row", 1), ("col", 2)), 1
     )
-    back_input, grad_one = backward_taps(
-        padded_hid, weight_one, features.reshape(channels, cell_count), tile_rows, tile_cols
-    )
-    grad_one = grad_one * scale
+    inner_grad = hidden_grad.reshape(channels, cell_count)
+    grad_one = jnp.stack(
+        [
+            lax.dot_general(
+                inner_grad,
+                window(padded_input, offset_y, offset_x, tile_rows, tile_cols),
+                (((1,), (1,)), ((), ())),
+                preferred_element_type=jnp.float32,
+            )
+            for offset_y in range(3)
+            for offset_x in range(3)
+        ]
+    ).reshape(-1) * scale
+    back_input, _ = backward_taps(padded_hid, weight_one, inner_grad, tile_rows, tile_cols)
     input_grad = (cotangent.reshape(channels, cell_count).astype(jnp.float32) + back_input).astype(
         jnp.bfloat16
     )
@@ -97,7 +108,7 @@
 def solution(mesh):
     placed = (P(None, "row", "col"), P(None, "row", "col"), P(), P(), P())
     return jax.shard_map(
-        local,
+        block,
         mesh=mesh,
         in_specs=placed,
         out_specs=(P(None, "row", "col"), P(("row", "col")), P(("row", "col"))),

time: 105 us -> 106 us (level)
  local copies, waits for them, and re-layouts: 17 us -> 19.6 us
  starting transfers between devices: 44 us -> 41.4 us
    ppermute x4, waiting for transfers between devices: 3.25 us -> 10.1 us  [padded_2(): lax.ppermute(head, axis, [((i + 1) % count, i) for i in range(ends)])]
    all_to_all x1, waiting for transfers between devices: 6.68 us -> 0.01 us  [reduce_weights(): stacked = lax.all_to_all(stacked, 'col', 2, 2, tiled=True)]
    mul x4, local copies, waits for them, and re-layouts: 1.02 us -> 4.62 us  [the longest x2 4.1 us: block(): jnp.stack([lax.dot_general(inner_grad, window(padded_input, offset_y, off...]
    dot_general x9 -> x18, matrix products: 4.83 us -> 8.14 us  [the longest x9 5.79 us: block(): jnp.dot(weight_one[offset_y, offset_x], patch, preferred_element_type=jnp...]
    dot_general x18 -> x9, matrix products: 5.31 us -> 2.37 us  [backward_taps(): lax.dot_general(patch, other, (((1,), (1,)), ((), ())), preferred_element...]
    unnamed x2 -> x1, other arithmetic: 2.21 us -> 0.16 us
    all_to_all x1, starting transfers between devices: 5.9 us -> 4.12 us  [reduce_weights(): stacked = lax.all_to_all(stacked, 'col', 2, 2, tiled=True)]
    concatenate x2 -> x5, other arithmetic: 2.44 us -> 4.07 us  [padded_2(): jnp.concatenate([lax.ppermute(tail, axis, [(i, (i + 1) % count) for i in...]
  transfers between devices with their start and end apart: 10 -> 10, of which waited for: 6 -> 4; matrix products, arithmetic and copies ran while one was open for 18% -> 17% of each run, Pallas kernels for 0% -> 0%
where the time goes in v6:
time: 106 us; the launch traced here: 105 us
  starting transfers between devices  41.4 us (39%)
  local copies, waits for them, and re-layouts  19.6 us (18%)
  waiting for transfers between devices  18.1 us (17%)
  matrix products  18 us (17%)
  other arithmetic  6.15 us (6%)
  between operations  1.55 us (1%)
    all_to_all x1, starting transfers between devices, reduce_weights(): summed = lax.all_to_all(stacked, 'row', 1, 1, tiled=True).sum(axis=1)  14.7 us
    ppermute x4, starting transfers between devices, padded_2(): lax.ppermute(tail, axis, [(i, (i + 1) % count) for i in range(ends)])  13.6 us
    ppermute x4, waiting for transfers between devices, padded_2(): lax.ppermute(head, axis, [((i + 1) % count, i) for i in range(ends)])  10.1 us
    ppermute x4, starting transfers between devices, padded_2(): lax.ppermute(head, axis, [((i + 1) % count, i) for i in range(ends)])  9.04 us
    all_to_all x1, waiting for transfers between devices, reduce_weights(): summed = lax.all_to_all(stacked, 'row', 1, 1, tiled=True).sum(axis=1)  7.94 us
    unnamed x52, local copies, waits for them, and re-layouts  7.53 us
    dot_general x18, matrix products, backward_taps(): lax.dot_general(kernel[offset_y, offset_x], patch, (((0,), (0,)), ((), ()...  7.49 us
    dot_general x9, matrix products, block(): jnp.dot(weight_one[offset_y, offset_x], patch, preferred_element_type=jnp...  5.79 us
  transfers between devices with their start and end apart: 10, of which 4 were waited for; matrix products, arithmetic and copies ran while one was open for 17% of the time, Pallas kernels for 0%

profile of v6, /device:TPU:1, one launch (start us, length us, event | category | flops | bytes accessed | tf_op | source)
XLA Modules:
  0.0 104.8 jit_solution(9387287812272431946)
XLA Ops:
  0.6 1.1 %copy_dynamic-update-slice_fusion.1 = bf16[192,8,256]{2,0,1:T(8,128)(2,1)S(1)} fusion(bf16[96,8,256]{2,1,0:T(8,128)(2,1)} %param.5), kind=kLoop, calls=%fused_computation.107 | loop fusion | bytes 786432
  1.8 1.1 %copy_dynamic-update-slice_fusion = bf16[192,8,256]{2,0,1:T(8,128)(2,1)S(1)} fusion(bf16[192,8,256]{2,0,1:T(8,128)(2,1)S(1)} %copy_dynamic-update-slice_fusion.1, bf16[96,8,256]{2,1,0:T(8,128)(2,1)} %param.6), kind=kLoop, calls=%fused_computation.106 | loop fusion | bytes 786432 | tf_op jit(solution)/shard_map/concatenate | solution.py:67
  3.0 4.0 %collective-permute-start = (bf16[192,1,256]{2,0,1:T(8,128)(2,1)S(1)}, bf16[192,1,256]{2,0,1:T(8,128)(2,1)S(1)}, u32[]{:S(2)}, u32[]{:S(2)}) collective-permute-start(bf16[192,1,256]{2,0,1:T(8,128)(2,1)S(1)} %get-tuple-element.35), channel_id=1, source_target_pairs={{0,8},{8,16},{16,24},{24,32},{32,40},{40,48},{48,56},{56,64},{64,7... | collective-permute-start | bytes 294920 | tf_op jit(solution)/shard_map/ppermute | solution.py:15
  7.0 1.3 %collective-permute-start.1 = (bf16[192,1,256]{2,0,1:T(8,128)(2,1)S(1)}, bf16[192,1,256]{2,0,1:T(8,128)(2,1)S(1)}, u32[]{:S(2)}, u32[]{:S(2)}) collective-permute-start(bf16[192,1,256]{2,0,1:T(8,128)(2,1)S(1)} %get-tuple-element.36), channel_id=1, source_target_pairs={{8,0},{16,8},{24,16},{32,24},{40,32},{48,40},{56,48},{64,56},{72,6... | collective-permute-start | bytes 294920 | tf_op jit(solution)/shard_map/ppermute | solution.py:17
  8.4 1.9 %fusion.47 = f32[96,2048]{1,0:T(8,128)} fusion(bf16[96,2048]{1,0:T(8,128)(2,1)S(1)} %bitcast.347, bf16[3,3,96,96]{3,2,1,0:T(8,128)(2,1)} %param.7), kind=kOutput, calls=%fused_computation.119 | convolution fusion | flops 37748736 | bytes 1204224 | tf_op jit(solution)/shard_map/dot_general | solution.py:74
  10.4 1.9 %collective-permute-done.1 = bf16[192,1,256]{2,0,1:T(8,128)(2,1)S(1)} collective-permute-done((bf16[192,1,256]{2,0,1:T(8,128)(2,1)S(1)}, bf16[192,1,256]{2,0,1:T(8,128)(2,1)S(1)}, u32[]{:S(2)}, u32[]{:S(2)}) %collective-permute-start.1) | collective-permute-done | bytes 98336 | tf_op jit(solution)/shard_map/ppermute | solution.py:17
  13.1 4.0 %collective-permute-start.2 = (bf16[192,10,1]{0,1,2:T(8,128)(2,1)S(1)}, bf16[192,10,1]{0,1,2:T(8,128)(2,1)S(1)}, u32[]{:S(2)}, u32[]{:S(2)}) collective-permute-start(bf16[192,10,1]{0,1,2:T(8,128)(2,1)S(1)} %copy.45), channel_id=1, source_target_pairs={{1,0},{2,1},{3,2},{4,3},{5,4},{6,5},{7,6},{9,8},{10,9},{11,10},{12... | collective-permute-start | bytes 11528 | tf_op jit(solution)/shard_map/ppermute | solution.py:17
  17.5 3.0 %collective-permute-start.3 = (bf16[192,10,1]{0,1,2:T(8,128)(2,1)S(1)}, bf16[192,10,1]{0,1,2:T(8,128)(2,1)S(1)}, u32[]{:S(2)}, u32[]{:S(2)}) collective-permute-start(bf16[192,10,1]{0,1,2:T(8,128)(2,1)S(1)} %copy.49), channel_id=1, source_target_pairs={{0,1},{1,2},{2,3},{3,4},{4,5},{5,6},{6,7},{8,9},{9,10},{10,11},{11... | collective-permute-start | bytes 11528 | tf_op jit(solution)/shard_map/ppermute | solution.py:15
  20.7 1.9 %convolution_bitcast_fusion.1 = f32[96,2048]{1,0:T(8,128)} fusion(bf16[96,2048]{1,0:T(8,128)(2,1)S(1)} %bitcast.349, bf16[3,3,96,96]{3,2,1,0:T(8,128)(2,1)} %param.7), kind=kOutput, calls=%fused_computation.1 | convolution fusion | flops 37748736 | bytes 1204224 | tf_op jit(solution)/shard_map/dot_general | solution.py:74
  22.7 1.9 %convolution_bitcast_fusion.5 = f32[96,2048]{1,0:T(8,128)} fusion(bf16[96,2048]{1,0:T(8,128)(2,1)S(1)} %bitcast.345, bf16[3,3,96,96]{3,2,1,0:T(8,128)(2,1)} %param.9), kind=kOutput, calls=%fused_computation.5 | convolution fusion | flops 37748736 | bytes 1204224 | tf_op jit(solution)/shard_map/dot_general | solution.py:39
  24.6 0.8 copy.79
  25.4 0.8 copy.71
  26.9 1.1 %pad_maximum_fusion = (bf16[192,10,257]{2,0,1:T(8,128)(2,1)S(1)}, bf16[192,10,257]{2,0,1:T(8,128)(2,1)S(1)}) fusion(bf16[192,10,1]{2,0,1:T(8,128)(2,1)S(1)} %copy.46, bf16[192,1,256]{2,0,1:T(8,128)(2,1)S(1)} %collective-permute-done.1, bf16[192,8,256]{2,0,1:T(8,128)(2,1)S(1)} %copy_dynamic-update-slice_fusion, ...), kind=kLoop, calls=%fused_computation.41 | loop fusion | flops 7895040 | bytes 2964480 | tf_op jit(solution)/shard_map/concatenate | solution.py:13
  28.0 1.1 %slice_bitcast_fusion.2 = (bf16[8,12,8,256]{3,2,1,0:T(8,128)(2,1)S(1)}, bf16[8,12,8,256]{3,2,1,0:T(8,128)(2,1)S(1)}, bf16[8,12,8,256]{3,2,1,0:T(8,128)(2,1)S(1)}...) fusion(bf16[192,10,257]{2,0,1:T(8,128)(2,1)S(1)} %get-tuple-ele, ...), kind=kLoop, calls=%fused_computation.92 | loop fusion | bytes 9437184
  33.0 0.7 copy-done
  35.1 0.8 copy-done.8
  40.4 0.8 broadcast_multiply_fusion.1
  41.2 2.2 %mul.45 = f32[1,32,8,324]{3,2,1,0:T(8,128)} reshape(f32[9,96,96]{2,1,0:T(8,128)} %broadcast_multiply_fusion.1) | data formatting | bytes 663552 | tf_op jit(solution)/shard_map/mul | solution.py:87
  43.4 1.9 %copy.66 = f32[1,32,8,324]{3,1,0,2:T(8,128)} copy(f32[1,32,8,324]{3,2,1,0:T(8,128)} %mul.45) | data formatting | bytes 663552 | tf_op jit(solution)/shard_map/mul | solution.py:87
  48.6 3.2 %collective-permute-start.4 = (bf16[96,1,256]{2,1,0:T(2,128)(2,1)S(1)}, bf16[96,1,256]{2,1,0:T(2,128)(2,1)S(1)}, u32[]{:S(2)}, u32[]{:S(2)}) collective-permute-start(bf16[96,1,256]{2,1,0:T(2,128)(2,1)S(1)} %get-tuple-element.41), channel_id=1, source_target_pairs={{0,8},{8,16},{16,24},{24,32},{32,40},{40,48},{48,56},{56,64},{64,7... | collective-permute-start | bytes 147464 | tf_op jit(solution)/shard_map/ppermute | solution.py:15
  51.8 1.3 %collective-permute-start.5 = (bf16[96,1,256]{2,1,0:T(2,128)(2,1)S(1)}, bf16[96,1,256]{2,1,0:T(2,128)(2,1)S(1)}, u32[]{:S(2)}, u32[]{:S(2)}) collective-permute-start(bf16[96,1,256]{2,1,0:T(2,128)(2,1)S(1)} %get-tuple-element.42), channel_id=1, source_target_pairs={{8,0},{16,8},{24,16},{32,24},{40,32},{48,40},{56,48},{64,56},{72,6... | collective-permute-start | bytes 147464 | tf_op jit(solution)/shard_map/ppermute | solution.py:17
  53.2 1.0 pad_maximum_fusion.4
  54.1 4.1 %all-to-all-start = ((f32[2,32,8,324]{3,1,0,2:T(8,128)}), f32[2,32,8,324]{3,1,0,2:T(8,128)S(1)}, u32[]{:S(2)}, u32[]{:S(2)}) async-start(f32[2,32,8,324]{3,1,0,2:T(8,128)} %pad_maximum_fusion.4), calls=%async_computation | async-start | bytes 1572864 | tf_op jit(solution)/shard_map/all_to_all | solution.py:56
  59.1 2.4 %collective-permute-start.6 = (bf16[96,10,1]{2,1,0:T(8,128)(2,1)S(1)}, bf16[96,10,1]{2,1,0:T(8,128)(2,1)S(1)}, u32[]{:S(2)}, u32[]{:S(2)}) collective-permute-start(bf16[96,10,1]{2,1,0:T(8,128)(2,1)S(1)} %get-tuple-element.32), channel_id=1, source_target_pairs={{1,0},{2,1},{3,2},{4,3},{5,4},{6,5},{7,6},{9,8},{10,9},{11,10},{12... | collective-permute-start | bytes 5768 | tf_op jit(solution)/shard_map/ppermute | solution.py:17
  61.6 3.3 %collective-permute-start.7 = (bf16[96,10,1]{2,1,0:T(8,128)(2,1)S(1)}, bf16[96,10,1]{2,1,0:T(8,128)(2,1)S(1)}, u32[]{:S(2)}, u32[]{:S(2)}) collective-permute-start(bf16[96,10,1]{2,1,0:T(8,128)(2,1)S(1)} %get-tuple-element.31), channel_id=1, source_target_pairs={{0,1},{1,2},{2,3},{3,4},{4,5},{5,6},{6,7},{8,9},{9,10},{10,11},{11... | collective-permute-start | bytes 5768 | tf_op jit(solution)/shard_map/ppermute | solution.py:15
  65.4 8.0 %collective-permute-done.6 = bf16[96,10,1]{2,1,0:T(8,128)(2,1)S(1)} collective-permute-done((bf16[96,10,1]{2,1,0:T(8,128)(2,1)S(1)}, bf16[96,10,1]{2,1,0:T(8,128)(2,1)S(1)}, u32[]{:S(2)}, u32[]{:S(2)}) %collective-permute-start.6) | collective-permute-done | bytes 1952 | tf_op jit(solution)/shard_map/ppermute | solution.py:17
  73.4 2.0 %maximum_maximum_fusion.1 = (bf16[96,10,257]{2,1,0:T(8,128)(2,1)S(1)}, bf16[96,10,257]{2,1,0:T(8,128)(2,1)S(1)}) fusion(bf16[96,1,256]{2,1,0:T(2,128)(2,1)S(1)} %collective-permute-done.5, bf16[96,8,256]{2,1,0:T(8,128)(2,1)S(1)} %bitcast.339, bf16[96,1,256]{2,1,0:T(2,128)(2,1)S(1)} %collective-permute-done.4, ...), kind=kLoop, calls=%fused_computation.44 | loop fusion | flops 3947520 | bytes 1482240 | tf_op jit(solution)/shard_map/concatenate | solution.py:13
  75.4 0.8 fusion.97
  79.6 0.7 copy.68
  80.3 14.7 %all-to-all-start.1 = ((f32[2,32,324]{2,0,1:T(2,128)}), f32[2,32,324]{2,0,1:T(2,128)S(1)}, u32[]{:S(2)}, u32[]{:S(2)}) async-start(f32[2,32,324]{2,0,1:T(2,128)} %copy.68), calls=%async_computation.1 | async-start | bytes 196608 | tf_op jit(solution)/shard_map/all_to_all | solution.py:58
  95.3 0.8 copy.97
  96.2 7.9 %all-to-all-done.1 = f32[2,32,324]{2,0,1:T(2,128)S(1)} async-done(((f32[2,32,324]{2,0,1:T(2,128)}), f32[2,32,324]{2,0,1:T(2,128)S(1)}, u32[]{:S(2)}, u32[]{:S(2)}) %all-to-all-start.1) | async-done | bytes 82976 | tf_op jit(solution)/shard_map/all_to_all | solution.py:58
  (129 shorter events, 20.4 us)
Async XLA Ops:
  0.6 7.7 %copy-start.9 = (bf16[96,8,256]{2,1,0:T(8,128)(2,1)S(1)}, bf16[96,8,256]{2,1,0:T(8,128)(2,1)}, u32[]{:S(2)}) copy-start(bf16[96,8,256]{2,1,0:T(8,128)(2,1)} %param.5) | copy-start | bytes 1179652
  1.8 8.5 %copy-start.10 = (bf16[96,8,256]{2,1,0:T(8,128)(2,1)S(1)}, bf16[96,8,256]{2,1,0:T(8,128)(2,1)}, u32[]{:S(2)}) copy-start(bf16[96,8,256]{2,1,0:T(8,128)(2,1)} %param.6) | copy-start | bytes 1179652
  3.0 7.4 %collective-permute-start = (bf16[192,1,256]{2,0,1:T(8,128)(2,1)S(1)}, bf16[192,1,256]{2,0,1:T(8,128)(2,1)S(1)}, u32[]{:S(2)}, u32[]{:S(2)}) collective-permute-start(bf16[192,1,256]{2,0,1:T(8,128)(2,1)S(1)} %get-tuple-element.35), channel_id=1, source_target_pairs={{0,8},{8,16},{16,24},{24,32},{32,40},{40,48},{48,56},{56,64},{64,7... | collective-permute-start | bytes 294920 | tf_op jit(solution)/shard_map/ppermute | solution.py:15
  7.0 5.4 %collective-permute-start.1 = (bf16[192,1,256]{2,0,1:T(8,128)(2,1)S(1)}, bf16[192,1,256]{2,0,1:T(8,128)(2,1)S(1)}, u32[]{:S(2)}, u32[]{:S(2)}) collective-permute-start(bf16[192,1,256]{2,0,1:T(8,128)(2,1)S(1)} %get-tuple-element.36), channel_id=1, source_target_pairs={{8,0},{16,8},{24,16},{32,24},{40,32},{48,40},{56,48},{64,56},{72,6... | collective-permute-start | bytes 294920 | tf_op jit(solution)/shard_map/ppermute | solution.py:17
  13.1 13.1 %collective-permute-start.2 = (bf16[192,10,1]{0,1,2:T(8,128)(2,1)S(1)}, bf16[192,10,1]{0,1,2:T(8,128)(2,1)S(1)}, u32[]{:S(2)}, u32[]{:S(2)}) collective-permute-start(bf16[192,10,1]{0,1,2:T(8,128)(2,1)S(1)} %copy.45), channel_id=1, source_target_pairs={{1,0},{2,1},{3,2},{4,3},{5,4},{6,5},{7,6},{9,8},{10,9},{11,10},{12... | collective-permute-start | bytes 11528 | tf_op jit(solution)/shard_map/ppermute | solution.py:17
  17.5 9.0 %collective-permute-start.3 = (bf16[192,10,1]{0,1,2:T(8,128)(2,1)S(1)}, bf16[192,10,1]{0,1,2:T(8,128)(2,1)S(1)}, u32[]{:S(2)}, u32[]{:S(2)}) collective-permute-start(bf16[192,10,1]{0,1,2:T(8,128)(2,1)S(1)} %copy.49), channel_id=1, source_target_pairs={{0,1},{1,2},{2,3},{3,4},{4,5},{5,6},{6,7},{8,9},{9,10},{10,11},{11... | collective-permute-start | bytes 11528 | tf_op jit(solution)/shard_map/ppermute | solution.py:15
  28.0 1.1 %copy-start.14 = (bf16[3,3,96,96]{3,2,1,0:T(8,128)(2,1)S(1)}, bf16[3,3,96,96]{3,2,1,0:T(8,128)(2,1)}, u32[]{:S(2)}) copy-start(bf16[3,3,96,96]{3,2,1,0:T(8,128)(2,1)} %param.7) | copy-start | bytes 497668
  29.8 0.9 copy-start.17
  31.1 3.0 %copy-start.5 = (bf16[8,12,8,256]{3,2,0,1:T(8,128)(2,1)}, bf16[8,12,8,256]{3,2,0,1:T(8,128)(2,1)S(1)}, u32[]{:S(2)}) copy-start(bf16[8,12,8,256]{3,2,0,1:T(8,128)(2,1)S(1)} %copy.72) | copy-start | bytes 1179652
  31.2 3.3 %copy-start.3 = (bf16[8,12,8,256]{3,2,0,1:T(8,128)(2,1)}, bf16[8,12,8,256]{3,2,0,1:T(8,128)(2,1)S(1)}, u32[]{:S(2)}) copy-start(bf16[8,12,8,256]{3,2,0,1:T(8,128)(2,1)S(1)} %copy.73) | copy-start | bytes 1179652
  31.5 1.0 copy-start.2
  31.9 4.8 %copy-start.11 = (bf16[8,12,8,256]{3,2,0,1:T(8,128)(2,1)}, bf16[8,12,8,256]{3,2,0,1:T(8,128)(2,1)S(1)}, u32[]{:S(2)}) copy-start(bf16[8,12,8,256]{3,2,0,1:T(8,128)(2,1)S(1)} %copy.74) | copy-start | bytes 1179652
  32.8 1.0 copy-start
  34.8 1.1 %copy-start.8 = (f32[96,2048]{1,0:T(8,128)S(1)}, f32[96,2048]{1,0:T(8,128)}, u32[]{:S(2)}) copy-start(f32[96,2048]{1,0:T(8,128)} %fusion.47) | copy-start | bytes 2359300
  35.1 1.2 %copy-start.7 = (f32[96,2048]{1,0:T(8,128)S(1)}, f32[96,2048]{1,0:T(8,128)}, u32[]{:S(2)}) copy-start(f32[96,2048]{1,0:T(8,128)} %convolution_bitcast_fusion.1) | copy-start | bytes 2359300
  35.1 1.2 %copy-start.18 = (f32[96]{0:T(128)S(1)}, f32[96]{0:T(128)}, u32[]{:S(2)}) copy-start(f32[96]{0:T(128)} %param.8) | copy-start | bytes 1156
  36.3 1.1 %copy-start.16 = (f32[96,2048]{1,0:T(8,128)S(1)}, f32[96,2048]{1,0:T(8,128)}, u32[]{:S(2)}) copy-start(f32[96,2048]{1,0:T(8,128)} %convolution_bitcast_fusion.5) | copy-start | bytes 2359300
  40.4 5.2 %copy-start.1 = (bf16[8,12,8,256]{3,2,0,1:T(8,128)(2,1)S(1)}, bf16[8,12,8,256]{3,2,0,1:T(8,128)(2,1)}, u32[]{:S(2)}) copy-start(bf16[8,12,8,256]{3,2,0,1:T(8,128)(2,1)} %copy.71) | copy-start | bytes 1179652
  43.4 2.5 %copy-start.6 = (bf16[8,12,8,256]{3,2,0,1:T(8,128)(2,1)S(1)}, bf16[8,12,8,256]{3,2,0,1:T(8,128)(2,1)}, u32[]{:S(2)}) copy-start(bf16[8,12,8,256]{3,2,0,1:T(8,128)(2,1)} %copy-done.5) | copy-start | bytes 1179652
  43.4 2.8 %copy-start.4 = (bf16[8,12,8,256]{3,2,0,1:T(8,128)(2,1)S(1)}, bf16[8,12,8,256]{3,2,0,1:T(8,128)(2,1)}, u32[]{:S(2)}) copy-start(bf16[8,12,8,256]{3,2,0,1:T(8,128)(2,1)} %copy-done.3) | copy-start | bytes 1179652
  45.6 1.1 %copy-start.12 = (bf16[8,12,8,256]{3,2,0,1:T(8,128)(2,1)S(1)}, bf16[8,12,8,256]{3,2,0,1:T(8,128)(2,1)}, u32[]{:S(2)}) copy-start(bf16[8,12,8,256]{3,2,0,1:T(8,128)(2,1)} %copy-done.11) | copy-start | bytes 1179652
  47.9 5.3 %copy-start.13 = (f32[1,32,8,324]{3,1,0,2:T(8,128)S(1)}, f32[1,32,8,324]{3,1,0,2:T(8,128)}, u32[]{:S(2)}) copy-start(f32[1,32,8,324]{3,1,0,2:T(8,128)} %copy.66) | copy-start | bytes 995332
  48.6 9.6 %collective-permute-start.4 = (bf16[96,1,256]{2,1,0:T(2,128)(2,1)S(1)}, bf16[96,1,256]{2,1,0:T(2,128)(2,1)S(1)}, u32[]{:S(2)}, u32[]{:S(2)}) collective-permute-start(bf16[96,1,256]{2,1,0:T(2,128)(2,1)S(1)} %get-tuple-element.41), channel_id=1, source_target_pairs={{0,8},{8,16},{16,24},{24,32},{32,40},{40,48},{48,56},{56,64},{64,7... | collective-permute-start | bytes 147464 | tf_op jit(solution)/shard_map/ppermute | solution.py:15
  51.8 6.6 %collective-permute-start.5 = (bf16[96,1,256]{2,1,0:T(2,128)(2,1)S(1)}, bf16[96,1,256]{2,1,0:T(2,128)(2,1)S(1)}, u32[]{:S(2)}, u32[]{:S(2)}) collective-permute-start(bf16[96,1,256]{2,1,0:T(2,128)(2,1)S(1)} %get-tuple-element.42), channel_id=1, source_target_pairs={{8,0},{16,8},{24,16},{32,24},{40,32},{48,40},{56,48},{64,56},{72,6... | collective-permute-start | bytes 147464 | tf_op jit(solution)/shard_map/ppermute | solution.py:17
  54.1 25.4 %all-to-all-start = ((f32[2,32,8,324]{3,1,0,2:T(8,128)}), f32[2,32,8,324]{3,1,0,2:T(8,128)S(1)}, u32[]{:S(2)}, u32[]{:S(2)}) async-start(f32[2,32,8,324]{3,1,0,2:T(8,128)} %pad_maximum_fusion.4), calls=%async_computation | async-start | bytes 1572864 | tf_op jit(solution)/shard_map/all_to_all | solution.py:56
  59.1 14.3 %collective-permute-start.6 = (bf16[96,10,1]{2,1,0:T(8,128)(2,1)S(1)}, bf16[96,10,1]{2,1,0:T(8,128)(2,1)S(1)}, u32[]{:S(2)}, u32[]{:S(2)}) collective-permute-start(bf16[96,10,1]{2,1,0:T(8,128)(2,1)S(1)} %get-tuple-element.32), channel_id=1, source_target_pairs={{1,0},{2,1},{3,2},{4,3},{5,4},{6,5},{7,6},{9,8},{10,9},{11,10},{12... | collective-permute-start | bytes 5768 | tf_op jit(solution)/shard_map/ppermute | solution.py:17
  61.6 11.8 %collective-permute-start.7 = (bf16[96,10,1]{2,1,0:T(8,128)(2,1)S(1)}, bf16[96,10,1]{2,1,0:T(8,128)(2,1)S(1)}, u32[]{:S(2)}, u32[]{:S(2)}) collective-permute-start(bf16[96,10,1]{2,1,0:T(8,128)(2,1)S(1)} %get-tuple-element.31), channel_id=1, source_target_pairs={{0,1},{1,2},{2,3},{3,4},{4,5},{5,6},{6,7},{8,9},{9,10},{10,11},{11... | collective-permute-start | bytes 5768 | tf_op jit(solution)/shard_map/ppermute | solution.py:15
  75.4 0.9 copy-start.15
  80.3 23.8 %all-to-all-start.1 = ((f32[2,32,324]{2,0,1:T(2,128)}), f32[2,32,324]{2,0,1:T(2,128)S(1)}, u32[]{:S(2)}, u32[]{:S(2)}) async-start(f32[2,32,324]{2,0,1:T(2,128)} %copy.68), calls=%async_computation.1 | async-start | bytes 196608 | tf_op jit(solution)/shard_map/all_to_all | solution.py:58

commit v7 on v5

--- a/solution.py
+++ b/solution.py
@@ -19,6 +19,22 @@
             axis=dim,
         )
     return cells
+
+
+def padded_pair(first, second, width):
+    count = lax.axis_size("row")
+    ends = count - 1
+    rows = first.shape[1]
+    head = jnp.concatenate([first[:, :width], second[:, :width]], axis=0)
+    tail = jnp.concatenate([first[:, rows - width :], second[:, rows - width :]], axis=0)
+    return jnp.concatenate(
+        [
+            lax.ppermute(tail, "row", [(i, (i + 1) % count) for i in range(ends)]),
+            jnp.concatenate([first, second], axis=0),
+            lax.ppermute(head, "row", [((i + 1) % count, i) for i in range(ends)]),
+        ],
+        axis=1,
+    )
 
 
 def window(padded, start_y, start_x, tile_rows, tile_cols):
@@ -62,9 +78,7 @@
     channels, tile_rows, tile_cols = features.shape
     cell_count = tile_rows * tile_cols
     scale = float(cell_count * lax.axis_size("row") * lax.axis_size("col")) ** (-0.5)
-    padded_both = padded_2(
-        jnp.concatenate([features, cotangent], axis=0), (("row", 1), ("col", 2)), 1
-    )
+    padded_both = padded_2(padded_pair(features, cotangent, 1), (("col", 2),), 1)
     padded_input, padded_cot = padded_both[:channels], padded_both[channels:]
     hidden = jnp.zeros((channels, cell_count), jnp.float32)
     for offset_y in range(3):

time: 105 us -> 106 us (level)
    ppermute x0 -> x2, starting transfers between devices: none -> 5.45 us  [the longest x1 4.02 us: padded_pair(): lax.ppermute(tail, 'row', [(i, (i + 1) % count) for i in range(ends)])]
    ppermute x4 -> x3, starting transfers between devices: 13.2 us -> 9.22 us  [padded_2(): lax.ppermute(tail, axis, [(i, (i + 1) % count) for i in range(ends)])]
    slice x0 -> x2, local copies, waits for them, and re-layouts: none -> 2.73 us  [the longest x1 1.37 us: padded_pair(): second[:, rows - width:]]
    ppermute x4 -> x3, waiting for transfers between devices: 3.25 us -> 1.25 us  [padded_2(): lax.ppermute(head, axis, [((i + 1) % count, i) for i in range(ends)])]
    ppermute x0 -> x2, waiting for transfers between devices: none -> 1.81 us  [the longest x1 1.81 us: padded_pair(): lax.ppermute(head, 'row', [((i + 1) % count, i) for i in range(ends)])]
    ppermute x4 -> x3, starting transfers between devices: 9.9 us -> 8.62 us  [padded_2(): lax.ppermute(head, axis, [((i + 1) % count, i) for i in range(ends)])]
    concatenate x1, local copies, waits for them, and re-layouts: 1.13 us -> 0.07 us  [padded_pair(): jnp.concatenate([first, second], axis=0)]
    unnamed x38 -> x44, local copies, waits for them, and re-layouts: 6.63 us -> 6.97 us
where the time goes in v7:
time: 106 us; the launch traced here: 105 us
  starting transfers between devices  44.1 us (42%)
  waiting for transfers between devices  18.2 us (17%)
  matrix products  17.7 us (17%)
  local copies, waits for them, and re-layouts  17.6 us (17%)
  other arithmetic  5.8 us (5%)
  between operations  1.57 us (1%)
    all_to_all x1, starting transfers between devices, reduce_weights(): summed = lax.all_to_all(stacked, 'row', 1, 1, tiled=True).sum(axis=1)  14.9 us
    ppermute x3, starting transfers between devices, padded_2(): lax.ppermute(tail, axis, [(i, (i + 1) % count) for i in range(ends)])  9.22 us
    ppermute x3, starting transfers between devices, padded_2(): lax.ppermute(head, axis, [((i + 1) % count, i) for i in range(ends)])  8.62 us
    all_to_all x1, waiting for transfers between devices, reduce_weights(): summed = lax.all_to_all(stacked, 'row', 1, 1, tiled=True).sum(axis=1)  7.94 us
    dot_general x18, matrix products, backward_taps(): lax.dot_general(kernel[offset_y, offset_x], patch, (((0,), (0,)), ((), ()...  7.53 us
    unnamed x44, local copies, waits for them, and re-layouts  6.97 us
    all_to_all x1, waiting for transfers between devices, reduce_weights(): stacked = lax.all_to_all(stacked, 'col', 2, 2, tiled=True).sum(axis=2)  6.68 us
    all_to_all x1, starting transfers between devices, reduce_weights(): stacked = lax.all_to_all(stacked, 'col', 2, 2, tiled=True).sum(axis=2)  5.91 us
  transfers between devices with their start and end apart: 10, of which 6 were waited for; matrix products, arithmetic and copies ran while one was open for 18% of the time, Pallas kernels for 0%

profile of v7, /device:TPU:1, one launch (start us, length us, event | category | flops | bytes accessed | tf_op | source)
XLA Modules:
  0.0 105.0 jit_solution(17795480419521463287)
XLA Ops:
  0.6 1.4 %fusion.124 = (bf16[96,1,256]{2,1,0:T(2,128)(2,1)S(1)}, bf16[96,1,256]{2,1,0:T(2,128)(2,1)S(1)}) fusion(bf16[96,8,256]{2,1,0:T(8,128)(2,1)} %param.6), kind=kLoop, calls=%fused_computation.211 | loop fusion | bytes 196608 | tf_op jit(solution)/shard_map/slice | solution.py:29
  2.0 1.4 %fusion.123 = (bf16[96,1,256]{2,1,0:T(2,128)(2,1)S(1)}, bf16[96,1,256]{2,1,0:T(2,128)(2,1)S(1)}) fusion(bf16[96,8,256]{2,1,0:T(8,128)(2,1)} %param.5), kind=kLoop, calls=%fused_computation.210 | loop fusion | bytes 196608 | tf_op jit(solution)/shard_map/slice | solution.py:29
  3.4 4.0 %collective-permute-start = (bf16[192,1,256]{2,0,1:T(8,128)(2,1)S(1)}, bf16[192,1,256]{2,0,1:T(8,128)(2,1)S(1)}, u32[]{:S(2)}, u32[]{:S(2)}) collective-permute-start(bf16[192,1,256]{2,0,1:T(8,128)(2,1)S(1)} %pad_maximum_fusion.7), channel_id=1, source_target_pairs={{0,8},{8,16},{16,24},{24,32},{32,40},{40,48},{48,56},{56,64},{64,7... | collective-permute-start | bytes 294920 | tf_op jit(solution)/shard_map/ppermute | solution.py:32
  7.5 1.4 %collective-permute-start.1 = (bf16[192,1,256]{2,0,1:T(8,128)(2,1)S(1)}, bf16[192,1,256]{2,0,1:T(8,128)(2,1)S(1)}, u32[]{:S(2)}, u32[]{:S(2)}) collective-permute-start(bf16[192,1,256]{2,0,1:T(8,128)(2,1)S(1)} %pad_maximum_fusion.8), channel_id=1, source_target_pairs={{8,0},{16,8},{24,16},{32,24},{40,32},{48,40},{56,48},{64,56},{72,6... | collective-permute-start | bytes 294920 | tf_op jit(solution)/shard_map/ppermute | solution.py:34
  9.1 1.9 %fusion.53 = f32[96,2048]{1,0:T(8,128)} fusion(bf16[96,2048]{1,0:T(8,128)(2,1)S(1)} %bitcast.351, bf16[3,3,96,96]{3,2,1,0:T(8,128)(2,1)} %param.7), kind=kOutput, calls=%fused_computation.142 | convolution fusion | flops 37748736 | bytes 1204224 | tf_op jit(solution)/shard_map/dot_general | solution.py:87
  11.2 1.8 %collective-permute-done.1 = bf16[192,1,256]{2,0,1:T(8,128)(2,1)S(1)} collective-permute-done((bf16[192,1,256]{2,0,1:T(8,128)(2,1)S(1)}, bf16[192,1,256]{2,0,1:T(8,128)(2,1)S(1)}, u32[]{:S(2)}, u32[]{:S(2)}) %collective-permute-start.1) | collective-permute-done | bytes 98336 | tf_op jit(solution)/shard_map/ppermute | solution.py:34
  13.8 4.0 %collective-permute-start.2 = (bf16[192,10,1]{0,1,2:T(8,128)(2,1)S(1)}, bf16[192,10,1]{0,1,2:T(8,128)(2,1)S(1)}, u32[]{:S(2)}, u32[]{:S(2)}) collective-permute-start(bf16[192,10,1]{0,1,2:T(8,128)(2,1)S(1)} %copy.180), channel_id=1, source_target_pairs={{1,0},{2,1},{3,2},{4,3},{5,4},{6,5},{7,6},{9,8},{10,9},{11,10},{12... | collective-permute-start | bytes 11528 | tf_op jit(solution)/shard_map/ppermute | solution.py:17
  17.8 1.0 copy.181
  18.8 3.0 %collective-permute-start.3 = (bf16[192,10,1]{0,1,2:T(8,128)(2,1)}, bf16[192,10,1]{0,1,2:T(8,128)(2,1)}, u32[]{:S(2)}, u32[]{:S(2)}) collective-permute-start(bf16[192,10,1]{0,1,2:T(8,128)(2,1)} %copy.181), channel_id=1, source_target_pairs={{0,1},{1,2},{2,3},{3,4},{4,5},{5,6},{6,7},{8,9},{9,10},{10,11},{11... | collective-permute-start | bytes 11528 | tf_op jit(solution)/shard_map/ppermute | solution.py:15
  22.0 1.0 convolution_bitcast_fusion.1
  23.0 2.0 %convolution_bitcast_fusion.5 = f32[96,2048]{1,0:T(8,128)} fusion(bf16[96,2048]{1,0:T(8,128)(2,1)S(1)} %bitcast.353, bf16[3,3,96,96]{3,2,1,0:T(8,128)(2,1)} %param.9), kind=kOutput, calls=%fused_computation.5 | convolution fusion | flops 37748736 | bytes 1204224 | tf_op jit(solution)/shard_map/dot_general | solution.py:55
  25.0 0.8 copy.192
  25.8 1.1 %copy.135 = bf16[192,10,1]{2,0,1:T(8,128)(2,1)} copy(bf16[192,10,1]{0,1,2:T(8,128)(2,1)S(1)} %collective-permute-done.2) | data formatting | bytes 7680 | tf_op jit(solution)/shard_map/ppermute | solution.py:17
  26.9 1.8 %copy.139 = bf16[192,10,1]{2,0,1:T(8,128)(2,1)} copy(bf16[192,10,1]{0,1,2:T(8,128)(2,1)} %collective-permute-done.3) | data formatting | bytes 7680 | tf_op jit(solution)/shard_map/ppermute | solution.py:15
  28.6 2.3 %pad_maximum_fusion = (bf16[192,10,257]{2,0,1:T(8,128)(2,1)S(1)}, bf16[192,10,257]{2,0,1:T(8,128)(2,1)S(1)}) fusion(bf16[192,10,1]{2,0,1:T(8,128)(2,1)} %copy.135, bf16[192,1,256]{2,0,1:T(8,128)(2,1)} %copy-done.8, bf16[192,8,256]{2,0,1:T(8,128)(2,1)S(1)} %constant_dynamic-update-slice_fusion, bf16[192,1,256]{2,0,1:T(8,128)(2,1)} %copy-done.7, ...), kind=kLoop, calls=%fused_computation.41 | loop fusion | flops 7895040 | bytes 2964480 | tf_op jit(solution)/shard_map/concatenate | solution.py:13
  31.0 1.1 %slice_bitcast_fusion.4 = (bf16[8,12,8,256]{3,2,1,0:T(8,128)(2,1)S(1)}, bf16[8,12,8,256]{3,2,1,0:T(8,128)(2,1)S(1)}, bf16[8,12,8,256]{3,2,1,0:T(8,128)(2,1)S(1)}...) fusion(bf16[192,10,257]{2,0,1:T(8,128)(2,1)S(1)} %get-tuple-ele, ...), kind=kLoop, calls=%fused_computation.104 | loop fusion | bytes 9437184
  37.3 0.8 copy-done.1
  38.8 0.7 copy-done.9
  40.1 3.2 %collective-permute-start.4 = (bf16[96,1,256]{2,0,1:T(8,128)(2,1)S(1)}, bf16[96,1,256]{2,0,1:T(8,128)(2,1)S(1)}, u32[]{:S(2)}, u32[]{:S(2)}) collective-permute-start(bf16[96,1,256]{2,0,1:T(8,128)(2,1)S(1)} %get-tuple-element.42), channel_id=1, source_target_pairs={{0,8},{8,16},{16,24},{24,32},{32,40},{40,48},{48,56},{56,64},{64,7... | collective-permute-start | bytes 147464 | tf_op jit(solution)/shard_map/ppermute | solution.py:15
  43.3 1.3 %collective-permute-start.5 = (bf16[96,1,256]{2,0,1:T(8,128)(2,1)S(1)}, bf16[96,1,256]{2,0,1:T(8,128)(2,1)S(1)}, u32[]{:S(2)}, u32[]{:S(2)}) collective-permute-start(bf16[96,1,256]{2,0,1:T(8,128)(2,1)S(1)} %get-tuple-element.41), channel_id=1, source_target_pairs={{8,0},{16,8},{24,16},{32,24},{40,32},{48,40},{56,48},{64,56},{72,6... | collective-permute-start | bytes 147464 | tf_op jit(solution)/shard_map/ppermute | solution.py:17
  48.3 3.3 %collective-permute-start.6 = (bf16[96,10,1]{2,0,1:T(8,128)(2,1)S(1)}, bf16[96,10,1]{2,0,1:T(8,128)(2,1)S(1)}, u32[]{:S(2)}, u32[]{:S(2)}) collective-permute-start(bf16[96,10,1]{2,0,1:T(8,128)(2,1)S(1)} %get-tuple-element.37), channel_id=1, source_target_pairs={{1,0},{2,1},{3,2},{4,3},{5,4},{6,5},{7,6},{9,8},{10,9},{11,10},{12... | collective-permute-start | bytes 5768 | tf_op jit(solution)/shard_map/ppermute | solution.py:17
  51.6 3.0 %collective-permute-start.7 = (bf16[96,10,1]{2,0,1:T(8,128)(2,1)S(1)}, bf16[96,10,1]{2,0,1:T(8,128)(2,1)S(1)}, u32[]{:S(2)}, u32[]{:S(2)}) collective-permute-start(bf16[96,10,1]{2,0,1:T(8,128)(2,1)S(1)} %get-tuple-element.36), channel_id=1, source_target_pairs={{0,1},{1,2},{2,3},{3,4},{4,5},{5,6},{6,7},{8,9},{9,10},{10,11},{11... | collective-permute-start | bytes 5768 | tf_op jit(solution)/shard_map/ppermute | solution.py:15
  54.7 0.8 copy.200
  55.5 0.9 collective-permute-done.6
  60.6 0.9 pad_maximum_fusion.2
  61.5 5.9 %all-to-all-start = ((f32[2,32,8,324]{3,1,0,2:T(8,128)}), f32[2,32,8,324]{3,1,0,2:T(8,128)S(1)}, u32[]{:S(2)}, u32[]{:S(2)}) async-start(f32[2,32,8,324]{3,1,0,2:T(8,128)} %pad_maximum_fusion.2), calls=%async_computation | async-start | bytes 1572864 | tf_op jit(solution)/shard_map/all_to_all | solution.py:72
  67.4 2.1 %fusion.43 = (bf16[8,12,8,256]{3,2,1,0:T(8,128)(2,1)S(1)}, bf16[8,12,8,256]{3,2,1,0:T(8,128)(2,1)S(1)}, bf16[8,12,8,256]{3,2,1,0:T(8,128)(2,1)S(1)}, bf16[8,12,8...) fusion(bf16[96,10,256]{2,0,1:T(8,128)(2,1)S(1)} %get-tuple-element.50, ...), kind=kLoop, calls=%fused_computation.123 | loop fusion | flops 4718592 | bytes 2854656
  72.9 6.7 %all-to-all-done = f32[2,32,8,324]{3,1,0,2:T(8,128)S(1)} async-done(((f32[2,32,8,324]{3,1,0,2:T(8,128)}), f32[2,32,8,324]{3,1,0,2:T(8,128)S(1)}, u32[]{:S(2)}, u32[]{:S(2)}) %all-to-all-start) | async-done | bytes 663584 | tf_op jit(solution)/shard_map/all_to_all | solution.py:72
  79.6 0.7 copy.178
  80.3 14.9 %all-to-all-start.1 = ((f32[2,32,324]{2,0,1:T(2,128)}), f32[2,32,324]{2,0,1:T(2,128)S(1)}, u32[]{:S(2)}, u32[]{:S(2)}) async-start(f32[2,32,324]{2,0,1:T(2,128)} %copy.178), calls=%async_computation.1 | async-start | bytes 196608 | tf_op jit(solution)/shard_map/all_to_all | solution.py:73
  95.6 0.8 copy.209
  96.4 7.9 %all-to-all-done.1 = f32[2,32,324]{2,0,1:T(2,128)S(1)} async-done(((f32[2,32,324]{2,0,1:T(2,128)}), f32[2,32,324]{2,0,1:T(2,128)S(1)}, u32[]{:S(2)}, u32[]{:S(2)}) %all-to-all-start.1) | async-done | bytes 82976 | tf_op jit(solution)/shard_map/all_to_all | solution.py:73
  (129 shorter events, 19.6 us)
Async XLA Ops:
  0.6 8.3 %copy-start = (bf16[96,8,256]{2,1,0:T(8,128)(2,1)S(1)}, bf16[96,8,256]{2,1,0:T(8,128)(2,1)}, u32[]{:S(2)}) copy-start(bf16[96,8,256]{2,1,0:T(8,128)(2,1)} %param.5) | copy-start | bytes 1179652
  3.4 7.8 %collective-permute-start = (bf16[192,1,256]{2,0,1:T(8,128)(2,1)S(1)}, bf16[192,1,256]{2,0,1:T(8,128)(2,1)S(1)}, u32[]{:S(2)}, u32[]{:S(2)}) collective-permute-start(bf16[192,1,256]{2,0,1:T(8,128)(2,1)S(1)} %pad_maximum_fusion.7), channel_id=1, source_target_pairs={{0,8},{8,16},{16,24},{24,32},{32,40},{40,48},{48,56},{56,64},{64,7... | collective-permute-start | bytes 294920 | tf_op jit(solution)/shard_map/ppermute | solution.py:32
  7.5 3.5 %copy-start.2 = (bf16[96,8,256]{2,1,0:T(8,128)(2,1)S(1)}, bf16[96,8,256]{2,1,0:T(8,128)(2,1)}, u32[]{:S(2)}) copy-start(bf16[96,8,256]{2,1,0:T(8,128)(2,1)} %param.6) | copy-start | bytes 1179652
  7.5 5.5 %collective-permute-start.1 = (bf16[192,1,256]{2,0,1:T(8,128)(2,1)S(1)}, bf16[192,1,256]{2,0,1:T(8,128)(2,1)S(1)}, u32[]{:S(2)}, u32[]{:S(2)}) collective-permute-start(bf16[192,1,256]{2,0,1:T(8,128)(2,1)S(1)} %pad_maximum_fusion.8), channel_id=1, source_target_pairs={{8,0},{16,8},{24,16},{32,24},{40,32},{48,40},{56,48},{64,56},{72,6... | collective-permute-start | bytes 294920 | tf_op jit(solution)/shard_map/ppermute | solution.py:34
  11.2 10.8 %copy-start.7 = (bf16[192,1,256]{2,0,1:T(8,128)(2,1)}, bf16[192,1,256]{2,0,1:T(8,128)(2,1)S(1)}, u32[]{:S(2)}) copy-start(bf16[192,1,256]{2,0,1:T(8,128)(2,1)S(1)} %collective-permute-done) | copy-start | bytes 294916
  13.0 8.9 %copy-start.8 = (bf16[192,1,256]{2,0,1:T(8,128)(2,1)}, bf16[192,1,256]{2,0,1:T(8,128)(2,1)S(1)}, u32[]{:S(2)}) copy-start(bf16[192,1,256]{2,0,1:T(8,128)(2,1)S(1)} %collective-permute-done.1) | copy-start | bytes 294916
  13.8 12.0 %collective-permute-start.2 = (bf16[192,10,1]{0,1,2:T(8,128)(2,1)S(1)}, bf16[192,10,1]{0,1,2:T(8,128)(2,1)S(1)}, u32[]{:S(2)}, u32[]{:S(2)}) collective-permute-start(bf16[192,10,1]{0,1,2:T(8,128)(2,1)S(1)} %copy.180), channel_id=1, source_target_pairs={{1,0},{2,1},{3,2},{4,3},{5,4},{6,5},{7,6},{9,8},{10,9},{11,10},{12... | collective-permute-start | bytes 11528 | tf_op jit(solution)/shard_map/ppermute | solution.py:17
  18.8 8.1 %collective-permute-start.3 = (bf16[192,10,1]{0,1,2:T(8,128)(2,1)}, bf16[192,10,1]{0,1,2:T(8,128)(2,1)}, u32[]{:S(2)}, u32[]{:S(2)}) collective-permute-start(bf16[192,10,1]{0,1,2:T(8,128)(2,1)} %copy.181), channel_id=1, source_target_pairs={{0,1},{1,2},{2,3},{3,4},{4,5},{5,6},{6,7},{8,9},{9,10},{10,11},{11... | collective-permute-start | bytes 11528 | tf_op jit(solution)/shard_map/ppermute | solution.py:15
  31.0 1.2 %copy-start.5 = (bf16[3,3,96,96]{3,2,1,0:T(8,128)(2,1)S(1)}, bf16[3,3,96,96]{3,2,1,0:T(8,128)(2,1)}, u32[]{:S(2)}) copy-start(bf16[3,3,96,96]{3,2,1,0:T(8,128)(2,1)} %param.7) | copy-start | bytes 497668
  32.8 0.9 copy-start.13
  34.5 1.0 copy-start.3
  36.9 1.1 %copy-start.1 = (f32[96,2048]{1,0:T(8,128)S(1)}, f32[96,2048]{1,0:T(8,128)}, u32[]{:S(2)}) copy-start(f32[96,2048]{1,0:T(8,128)} %fusion.53) | copy-start | bytes 2359300
  37.3 1.1 %copy-start.14 = (f32[96]{0:T(128)S(1)}, f32[96]{0:T(128)}, u32[]{:S(2)}) copy-start(f32[96]{0:T(128)} %param.8) | copy-start | bytes 1156
  38.3 1.1 %copy-start.9 = (f32[96,2048]{1,0:T(8,128)S(1)}, f32[96,2048]{1,0:T(8,128)}, u32[]{:S(2)}) copy-start(f32[96,2048]{1,0:T(8,128)} %convolution_bitcast_fusion.5) | copy-start | bytes 2359300
  40.1 7.5 %collective-permute-start.4 = (bf16[96,1,256]{2,0,1:T(8,128)(2,1)S(1)}, bf16[96,1,256]{2,0,1:T(8,128)(2,1)S(1)}, u32[]{:S(2)}, u32[]{:S(2)}) collective-permute-start(bf16[96,1,256]{2,0,1:T(8,128)(2,1)S(1)} %get-tuple-element.42), channel_id=1, source_target_pairs={{0,8},{8,16},{16,24},{24,32},{32,40},{40,48},{48,56},{56,64},{64,7... | collective-permute-start | bytes 147464 | tf_op jit(solution)/shard_map/ppermute | solution.py:15
  43.3 4.8 %collective-permute-start.5 = (bf16[96,1,256]{2,0,1:T(8,128)(2,1)S(1)}, bf16[96,1,256]{2,0,1:T(8,128)(2,1)S(1)}, u32[]{:S(2)}, u32[]{:S(2)}) collective-permute-start(bf16[96,1,256]{2,0,1:T(8,128)(2,1)S(1)} %get-tuple-element.41), channel_id=1, source_target_pairs={{8,0},{16,8},{24,16},{32,24},{40,32},{48,40},{56,48},{64,56},{72,6... | collective-permute-start | bytes 147464 | tf_op jit(solution)/shard_map/ppermute | solution.py:17
  48.3 8.1 %collective-permute-start.6 = (bf16[96,10,1]{2,0,1:T(8,128)(2,1)S(1)}, bf16[96,10,1]{2,0,1:T(8,128)(2,1)S(1)}, u32[]{:S(2)}, u32[]{:S(2)}) collective-permute-start(bf16[96,10,1]{2,0,1:T(8,128)(2,1)S(1)} %get-tuple-element.37), channel_id=1, source_target_pairs={{1,0},{2,1},{3,2},{4,3},{5,4},{6,5},{7,6},{9,8},{10,9},{11,10},{12... | collective-permute-start | bytes 5768 | tf_op jit(solution)/shard_map/ppermute | solution.py:17
  51.6 6.0 %collective-permute-start.7 = (bf16[96,10,1]{2,0,1:T(8,128)(2,1)S(1)}, bf16[96,10,1]{2,0,1:T(8,128)(2,1)S(1)}, u32[]{:S(2)}, u32[]{:S(2)}) collective-permute-start(bf16[96,10,1]{2,0,1:T(8,128)(2,1)S(1)} %get-tuple-element.36), channel_id=1, source_target_pairs={{0,1},{1,2},{2,3},{3,4},{4,5},{5,6},{6,7},{8,9},{9,10},{10,11},{11... | collective-permute-start | bytes 5768 | tf_op jit(solution)/shard_map/ppermute | solution.py:15
  56.4 2.5 %copy-start.10 = (bf16[96,10,1]{2,0,1:T(8,128)(2,1)}, bf16[96,10,1]{2,0,1:T(8,128)(2,1)S(1)}, u32[]{:S(2)}) copy-start(bf16[96,10,1]{2,0,1:T(8,128)(2,1)S(1)} %collective-permute-done.6) | copy-start | bytes 5764
  57.6 2.0 %copy-start.12 = (bf16[96,10,1]{2,0,1:T(8,128)(2,1)}, bf16[96,10,1]{2,0,1:T(8,128)(2,1)S(1)}, u32[]{:S(2)}) copy-start(bf16[96,10,1]{2,0,1:T(8,128)(2,1)S(1)} %collective-permute-done.7) | copy-start | bytes 5764
  61.5 5.9 %copy-start.11 = (bf16[96,10,1]{2,0,1:T(8,128)(2,1)S(1)}, bf16[96,10,1]{2,0,1:T(8,128)(2,1)}, u32[]{:S(2)}) copy-start(bf16[96,10,1]{2,0,1:T(8,128)(2,1)} %copy-done.10) | copy-start | bytes 5764
  61.5 18.1 %all-to-all-start = ((f32[2,32,8,324]{3,1,0,2:T(8,128)}), f32[2,32,8,324]{3,1,0,2:T(8,128)S(1)}, u32[]{:S(2)}, u32[]{:S(2)}) async-start(f32[2,32,8,324]{3,1,0,2:T(8,128)} %pad_maximum_fusion.2), calls=%async_computation | async-start | bytes 1572864 | tf_op jit(solution)/shard_map/all_to_all | solution.py:72
  67.4 2.2 %copy-start.6 = (bf16[3,3,96,96]{3,2,1,0:T(8,128)(2,1)S(1)}, bf16[3,3,96,96]{3,2,1,0:T(8,128)(2,1)}, u32[]{:S(2)}) copy-start(bf16[3,3,96,96]{3,2,1,0:T(8,128)(2,1)} %param.7) | copy-start | bytes 497668
  69.6 1.0 copy-start.4
  80.3 24.0 %all-to-all-start.1 = ((f32[2,32,324]{2,0,1:T(2,128)}), f32[2,32,324]{2,0,1:T(2,128)S(1)}, u32[]{:S(2)}, u32[]{:S(2)}) async-start(f32[2,32,324]{2,0,1:T(2,128)} %copy.178), calls=%async_computation.1 | async-start | bytes 196608 | tf_op jit(solution)/shard_map/all_to_all | solution.py:73

commit v8 on v6

--- a/solution.py
+++ b/solution.py
@@ -50,6 +50,21 @@
     return (total, jnp.stack(grads).reshape(-1))
 
 
+def grad_taps(upper, padded, tile_rows, tile_cols):
+    return jnp.stack(
+        [
+            lax.dot_general(
+                upper,
+                window(padded, offset_y, offset_x, tile_rows, tile_cols),
+                (((1,), (1,)), ((), ())),
+                preferred_element_type=jnp.float32,
+            )
+            for offset_y in range(3)
+            for offset_x in range(3)
+        ]
+    ).reshape(-1)
+
+
 def reduce_weights(grads):
     rows, cols = lax.axis_size("row"), lax.axis_size("col")
     stacked = jnp.stack(grads).reshape(len(grads), rows, cols, -1)
@@ -80,22 +95,10 @@
     grad_two = grad_two * scale
     sig = jax.nn.sigmoid(hidden)
     hidden_grad = (act_grad * sig * (1.0 + hidden * (1.0 - sig))).astype(jnp.bfloat16)
-    padded_hid = padded_2(
-        hidden_grad.reshape(channels, tile_rows, tile_cols), (("row", 1), ("col", 2)), 1
-    )
+    padded_hid = padded_2(hidden_grad.reshape(channels, tile_rows, tile_cols), (("row", 1),), 1)
+    padded_hid = padded_2(padded_hid, (("col", 2),), 1)
     inner_grad = hidden_grad.reshape(channels, cell_count)
-    grad_one = jnp.stack(
-        [
-            lax.dot_general(
-                inner_grad,
-                window(padded_input, offset_y, offset_x, tile_rows, tile_cols),
-                (((1,), (1,)), ((), ())),
-                preferred_element_type=jnp.float32,
-            )
-            for offset_y in range(3)
-            for offset_x in range(3)
-        ]
-    ).reshape(-1) * scale
+    grad_one = grad_taps(inner_grad, padded_input, tile_rows, tile_cols) * scale
     back_input, _ = backward_taps(padded_hid, weight_one, inner_grad, tile_rows, tile_cols)
     input_grad = (cotangent.reshape(channels, cell_count).astype(jnp.float32) + back_input).astype(
         jnp.bfloat16

time: 106 us -> 106 us (level)
  no operation moved by 1% of the time
where the time goes in v8:
time: 106 us; the launch traced here: 105 us
  starting transfers between devices  41.4 us (39%)
  local copies, waits for them, and re-layouts  19.6 us (18%)
  waiting for transfers between devices  18.1 us (17%)
  matrix products  18 us (17%)
  other arithmetic  6.15 us (6%)
  between operations  1.55 us (1%)
    all_to_all x1, starting transfers between devices, reduce_weights(): summed = lax.all_to_all(stacked, 'row', 1, 1, tiled=True).sum(axis=1)  14.7 us
    ppermute x4, starting transfers between devices, padded_2(): lax.ppermute(tail, axis, [(i, (i + 1) % count) for i in range(ends)])  13.6 us
    ppermute x4, waiting for transfers between devices, padded_2(): lax.ppermute(head, axis, [((i + 1) % count, i) for i in range(ends)])  10.1 us
    ppermute x4, starting transfers between devices, padded_2(): lax.ppermute(head, axis, [((i + 1) % count, i) for i in range(ends)])  9.04 us
    all_to_all x1, waiting for transfers between devices, reduce_weights(): summed = lax.all_to_all(stacked, 'row', 1, 1, tiled=True).sum(axis=1)  7.94 us
    unnamed x52, local copies, waits for them, and re-layouts  7.53 us
    dot_general x18, matrix products, backward_taps(): lax.dot_general(kernel[offset_y, offset_x], patch, (((0,), (0,)), ((), ()...  7.49 us
    dot_general x9, matrix products, block(): jnp.dot(weight_one[offset_y, offset_x], patch, preferred_element_type=jnp...  5.79 us
  transfers between devices with their start and end apart: 10, of which 4 were waited for; matrix products, arithmetic and copies ran while one was open for 17% of the time, Pallas kernels for 0%

profile of v8, /device:TPU:1, one launch (start us, length us, event | category | flops | bytes accessed | tf_op | source)
XLA Modules:
  0.0 104.8 jit_solution(9387287812272431946)
XLA Ops:
  0.6 1.1 %copy_dynamic-update-slice_fusion.1 = bf16[192,8,256]{2,0,1:T(8,128)(2,1)S(1)} fusion(bf16[96,8,256]{2,1,0:T(8,128)(2,1)} %param.5), kind=kLoop, calls=%fused_computation.107 | loop fusion | bytes 786432
  1.8 1.1 %copy_dynamic-update-slice_fusion = bf16[192,8,256]{2,0,1:T(8,128)(2,1)S(1)} fusion(bf16[192,8,256]{2,0,1:T(8,128)(2,1)S(1)} %copy_dynamic-update-slice_fusion.1, bf16[96,8,256]{2,1,0:T(8,128)(2,1)} %param.6), kind=kLoop, calls=%fused_computation.106 | loop fusion | bytes 786432 | tf_op jit(solution)/shard_map/concatenate | solution.py:82
  3.0 4.0 %collective-permute-start = (bf16[192,1,256]{2,0,1:T(8,128)(2,1)S(1)}, bf16[192,1,256]{2,0,1:T(8,128)(2,1)S(1)}, u32[]{:S(2)}, u32[]{:S(2)}) collective-permute-start(bf16[192,1,256]{2,0,1:T(8,128)(2,1)S(1)} %get-tuple-element.35), channel_id=1, source_target_pairs={{0,8},{8,16},{16,24},{24,32},{32,40},{40,48},{48,56},{56,64},{64,7... | collective-permute-start | bytes 294920 | tf_op jit(solution)/shard_map/ppermute | solution.py:15
  7.0 1.3 %collective-permute-start.1 = (bf16[192,1,256]{2,0,1:T(8,128)(2,1)S(1)}, bf16[192,1,256]{2,0,1:T(8,128)(2,1)S(1)}, u32[]{:S(2)}, u32[]{:S(2)}) collective-permute-start(bf16[192,1,256]{2,0,1:T(8,128)(2,1)S(1)} %get-tuple-element.36), channel_id=1, source_target_pairs={{8,0},{16,8},{24,16},{32,24},{40,32},{48,40},{56,48},{64,56},{72,6... | collective-permute-start | bytes 294920 | tf_op jit(solution)/shard_map/ppermute | solution.py:17
  8.4 1.9 %fusion.47 = f32[96,2048]{1,0:T(8,128)} fusion(bf16[96,2048]{1,0:T(8,128)(2,1)S(1)} %bitcast.347, bf16[3,3,96,96]{3,2,1,0:T(8,128)(2,1)} %param.7), kind=kOutput, calls=%fused_computation.119 | convolution fusion | flops 37748736 | bytes 1204224 | tf_op jit(solution)/shard_map/dot_general | solution.py:89
  10.4 1.9 %collective-permute-done.1 = bf16[192,1,256]{2,0,1:T(8,128)(2,1)S(1)} collective-permute-done((bf16[192,1,256]{2,0,1:T(8,128)(2,1)S(1)}, bf16[192,1,256]{2,0,1:T(8,128)(2,1)S(1)}, u32[]{:S(2)}, u32[]{:S(2)}) %collective-permute-start.1) | collective-permute-done | bytes 98336 | tf_op jit(solution)/shard_map/ppermute | solution.py:17
  13.1 4.0 %collective-permute-start.2 = (bf16[192,10,1]{0,1,2:T(8,128)(2,1)S(1)}, bf16[192,10,1]{0,1,2:T(8,128)(2,1)S(1)}, u32[]{:S(2)}, u32[]{:S(2)}) collective-permute-start(bf16[192,10,1]{0,1,2:T(8,128)(2,1)S(1)} %copy.45), channel_id=1, source_target_pairs={{1,0},{2,1},{3,2},{4,3},{5,4},{6,5},{7,6},{9,8},{10,9},{11,10},{12... | collective-permute-start | bytes 11528 | tf_op jit(solution)/shard_map/ppermute | solution.py:17
  17.5 3.0 %collective-permute-start.3 = (bf16[192,10,1]{0,1,2:T(8,128)(2,1)S(1)}, bf16[192,10,1]{0,1,2:T(8,128)(2,1)S(1)}, u32[]{:S(2)}, u32[]{:S(2)}) collective-permute-start(bf16[192,10,1]{0,1,2:T(8,128)(2,1)S(1)} %copy.49), channel_id=1, source_target_pairs={{0,1},{1,2},{2,3},{3,4},{4,5},{5,6},{6,7},{8,9},{9,10},{10,11},{11... | collective-permute-start | bytes 11528 | tf_op jit(solution)/shard_map/ppermute | solution.py:15
  20.7 1.9 %convolution_bitcast_fusion.1 = f32[96,2048]{1,0:T(8,128)} fusion(bf16[96,2048]{1,0:T(8,128)(2,1)S(1)} %bitcast.349, bf16[3,3,96,96]{3,2,1,0:T(8,128)(2,1)} %param.7), kind=kOutput, calls=%fused_computation.1 | convolution fusion | flops 37748736 | bytes 1204224 | tf_op jit(solution)/shard_map/dot_general | solution.py:89
  22.7 1.9 %convolution_bitcast_fusion.5 = f32[96,2048]{1,0:T(8,128)} fusion(bf16[96,2048]{1,0:T(8,128)(2,1)S(1)} %bitcast.345, bf16[3,3,96,96]{3,2,1,0:T(8,128)(2,1)} %param.9), kind=kOutput, calls=%fused_computation.5 | convolution fusion | flops 37748736 | bytes 1204224 | tf_op jit(solution)/shard_map/dot_general | solution.py:39
  24.6 0.8 copy.79
  25.4 0.8 copy.71
  26.9 1.1 %pad_maximum_fusion = (bf16[192,10,257]{2,0,1:T(8,128)(2,1)S(1)}, bf16[192,10,257]{2,0,1:T(8,128)(2,1)S(1)}) fusion(bf16[192,10,1]{2,0,1:T(8,128)(2,1)S(1)} %copy.46, bf16[192,1,256]{2,0,1:T(8,128)(2,1)S(1)} %collective-permute-done.1, bf16[192,8,256]{2,0,1:T(8,128)(2,1)S(1)} %copy_dynamic-update-slice_fusion, ...), kind=kLoop, calls=%fused_computation.41 | loop fusion | flops 7895040 | bytes 2964480 | tf_op jit(solution)/shard_map/concatenate | solution.py:13
  28.0 1.1 %slice_bitcast_fusion.2 = (bf16[8,12,8,256]{3,2,1,0:T(8,128)(2,1)S(1)}, bf16[8,12,8,256]{3,2,1,0:T(8,128)(2,1)S(1)}, bf16[8,12,8,256]{3,2,1,0:T(8,128)(2,1)S(1)}...) fusion(bf16[192,10,257]{2,0,1:T(8,128)(2,1)S(1)} %get-tuple-ele, ...), kind=kLoop, calls=%fused_computation.92 | loop fusion | bytes 9437184
  33.0 0.7 copy-done
  35.1 0.8 copy-done.8
  40.4 0.8 broadcast_multiply_fusion.1
  41.2 2.2 %mul.45 = f32[1,32,8,324]{3,2,1,0:T(8,128)} reshape(f32[9,96,96]{2,1,0:T(8,128)} %broadcast_multiply_fusion.1) | data formatting | bytes 663552 | tf_op jit(solution)/shard_map/mul | solution.py:101
  43.4 1.9 %copy.66 = f32[1,32,8,324]{3,1,0,2:T(8,128)} copy(f32[1,32,8,324]{3,2,1,0:T(8,128)} %mul.45) | data formatting | bytes 663552 | tf_op jit(solution)/shard_map/mul | solution.py:101
  48.6 3.2 %collective-permute-start.4 = (bf16[96,1,256]{2,1,0:T(2,128)(2,1)S(1)}, bf16[96,1,256]{2,1,0:T(2,128)(2,1)S(1)}, u32[]{:S(2)}, u32[]{:S(2)}) collective-permute-start(bf16[96,1,256]{2,1,0:T(2,128)(2,1)S(1)} %get-tuple-element.41), channel_id=1, source_target_pairs={{0,8},{8,16},{16,24},{24,32},{32,40},{40,48},{48,56},{56,64},{64,7... | collective-permute-start | bytes 147464 | tf_op jit(solution)/shard_map/ppermute | solution.py:15
  51.8 1.3 %collective-permute-start.5 = (bf16[96,1,256]{2,1,0:T(2,128)(2,1)S(1)}, bf16[96,1,256]{2,1,0:T(2,128)(2,1)S(1)}, u32[]{:S(2)}, u32[]{:S(2)}) collective-permute-start(bf16[96,1,256]{2,1,0:T(2,128)(2,1)S(1)} %get-tuple-element.42), channel_id=1, source_target_pairs={{8,0},{16,8},{24,16},{32,24},{40,32},{48,40},{56,48},{64,56},{72,6... | collective-permute-start | bytes 147464 | tf_op jit(solution)/shard_map/ppermute | solution.py:17
  53.2 1.0 pad_maximum_fusion.4
  54.1 4.1 %all-to-all-start = ((f32[2,32,8,324]{3,1,0,2:T(8,128)}), f32[2,32,8,324]{3,1,0,2:T(8,128)S(1)}, u32[]{:S(2)}, u32[]{:S(2)}) async-start(f32[2,32,8,324]{3,1,0,2:T(8,128)} %pad_maximum_fusion.4), calls=%async_computation | async-start | bytes 1572864 | tf_op jit(solution)/shard_map/all_to_all | solution.py:71
  59.1 2.4 %collective-permute-start.6 = (bf16[96,10,1]{2,1,0:T(8,128)(2,1)S(1)}, bf16[96,10,1]{2,1,0:T(8,128)(2,1)S(1)}, u32[]{:S(2)}, u32[]{:S(2)}) collective-permute-start(bf16[96,10,1]{2,1,0:T(8,128)(2,1)S(1)} %get-tuple-element.32), channel_id=1, source_target_pairs={{1,0},{2,1},{3,2},{4,3},{5,4},{6,5},{7,6},{9,8},{10,9},{11,10},{12... | collective-permute-start | bytes 5768 | tf_op jit(solution)/shard_map/ppermute | solution.py:17
  61.6 3.3 %collective-permute-start.7 = (bf16[96,10,1]{2,1,0:T(8,128)(2,1)S(1)}, bf16[96,10,1]{2,1,0:T(8,128)(2,1)S(1)}, u32[]{:S(2)}, u32[]{:S(2)}) collective-permute-start(bf16[96,10,1]{2,1,0:T(8,128)(2,1)S(1)} %get-tuple-element.31), channel_id=1, source_target_pairs={{0,1},{1,2},{2,3},{3,4},{4,5},{5,6},{6,7},{8,9},{9,10},{10,11},{11... | collective-permute-start | bytes 5768 | tf_op jit(solution)/shard_map/ppermute | solution.py:15
  65.4 8.0 %collective-permute-done.6 = bf16[96,10,1]{2,1,0:T(8,128)(2,1)S(1)} collective-permute-done((bf16[96,10,1]{2,1,0:T(8,128)(2,1)S(1)}, bf16[96,10,1]{2,1,0:T(8,128)(2,1)S(1)}, u32[]{:S(2)}, u32[]{:S(2)}) %collective-permute-start.6) | collective-permute-done | bytes 1952 | tf_op jit(solution)/shard_map/ppermute | solution.py:17
  73.4 2.0 %maximum_maximum_fusion.1 = (bf16[96,10,257]{2,1,0:T(8,128)(2,1)S(1)}, bf16[96,10,257]{2,1,0:T(8,128)(2,1)S(1)}) fusion(bf16[96,1,256]{2,1,0:T(2,128)(2,1)S(1)} %collective-permute-done.5, bf16[96,8,256]{2,1,0:T(8,128)(2,1)S(1)} %bitcast.339, bf16[96,1,256]{2,1,0:T(2,128)(2,1)S(1)} %collective-permute-done.4, ...), kind=kLoop, calls=%fused_computation.44 | loop fusion | flops 3947520 | bytes 1482240 | tf_op jit(solution)/shard_map/concatenate | solution.py:13
  75.4 0.8 fusion.97
  79.6 0.7 copy.68
  80.3 14.7 %all-to-all-start.1 = ((f32[2,32,324]{2,0,1:T(2,128)}), f32[2,32,324]{2,0,1:T(2,128)S(1)}, u32[]{:S(2)}, u32[]{:S(2)}) async-start(f32[2,32,324]{2,0,1:T(2,128)} %copy.68), calls=%async_computation.1 | async-start | bytes 196608 | tf_op jit(solution)/shard_map/all_to_all | solution.py:73
  95.3 0.8 copy.97
  96.2 7.9 %all-to-all-done.1 = f32[2,32,324]{2,0,1:T(2,128)S(1)} async-done(((f32[2,32,324]{2,0,1:T(2,128)}), f32[2,32,324]{2,0,1:T(2,128)S(1)}, u32[]{:S(2)}, u32[]{:S(2)}) %all-to-all-start.1) | async-done | bytes 82976 | tf_op jit(solution)/shard_map/all_to_all | solution.py:73
  (129 shorter events, 20.4 us)
Async XLA Ops:
  0.6 7.7 %copy-start.9 = (bf16[96,8,256]{2,1,0:T(8,128)(2,1)S(1)}, bf16[96,8,256]{2,1,0:T(8,128)(2,1)}, u32[]{:S(2)}) copy-start(bf16[96,8,256]{2,1,0:T(8,128)(2,1)} %param.5) | copy-start | bytes 1179652
  1.8 8.5 %copy-start.10 = (bf16[96,8,256]{2,1,0:T(8,128)(2,1)S(1)}, bf16[96,8,256]{2,1,0:T(8,128)(2,1)}, u32[]{:S(2)}) copy-start(bf16[96,8,256]{2,1,0:T(8,128)(2,1)} %param.6) | copy-start | bytes 1179652
  3.0 7.4 %collective-permute-start = (bf16[192,1,256]{2,0,1:T(8,128)(2,1)S(1)}, bf16[192,1,256]{2,0,1:T(8,128)(2,1)S(1)}, u32[]{:S(2)}, u32[]{:S(2)}) collective-permute-start(bf16[192,1,256]{2,0,1:T(8,128)(2,1)S(1)} %get-tuple-element.35), channel_id=1, source_target_pairs={{0,8},{8,16},{16,24},{24,32},{32,40},{40,48},{48,56},{56,64},{64,7... | collective-permute-start | bytes 294920 | tf_op jit(solution)/shard_map/ppermute | solution.py:15
  7.0 5.4 %collective-permute-start.1 = (bf16[192,1,256]{2,0,1:T(8,128)(2,1)S(1)}, bf16[192,1,256]{2,0,1:T(8,128)(2,1)S(1)}, u32[]{:S(2)}, u32[]{:S(2)}) collective-permute-start(bf16[192,1,256]{2,0,1:T(8,128)(2,1)S(1)} %get-tuple-element.36), channel_id=1, source_target_pairs={{8,0},{16,8},{24,16},{32,24},{40,32},{48,40},{56,48},{64,56},{72,6... | collective-permute-start | bytes 294920 | tf_op jit(solution)/shard_map/ppermute | solution.py:17
  13.1 13.1 %collective-permute-start.2 = (bf16[192,10,1]{0,1,2:T(8,128)(2,1)S(1)}, bf16[192,10,1]{0,1,2:T(8,128)(2,1)S(1)}, u32[]{:S(2)}, u32[]{:S(2)}) collective-permute-start(bf16[192,10,1]{0,1,2:T(8,128)(2,1)S(1)} %copy.45), channel_id=1, source_target_pairs={{1,0},{2,1},{3,2},{4,3},{5,4},{6,5},{7,6},{9,8},{10,9},{11,10},{12... | collective-permute-start | bytes 11528 | tf_op jit(solution)/shard_map/ppermute | solution.py:17
  17.5 9.0 %collective-permute-start.3 = (bf16[192,10,1]{0,1,2:T(8,128)(2,1)S(1)}, bf16[192,10,1]{0,1,2:T(8,128)(2,1)S(1)}, u32[]{:S(2)}, u32[]{:S(2)}) collective-permute-start(bf16[192,10,1]{0,1,2:T(8,128)(2,1)S(1)} %copy.49), channel_id=1, source_target_pairs={{0,1},{1,2},{2,3},{3,4},{4,5},{5,6},{6,7},{8,9},{9,10},{10,11},{11... | collective-permute-start | bytes 11528 | tf_op jit(solution)/shard_map/ppermute | solution.py:15
  28.0 1.1 %copy-start.14 = (bf16[3,3,96,96]{3,2,1,0:T(8,128)(2,1)S(1)}, bf16[3,3,96,96]{3,2,1,0:T(8,128)(2,1)}, u32[]{:S(2)}) copy-start(bf16[3,3,96,96]{3,2,1,0:T(8,128)(2,1)} %param.7) | copy-start | bytes 497668
  29.8 0.9 copy-start.17
  31.1 3.0 %copy-start.5 = (bf16[8,12,8,256]{3,2,0,1:T(8,128)(2,1)}, bf16[8,12,8,256]{3,2,0,1:T(8,128)(2,1)S(1)}, u32[]{:S(2)}) copy-start(bf16[8,12,8,256]{3,2,0,1:T(8,128)(2,1)S(1)} %copy.72) | copy-start | bytes 1179652
  31.2 3.3 %copy-start.3 = (bf16[8,12,8,256]{3,2,0,1:T(8,128)(2,1)}, bf16[8,12,8,256]{3,2,0,1:T(8,128)(2,1)S(1)}, u32[]{:S(2)}) copy-start(bf16[8,12,8,256]{3,2,0,1:T(8,128)(2,1)S(1)} %copy.73) | copy-start | bytes 1179652
  31.5 1.0 copy-start.2
  31.9 4.8 %copy-start.11 = (bf16[8,12,8,256]{3,2,0,1:T(8,128)(2,1)}, bf16[8,12,8,256]{3,2,0,1:T(8,128)(2,1)S(1)}, u32[]{:S(2)}) copy-start(bf16[8,12,8,256]{3,2,0,1:T(8,128)(2,1)S(1)} %copy.74) | copy-start | bytes 1179652
  32.8 1.0 copy-start
  34.8 1.1 %copy-start.8 = (f32[96,2048]{1,0:T(8,128)S(1)}, f32[96,2048]{1,0:T(8,128)}, u32[]{:S(2)}) copy-start(f32[96,2048]{1,0:T(8,128)} %fusion.47) | copy-start | bytes 2359300
  35.1 1.2 %copy-start.7 = (f32[96,2048]{1,0:T(8,128)S(1)}, f32[96,2048]{1,0:T(8,128)}, u32[]{:S(2)}) copy-start(f32[96,2048]{1,0:T(8,128)} %convolution_bitcast_fusion.1) | copy-start | bytes 2359300
  35.1 1.2 %copy-start.18 = (f32[96]{0:T(128)S(1)}, f32[96]{0:T(128)}, u32[]{:S(2)}) copy-start(f32[96]{0:T(128)} %param.8) | copy-start | bytes 1156
  36.3 1.1 %copy-start.16 = (f32[96,2048]{1,0:T(8,128)S(1)}, f32[96,2048]{1,0:T(8,128)}, u32[]{:S(2)}) copy-start(f32[96,2048]{1,0:T(8,128)} %convolution_bitcast_fusion.5) | copy-start | bytes 2359300
  40.4 5.2 %copy-start.1 = (bf16[8,12,8,256]{3,2,0,1:T(8,128)(2,1)S(1)}, bf16[8,12,8,256]{3,2,0,1:T(8,128)(2,1)}, u32[]{:S(2)}) copy-start(bf16[8,12,8,256]{3,2,0,1:T(8,128)(2,1)} %copy.71) | copy-start | bytes 1179652
  43.4 2.5 %copy-start.6 = (bf16[8,12,8,256]{3,2,0,1:T(8,128)(2,1)S(1)}, bf16[8,12,8,256]{3,2,0,1:T(8,128)(2,1)}, u32[]{:S(2)}) copy-start(bf16[8,12,8,256]{3,2,0,1:T(8,128)(2,1)} %copy-done.5) | copy-start | bytes 1179652
  43.4 2.8 %copy-start.4 = (bf16[8,12,8,256]{3,2,0,1:T(8,128)(2,1)S(1)}, bf16[8,12,8,256]{3,2,0,1:T(8,128)(2,1)}, u32[]{:S(2)}) copy-start(bf16[8,12,8,256]{3,2,0,1:T(8,128)(2,1)} %copy-done.3) | copy-start | bytes 1179652
  45.6 1.1 %copy-start.12 = (bf16[8,12,8,256]{3,2,0,1:T(8,128)(2,1)S(1)}, bf16[8,12,8,256]{3,2,0,1:T(8,128)(2,1)}, u32[]{:S(2)}) copy-start(bf16[8,12,8,256]{3,2,0,1:T(8,128)(2,1)} %copy-done.11) | copy-start | bytes 1179652
  47.9 5.3 %copy-start.13 = (f32[1,32,8,324]{3,1,0,2:T(8,128)S(1)}, f32[1,32,8,324]{3,1,0,2:T(8,128)}, u32[]{:S(2)}) copy-start(f32[1,32,8,324]{3,1,0,2:T(8,128)} %copy.66) | copy-start | bytes 995332
  48.6 9.6 %collective-permute-start.4 = (bf16[96,1,256]{2,1,0:T(2,128)(2,1)S(1)}, bf16[96,1,256]{2,1,0:T(2,128)(2,1)S(1)}, u32[]{:S(2)}, u32[]{:S(2)}) collective-permute-start(bf16[96,1,256]{2,1,0:T(2,128)(2,1)S(1)} %get-tuple-element.41), channel_id=1, source_target_pairs={{0,8},{8,16},{16,24},{24,32},{32,40},{40,48},{48,56},{56,64},{64,7... | collective-permute-start | bytes 147464 | tf_op jit(solution)/shard_map/ppermute | solution.py:15
  51.8 6.6 %collective-permute-start.5 = (bf16[96,1,256]{2,1,0:T(2,128)(2,1)S(1)}, bf16[96,1,256]{2,1,0:T(2,128)(2,1)S(1)}, u32[]{:S(2)}, u32[]{:S(2)}) collective-permute-start(bf16[96,1,256]{2,1,0:T(2,128)(2,1)S(1)} %get-tuple-element.42), channel_id=1, source_target_pairs={{8,0},{16,8},{24,16},{32,24},{40,32},{48,40},{56,48},{64,56},{72,6... | collective-permute-start | bytes 147464 | tf_op jit(solution)/shard_map/ppermute | solution.py:17
  54.1 25.4 %all-to-all-start = ((f32[2,32,8,324]{3,1,0,2:T(8,128)}), f32[2,32,8,324]{3,1,0,2:T(8,128)S(1)}, u32[]{:S(2)}, u32[]{:S(2)}) async-start(f32[2,32,8,324]{3,1,0,2:T(8,128)} %pad_maximum_fusion.4), calls=%async_computation | async-start | bytes 1572864 | tf_op jit(solution)/shard_map/all_to_all | solution.py:71
  59.1 14.3 %collective-permute-start.6 = (bf16[96,10,1]{2,1,0:T(8,128)(2,1)S(1)}, bf16[96,10,1]{2,1,0:T(8,128)(2,1)S(1)}, u32[]{:S(2)}, u32[]{:S(2)}) collective-permute-start(bf16[96,10,1]{2,1,0:T(8,128)(2,1)S(1)} %get-tuple-element.32), channel_id=1, source_target_pairs={{1,0},{2,1},{3,2},{4,3},{5,4},{6,5},{7,6},{9,8},{10,9},{11,10},{12... | collective-permute-start | bytes 5768 | tf_op jit(solution)/shard_map/ppermute | solution.py:17
  61.6 11.8 %collective-permute-start.7 = (bf16[96,10,1]{2,1,0:T(8,128)(2,1)S(1)}, bf16[96,10,1]{2,1,0:T(8,128)(2,1)S(1)}, u32[]{:S(2)}, u32[]{:S(2)}) collective-permute-start(bf16[96,10,1]{2,1,0:T(8,128)(2,1)S(1)} %get-tuple-element.31), channel_id=1, source_target_pairs={{0,1},{1,2},{2,3},{3,4},{4,5},{5,6},{6,7},{8,9},{9,10},{10,11},{11... | collective-permute-start | bytes 5768 | tf_op jit(solution)/shard_map/ppermute | solution.py:15
  75.4 0.9 copy-start.15
  80.3 23.8 %all-to-all-start.1 = ((f32[2,32,324]{2,0,1:T(2,128)}), f32[2,32,324]{2,0,1:T(2,128)S(1)}, u32[]{:S(2)}, u32[]{:S(2)}) async-start(f32[2,32,324]{2,0,1:T(2,128)} %copy.68), calls=%async_computation.1 | async-start | bytes 196608 | tf_op jit(solution)/shard_map/all_to_all | solution.py:73

commit v9 on v5

--- a/solution.py
+++ b/solution.py
@@ -10,14 +10,18 @@
         ends = count - 1
         head = lax.slice_in_dim(cells, 0, width, axis=dim)
         tail = lax.slice_in_dim(cells, cells.shape[dim] - width, cells.shape[dim], axis=dim)
-        cells = jnp.concatenate(
-            [
-                lax.ppermute(tail, axis, [(i, (i + 1) % count) for i in range(ends)]),
-                cells,
-                lax.ppermute(head, axis, [((i + 1) % count, i) for i in range(ends)]),
-            ],
-            axis=dim,
-        )
+        before = lax.ppermute(tail, axis, [(i, (i + 1) % count) for i in range(ends)])
+        after = lax.ppermute(head, axis, [((i + 1) % count, i) for i in range(ends)])
+        if dim == cells.ndim - 1 and width == 1:
+            spread = [(0, 0)] * dim + [(1, 1)]
+            lane = lax.broadcasted_iota(jnp.int32, (cells.shape[dim] + 2,), 0)
+            cells = jnp.where(
+                lane == 0,
+                before,
+                jnp.where(lane == cells.shape[dim] + 1, after, jnp.pad(cells, spread)),
+            )
+        else:
+            cells = jnp.concatenate([before, cells, after], axis=dim)
     return cells
 
 

time: 105 us -> 104 us (level)
  waiting for transfers between devices: 18.4 us -> 25.6 us
  matrix products: 17.7 us -> 14.8 us
  starting transfers between devices: 44 us -> 41.2 us
  local copies, waits for them, and re-layouts: 17 us -> 15.8 us
  other arithmetic: 5.79 us -> 4.69 us
    ppermute x4, waiting for transfers between devices: 3.25 us -> 11.6 us  [padded_2(): lax.ppermute(head, axis, [((i + 1) % count, i) for i in range(ends)])]
    ppermute x4, starting transfers between devices: 9.9 us -> 6.61 us  [padded_2(): lax.ppermute(head, axis, [((i + 1) % count, i) for i in range(ends)])]
    ppermute x2 -> x0, local copies, waits for them, and re-layouts: 2.82 us -> none  [the longest x1 1.76 us: padded_2(): lax.ppermute(tail, axis, [(i, (i + 1) % count) for i in range(ends)])]
    unnamed x38 -> x31, local copies, waits for them, and re-layouts: 6.63 us -> 9.4 us
    ppermute x4, starting transfers between devices: 13.2 us -> 15.9 us  [padded_2(): lax.ppermute(tail, axis, [(i, (i + 1) % count) for i in range(ends)])]
    dot_general x9, matrix products: 4.83 us -> 2.41 us  [local(): jnp.dot(weight_one[offset_y, offset_x], patch, preferred_element_type=jnp...]
    concatenate x2 -> x1, other arithmetic: 2.44 us -> 0.12 us  [padded_2(): cells = jnp.concatenate([before, cells, after], axis=dim)]
    unnamed x2 -> x0, other arithmetic: 2.21 us -> none
  transfers between devices with their start and end apart: 10 -> 10, of which waited for: 6 -> 7; matrix products, arithmetic and copies ran while one was open for 18% -> 10% of each run, Pallas kernels for 0% -> 0%
where the time goes in v9:
time: 104 us
  starting transfers between devices  41.2 us (40%)
  waiting for transfers between devices  25.6 us (25%)
  local copies, waits for them, and re-layouts  15.8 us (15%)
  matrix products  14.8 us (14%)
  other arithmetic  4.69 us (5%)
  between operations  1.53 us (1%)
    ppermute x4, starting transfers between devices, padded_2(): lax.ppermute(tail, axis, [(i, (i + 1) % count) for i in range(ends)])  15.9 us
    all_to_all x1, starting transfers between devices, reduce_weights(): summed = lax.all_to_all(stacked, 'row', 1, 1, tiled=True).sum(axis=1)  14.7 us
    ppermute x4, waiting for transfers between devices, padded_2(): lax.ppermute(head, axis, [((i + 1) % count, i) for i in range(ends)])  11.6 us
    unnamed x31, local copies, waits for them, and re-layouts  9.4 us
    dot_general x18, matrix products, backward_taps(): lax.dot_general(kernel[offset_y, offset_x], patch, (((0,), (0,)), ((), ()...  7.26 us
    all_to_all x1, waiting for transfers between devices, reduce_weights(): summed = lax.all_to_all(stacked, 'row', 1, 1, tiled=True).sum(axis=1)  7.2 us
    ppermute x4, starting transfers between devices, padded_2(): lax.ppermute(head, axis, [((i + 1) % count, i) for i in range(ends)])  6.61 us
    all_to_all x1, waiting for transfers between devices, reduce_weights(): stacked = lax.all_to_all(stacked, 'col', 2, 2, tiled=True).sum(axis=2)  6.52 us
  transfers between devices with their start and end apart: 10, of which 7 were waited for; matrix products, arithmetic and copies ran while one was open for 10% of the time, Pallas kernels for 0%

profile of v9, /device:TPU:1, one launch (start us, length us, event | category | flops | bytes accessed | tf_op | source)
XLA Modules:
  0.0 103.7 jit_solution(4289507327629619468)
XLA Ops:
  0.6 1.1 %constant_dynamic-update-slice_fusion = bf16[192,8,256]{2,0,1:T(8,128)(2,1)S(1)} fusion(bf16[96,8,256]{2,1,0:T(8,128)(2,1)} %param.5), kind=kLoop, calls=%fused_computation.115 | loop fusion | bytes 786432
  1.7 1.1 %copy_dynamic-update-slice_fusion = bf16[192,8,256]{2,0,1:T(8,128)(2,1)S(1)} fusion(bf16[192,8,256]{2,0,1:T(8,128)(2,1)S(1)} %constant_dynamic-update-slice_fusion, bf16[96,8,256]{2,1,0:T(8,128)(2,1)} %param.6), kind=kLoop, calls=%fused_computation.94 | loop fusion | bytes 786432 | tf_op jit(solution)/shard_map/concatenate | solution.py:70
  2.8 4.0 %collective-permute-start = (bf16[192,1,256]{2,0,1:T(8,128)(2,1)S(1)}, bf16[192,1,256]{2,0,1:T(8,128)(2,1)S(1)}, u32[]{:S(2)}, u32[]{:S(2)}) collective-permute-start(bf16[192,1,256]{2,0,1:T(8,128)(2,1)S(1)} %get-tuple-element.25), channel_id=1, source_target_pairs={{0,8},{8,16},{16,24},{24,32},{32,40},{40,48},{48,56},{56,64},{64,7... | collective-permute-start | bytes 294920 | tf_op jit(solution)/shard_map/ppermute | solution.py:13
  6.8 1.3 %collective-permute-start.1 = (bf16[192,1,256]{2,0,1:T(8,128)(2,1)S(1)}, bf16[192,1,256]{2,0,1:T(8,128)(2,1)S(1)}, u32[]{:S(2)}, u32[]{:S(2)}) collective-permute-start(bf16[192,1,256]{2,0,1:T(8,128)(2,1)S(1)} %get-tuple-element.26), channel_id=1, source_target_pairs={{8,0},{16,8},{24,16},{32,24},{40,32},{48,40},{56,48},{64,56},{72,6... | collective-permute-start | bytes 294920 | tf_op jit(solution)/shard_map/ppermute | solution.py:14
  8.5 3.7 %collective-permute-done.1 = bf16[192,1,256]{2,0,1:T(8,128)(2,1)S(1)} collective-permute-done((bf16[192,1,256]{2,0,1:T(8,128)(2,1)S(1)}, bf16[192,1,256]{2,0,1:T(8,128)(2,1)S(1)}, u32[]{:S(2)}, u32[]{:S(2)}) %collective-permute-start.1) | collective-permute-done | bytes 98336 | tf_op jit(solution)/shard_map/ppermute | solution.py:14
  13.0 5.1 %collective-permute-start.2 = (bf16[192,10,1]{0,1,2:T(8,128)(2,1)S(1)}, bf16[192,10,1]{0,1,2:T(8,128)(2,1)S(1)}, u32[]{:S(2)}, u32[]{:S(2)}) collective-permute-start(bf16[192,10,1]{0,1,2:T(8,128)(2,1)S(1)} %copy.175), channel_id=1, source_target_pairs={{0,1},{1,2},{2,3},{3,4},{4,5},{5,6},{6,7},{8,9},{9,10},{10,11},{11... | collective-permute-start | bytes 11528 | tf_op jit(solution)/shard_map/ppermute | solution.py:13
  18.5 1.9 %collective-permute-start.3 = (bf16[192,10,1]{0,1,2:T(8,128)(2,1)S(1)}, bf16[192,10,1]{0,1,2:T(8,128)(2,1)S(1)}, u32[]{:S(2)}, u32[]{:S(2)}) collective-permute-start(bf16[192,10,1]{0,1,2:T(8,128)(2,1)S(1)} %copy.176), channel_id=1, source_target_pairs={{1,0},{2,1},{3,2},{4,3},{5,4},{6,5},{7,6},{9,8},{10,9},{11,10},{12... | collective-permute-start | bytes 11528 | tf_op jit(solution)/shard_map/ppermute | solution.py:14
  20.5 2.9 %collective-permute-done.3 = bf16[192,10,1]{0,1,2:T(8,128)(2,1)S(1)} collective-permute-done((bf16[192,10,1]{0,1,2:T(8,128)(2,1)S(1)}, bf16[192,10,1]{0,1,2:T(8,128)(2,1)S(1)}, u32[]{:S(2)}, u32[]{:S(2)}) %collective-permute-start.3) | collective-permute-done | bytes 3872 | tf_op jit(solution)/shard_map/ppermute | solution.py:14
  23.4 1.3 %select_select_fusion = bf16[192,10,258]{2,0,1:T(8,128)(2,1)S(1)} fusion(bf16[192,10,256]{2,0,1:T(8,128)(2,1)S(1)} %pad_maximum_fusion, pred[258]{0:T(512)(128)(4,1)S(1)} %get-tuple-element.42, pred[258]{0:T(512)(128)(4,1)S(1)} %get-tuple-element.43, bf16[192,10]{0,1:T(8,128)(2,1)S(1)} %bitcast.354, bf16[192,10]{0,1:T(8,128)(2,1)S(1)} %bitcast.353), kind=kLoop, calls=%fused_computation.33 | loop fusion | flops 990720 | bytes 1981956 | tf_op jit(solution)/shard_map/jit(_where)/select_n | solution.py:18
  24.7 1.8 %slice_bitcast_fusion = (bf16[8,12,8,256]{3,2,1,0:T(8,128)(2,1)S(1)}, bf16[8,12,8,256]{3,2,1,0:T(8,128)(2,1)S(1)}, bf16[8,12,8,256]{3,2,1,0:T(8,128)(2,1)S(1)}, ...) fusion(bf16[192,10,258]{2,0,1:T(8,128)(2,1)S(1)} %select_select, ...), kind=kLoop, calls=%fused_computation.76 | loop fusion | bytes 14155776
  27.2 0.8 copy-done.5
  30.1 0.7 copy-done.9
  34.5 3.2 %collective-permute-start.4 = (bf16[96,1,256]{2,0,1:T(8,128)(2,1)S(1)}, bf16[96,1,256]{2,0,1:T(8,128)(2,1)S(1)}, u32[]{:S(2)}, u32[]{:S(2)}) collective-permute-start(bf16[96,1,256]{2,0,1:T(8,128)(2,1)S(1)} %get-tuple-element.39), channel_id=1, source_target_pairs={{0,8},{8,16},{16,24},{24,32},{32,40},{40,48},{48,56},{56,64},{64,7... | collective-permute-start | bytes 147464 | tf_op jit(solution)/shard_map/ppermute | solution.py:13
  37.7 1.3 %collective-permute-start.5 = (bf16[96,1,256]{2,0,1:T(8,128)(2,1)S(1)}, bf16[96,1,256]{2,0,1:T(8,128)(2,1)S(1)}, u32[]{:S(2)}, u32[]{:S(2)}) collective-permute-start(bf16[96,1,256]{2,0,1:T(8,128)(2,1)S(1)} %get-tuple-element.38), channel_id=1, source_target_pairs={{8,0},{16,8},{24,16},{32,24},{40,32},{48,40},{56,48},{64,56},{72,6... | collective-permute-start | bytes 147464 | tf_op jit(solution)/shard_map/ppermute | solution.py:14
  41.5 1.1 %collective-permute-done.5 = bf16[96,1,256]{2,0,1:T(8,128)(2,1)S(1)} collective-permute-done((bf16[96,1,256]{2,0,1:T(8,128)(2,1)S(1)}, bf16[96,1,256]{2,0,1:T(8,128)(2,1)S(1)}, u32[]{:S(2)}, u32[]{:S(2)}) %collective-permute-start.5) | collective-permute-done | bytes 49184 | tf_op jit(solution)/shard_map/ppermute | solution.py:14
  42.7 3.6 %collective-permute-start.6 = (bf16[96,10,1]{2,0,1:T(8,128)(2,1)S(1)}, bf16[96,10,1]{2,0,1:T(8,128)(2,1)S(1)}, u32[]{:S(2)}, u32[]{:S(2)}) collective-permute-start(bf16[96,10,1]{2,0,1:T(8,128)(2,1)S(1)} %get-tuple-element.36), channel_id=1, source_target_pairs={{0,1},{1,2},{2,3},{3,4},{4,5},{5,6},{6,7},{8,9},{9,10},{10,11},{11... | collective-permute-start | bytes 5768 | tf_op jit(solution)/shard_map/ppermute | solution.py:13
  46.3 2.1 %collective-permute-start.7 = (bf16[96,10,1]{2,0,1:T(8,128)(2,1)S(1)}, bf16[96,10,1]{2,0,1:T(8,128)(2,1)S(1)}, u32[]{:S(2)}, u32[]{:S(2)}) collective-permute-start(bf16[96,10,1]{2,0,1:T(8,128)(2,1)S(1)} %get-tuple-element.37), channel_id=1, source_target_pairs={{1,0},{2,1},{3,2},{4,3},{5,4},{6,5},{7,6},{9,8},{10,9},{11,10},{12... | collective-permute-start | bytes 5768 | tf_op jit(solution)/shard_map/ppermute | solution.py:14
  48.9 0.8 copy.173
  50.0 3.8 %collective-permute-done.7 = bf16[96,10,1]{2,0,1:T(8,128)(2,1)S(1)} collective-permute-done((bf16[96,10,1]{2,0,1:T(8,128)(2,1)S(1)}, bf16[96,10,1]{2,0,1:T(8,128)(2,1)S(1)}, u32[]{:S(2)}, u32[]{:S(2)}) %collective-permute-start.7) | collective-permute-done | bytes 1952 | tf_op jit(solution)/shard_map/ppermute | solution.py:14
  54.1 0.6 select_select_fusion.1
  55.1 2.2 %slice_bitcast_fusion.18 = (bf16[8,12,8,256]{3,2,1,0:T(8,128)(2,1)S(1)}, bf16[8,12,8,256]{3,2,1,0:T(8,128)(2,1)S(1)}, bf16[8,12,8,256]{3,2,1,0:T(8,128)(2,1)S(1)...) fusion(bf16[96,10,258]{2,0,1:T(8,128)(2,1)S(1)} %select_select_, ...), kind=kLoop, calls=%fused_computation.96 | loop fusion | bytes 7077888
  60.4 2.0 %pad_maximum_fusion.1 = f32[2,32,8,324]{3,1,0,2:T(8,128)} fusion(f32[1,32,8,324]{3,1,0,2:T(8,128)} %copy.173, f32[1,32,8,324]{3,1,0,2:T(8,128)S(1)} %copy.172), kind=kLoop, calls=%fused_computation.71 | loop fusion | flops 165888 | bytes 1327104 | tf_op jit(solution)/shard_map/stack | solution.py:59
  62.3 3.9 %all-to-all-start = ((f32[2,32,8,324]{3,1,0,2:T(8,128)}), f32[2,32,8,324]{3,1,0,2:T(8,128)S(1)}, u32[]{:S(2)}, u32[]{:S(2)}) async-start(f32[2,32,8,324]{3,1,0,2:T(8,128)} %pad_maximum_fusion.1), calls=%async_computation | async-start | bytes 1572864 | tf_op jit(solution)/shard_map/all_to_all | solution.py:60
  66.3 1.1 %copy.196 = bf16[8,12,8,256]{3,2,0,1:T(8,128)(2,1)S(1)} copy(bf16[8,12,8,256]{3,2,1,0:T(8,128)(2,1)} %get-tuple-element.35) | data formatting | bytes 786432 | tf_op jit(solution)/shard_map/reshape | solution.py:33
  67.4 1.1 %fusion.52 = f32[2048,96]{0,1:T(8,128)S(1)} fusion(bf16[96,2048]{1,0:T(8,128)(2,1)S(1)} %bitcast.335, bf16[3,3,96,96]{3,2,1,0:T(8,128)(2,1)} %param.7), kind=kOutput, calls=%fused_computation.135 | convolution fusion | flops 37748736 | bytes 1204224 | tf_op jit(solution)/shard_map/dot_general | solution.py:43
  68.6 0.8 copy-done
  71.9 6.5 %all-to-all-done = f32[2,32,8,324]{3,1,0,2:T(8,128)S(1)} async-done(((f32[2,32,8,324]{3,1,0,2:T(8,128)}), f32[2,32,8,324]{3,1,0,2:T(8,128)S(1)}, u32[]{:S(2)}, u32[]{:S(2)}) %all-to-all-start) | async-done | bytes 663584 | tf_op jit(solution)/shard_map/all_to_all | solution.py:60
  78.5 0.7 copy.174
  79.2 14.7 %all-to-all-start.1 = ((f32[2,32,324]{2,0,1:T(2,128)}), f32[2,32,324]{2,0,1:T(2,128)S(1)}, u32[]{:S(2)}, u32[]{:S(2)}) async-start(f32[2,32,324]{2,0,1:T(2,128)} %copy.174), calls=%async_computation.1 | async-start | bytes 196608 | tf_op jit(solution)/shard_map/all_to_all | solution.py:61
  93.9 1.1 %fusion.7 = bf16[96,2048]{1,0:T(8,128)(2,1)S(1)} fusion(f32[96,2048]{1,0:T(8,128)S(1)} %bitcast.326, f32[2048,96]{0,1:T(8,128)S(1)} %convolution_add_fusion.9, bf16[96,2048]{1,0:T(8,128)(2,1)S(1)} %bitcast.331, bf16[3,3,96,96]{3,2,1,0:T(8,128)(2,1)} %param.7), kind=kOutput, calls=%fused_computation.31 | convolution fusion | flops 38338560 | bytes 2383872 | tf_op jit(solution)/shard_map/dot_general | solution.py:43
  95.0 0.8 copy.206
  95.8 7.2 %all-to-all-done.1 = f32[2,32,324]{2,0,1:T(2,128)S(1)} async-done(((f32[2,32,324]{2,0,1:T(2,128)}), f32[2,32,324]{2,0,1:T(2,128)S(1)}, u32[]{:S(2)}, u32[]{:S(2)}) %all-to-all-start.1) | async-done | bytes 82976 | tf_op jit(solution)/shard_map/all_to_all | solution.py:61
  (115 shorter events, 17.8 us)
Async XLA Ops:
  2.8 5.6 %collective-permute-start = (bf16[192,1,256]{2,0,1:T(8,128)(2,1)S(1)}, bf16[192,1,256]{2,0,1:T(8,128)(2,1)S(1)}, u32[]{:S(2)}, u32[]{:S(2)}) collective-permute-start(bf16[192,1,256]{2,0,1:T(8,128)(2,1)S(1)} %get-tuple-element.25), channel_id=1, source_target_pairs={{0,8},{8,16},{16,24},{24,32},{32,40},{40,48},{48,56},{56,64},{64,7... | collective-permute-start | bytes 294920 | tf_op jit(solution)/shard_map/ppermute | solution.py:13
  6.8 5.4 %collective-permute-start.1 = (bf16[192,1,256]{2,0,1:T(8,128)(2,1)S(1)}, bf16[192,1,256]{2,0,1:T(8,128)(2,1)S(1)}, u32[]{:S(2)}, u32[]{:S(2)}) collective-permute-start(bf16[192,1,256]{2,0,1:T(8,128)(2,1)S(1)} %get-tuple-element.26), channel_id=1, source_target_pairs={{8,0},{16,8},{24,16},{32,24},{40,32},{48,40},{56,48},{64,56},{72,6... | collective-permute-start | bytes 294920 | tf_op jit(solution)/shard_map/ppermute | solution.py:14
  12.3 8.1 %copy-start.4 = (bf16[96,8,256]{2,1,0:T(8,128)(2,1)S(1)}, bf16[96,8,256]{2,1,0:T(8,128)(2,1)}, u32[]{:S(2)}) copy-start(bf16[96,8,256]{2,1,0:T(8,128)(2,1)} %param.6) | copy-start | bytes 1179652
  13.0 7.5 %collective-permute-start.2 = (bf16[192,10,1]{0,1,2:T(8,128)(2,1)S(1)}, bf16[192,10,1]{0,1,2:T(8,128)(2,1)S(1)}, u32[]{:S(2)}, u32[]{:S(2)}) collective-permute-start(bf16[192,10,1]{0,1,2:T(8,128)(2,1)S(1)} %copy.175), channel_id=1, source_target_pairs={{0,1},{1,2},{2,3},{3,4},{4,5},{5,6},{6,7},{8,9},{9,10},{10,11},{11... | collective-permute-start | bytes 11528 | tf_op jit(solution)/shard_map/ppermute | solution.py:13
  18.5 5.0 %collective-permute-start.3 = (bf16[192,10,1]{0,1,2:T(8,128)(2,1)S(1)}, bf16[192,10,1]{0,1,2:T(8,128)(2,1)S(1)}, u32[]{:S(2)}, u32[]{:S(2)}) collective-permute-start(bf16[192,10,1]{0,1,2:T(8,128)(2,1)S(1)} %copy.176), channel_id=1, source_target_pairs={{1,0},{2,1},{3,2},{4,3},{5,4},{6,5},{7,6},{9,8},{10,9},{11,10},{12... | collective-permute-start | bytes 11528 | tf_op jit(solution)/shard_map/ppermute | solution.py:14
  27.0 0.9 copy-start.5
  29.8 0.9 copy-start.9
  33.0 0.7 copy-start.10
  34.5 6.9 %collective-permute-start.4 = (bf16[96,1,256]{2,0,1:T(8,128)(2,1)S(1)}, bf16[96,1,256]{2,0,1:T(8,128)(2,1)S(1)}, u32[]{:S(2)}, u32[]{:S(2)}) collective-permute-start(bf16[96,1,256]{2,0,1:T(8,128)(2,1)S(1)} %get-tuple-element.39), channel_id=1, source_target_pairs={{0,8},{8,16},{16,24},{24,32},{32,40},{40,48},{48,56},{56,64},{64,7... | collective-permute-start | bytes 147464 | tf_op jit(solution)/shard_map/ppermute | solution.py:13
  37.7 4.8 %collective-permute-start.5 = (bf16[96,1,256]{2,0,1:T(8,128)(2,1)S(1)}, bf16[96,1,256]{2,0,1:T(8,128)(2,1)S(1)}, u32[]{:S(2)}, u32[]{:S(2)}) collective-permute-start(bf16[96,1,256]{2,0,1:T(8,128)(2,1)S(1)} %get-tuple-element.38), channel_id=1, source_target_pairs={{8,0},{16,8},{24,16},{32,24},{40,32},{48,40},{56,48},{64,56},{72,6... | collective-permute-start | bytes 147464 | tf_op jit(solution)/shard_map/ppermute | solution.py:14
  42.7 7.0 %collective-permute-start.6 = (bf16[96,10,1]{2,0,1:T(8,128)(2,1)S(1)}, bf16[96,10,1]{2,0,1:T(8,128)(2,1)S(1)}, u32[]{:S(2)}, u32[]{:S(2)}) collective-permute-start(bf16[96,10,1]{2,0,1:T(8,128)(2,1)S(1)} %get-tuple-element.36), channel_id=1, source_target_pairs={{0,1},{1,2},{2,3},{3,4},{4,5},{5,6},{6,7},{8,9},{9,10},{10,11},{11... | collective-permute-start | bytes 5768 | tf_op jit(solution)/shard_map/ppermute | solution.py:13
  46.3 7.5 %collective-permute-start.7 = (bf16[96,10,1]{2,0,1:T(8,128)(2,1)S(1)}, bf16[96,10,1]{2,0,1:T(8,128)(2,1)S(1)}, u32[]{:S(2)}, u32[]{:S(2)}) collective-permute-start(bf16[96,10,1]{2,0,1:T(8,128)(2,1)S(1)} %get-tuple-element.37), channel_id=1, source_target_pairs={{1,0},{2,1},{3,2},{4,3},{5,4},{6,5},{7,6},{9,8},{10,9},{11,10},{12... | collective-permute-start | bytes 5768 | tf_op jit(solution)/shard_map/ppermute | solution.py:14
  48.5 6.3 %copy-start.7 = (bf16[96,8,256]{2,1,0:T(8,128)(2,1)S(1)}, bf16[96,8,256]{2,1,0:T(8,128)(2,1)}, u32[]{:S(2)}) copy-start(bf16[96,8,256]{2,1,0:T(8,128)(2,1)} %param.5) | copy-start | bytes 1179652
  55.1 2.2 %copy-start.8 = (bf16[96,8,256]{2,1,0:T(8,128)(2,1)S(1)}, bf16[96,8,256]{2,1,0:T(8,128)(2,1)}, u32[]{:S(2)}) copy-start(bf16[96,8,256]{2,1,0:T(8,128)(2,1)} %param.5) | copy-start | bytes 1179652
  62.3 16.1 %all-to-all-start = ((f32[2,32,8,324]{3,1,0,2:T(8,128)}), f32[2,32,8,324]{3,1,0,2:T(8,128)S(1)}, u32[]{:S(2)}, u32[]{:S(2)}) async-start(f32[2,32,8,324]{3,1,0,2:T(8,128)} %pad_maximum_fusion.1), calls=%async_computation | async-start | bytes 1572864 | tf_op jit(solution)/shard_map/all_to_all | solution.py:60
  66.3 2.2 %copy-start.3 = (bf16[8,12,8,256]{3,2,1,0:T(8,128)(2,1)S(1)}, bf16[8,12,8,256]{3,2,1,0:T(8,128)(2,1)}, u32[]{:S(2)}) copy-start(bf16[8,12,8,256]{3,2,1,0:T(8,128)(2,1)} %get-tuple-element.34) | copy-start | bytes 1179652
  66.3 2.3 %copy-start.2 = (bf16[8,12,8,256]{3,2,1,0:T(8,128)(2,1)S(1)}, bf16[8,12,8,256]{3,2,1,0:T(8,128)(2,1)}, u32[]{:S(2)}) copy-start(bf16[8,12,8,256]{3,2,1,0:T(8,128)(2,1)} %get-tuple-element.33) | copy-start | bytes 1179652
  67.4 1.2 %copy-start.1 = (bf16[8,12,8,256]{3,2,1,0:T(8,128)(2,1)S(1)}, bf16[8,12,8,256]{3,2,1,0:T(8,128)(2,1)}, u32[]{:S(2)}) copy-start(bf16[8,12,8,256]{3,2,1,0:T(8,128)(2,1)} %get-tuple-element.32) | copy-start | bytes 1179652
  68.5 1.0 copy-start
  68.5 1.0 copy-start.6
  79.2 23.8 %all-to-all-start.1 = ((f32[2,32,324]{2,0,1:T(2,128)}), f32[2,32,324]{2,0,1:T(2,128)S(1)}, u32[]{:S(2)}, u32[]{:S(2)}) async-start(f32[2,32,324]{2,0,1:T(2,128)} %copy.174), calls=%async_computation.1 | async-start | bytes 196608 | tf_op jit(solution)/shard_map/all_to_all | solution.py:61

commit v10 on v9

--- a/solution.py
+++ b/solution.py
@@ -80,7 +80,6 @@
     hidden = hidden + bias_one[:, None]
     act = jax.nn.silu(hidden).astype(jnp.bfloat16)
     act_grad, grad_two = backward_taps(padded_cot, weight_two, act, tile_rows, tile_cols)
-    grad_two = grad_two * scale
     sig = jax.nn.sigmoid(hidden)
     hidden_grad = (act_grad * sig * (1.0 + hidden * (1.0 - sig))).astype(jnp.bfloat16)
     padded_hid = padded_2(
@@ -89,12 +88,12 @@
     back_input, grad_one = backward_taps(
         padded_hid, weight_one, features.reshape(channels, cell_count), tile_rows, tile_cols
     )
-    grad_one = grad_one * scale
     input_grad = (cotangent.reshape(channels, cell_count).astype(jnp.float32) + back_input).astype(
         jnp.bfloat16
     )
     input_grad = input_grad.reshape(channels, tile_rows, tile_cols)
     summed_one, summed_two = reduce_weights((grad_one, grad_two))
+    summed_one, summed_two = summed_one * scale, summed_two * scale
     return (input_grad, summed_one, summed_two)
 
 

time: 104 us -> 110 us (1.058)
  matrix products: 14.8 us -> 20.4 us
    dot_general x18, matrix products: 5.17 us -> 10.7 us  [backward_taps(): lax.dot_general(patch, other, (((1,), (1,)), ((), ())), preferred_element...]
    another operation x0 -> x4, local copies, waits for them, and re-layouts: none -> 2.85 us  [reduce_weights(): stacked = jnp.stack(grads).reshape(len(grads), rows, cols, -1)]
    mul x4 -> x0, local copies, waits for them, and re-layouts: 1.76 us -> none  [the longest x2 1.25 us: local(): grad_two = grad_two * scale]
    unnamed x31 -> x33, local copies, waits for them, and re-layouts: 9.4 us -> 9.27 us
  transfers between devices with their start and end apart: 10 -> 10, of which waited for: 7 -> 7; matrix products, arithmetic and copies ran while one was open for 10% -> 9% of each run, Pallas kernels for 0% -> 0%
where the time goes in v10:
time: 110 us
  starting transfers between devices  41.2 us (37%)
  waiting for transfers between devices  26.7 us (24%)
  matrix products  20.4 us (19%)
  local copies, waits for them, and re-layouts  15.8 us (14%)
  other arithmetic  4.21 us (4%)
  between operations  1.45 us (1%)
    ppermute x4, starting transfers between devices, padded_2(): lax.ppermute(tail, axis, [(i, (i + 1) % count) for i in range(ends)])  15.9 us
    all_to_all x1, starting transfers between devices, reduce_weights(): summed = lax.all_to_all(stacked, 'row', 1, 1, tiled=True).sum(axis=1)  14.8 us
    ppermute x4, waiting for transfers between devices, padded_2(): lax.ppermute(head, axis, [((i + 1) % count, i) for i in range(ends)])  11.6 us
    dot_general x18, matrix products, backward_taps(): lax.dot_general(patch, other, (((1,), (1,)), ((), ())), preferred_element...  10.7 us
    unnamed x33, local copies, waits for them, and re-layouts  9.27 us
    all_to_all x1, waiting for transfers between devices, reduce_weights(): stacked = lax.all_to_all(stacked, 'col', 2, 2, tiled=True).sum(axis=2)  7.52 us
    dot_general x18, matrix products, backward_taps(): lax.dot_general(kernel[offset_y, offset_x], patch, (((0,), (0,)), ((), ()...  7.31 us
    all_to_all x1, waiting for transfers between devices, reduce_weights(): summed = lax.all_to_all(stacked, 'row', 1, 1, tiled=True).sum(axis=1)  7.2 us
  transfers between devices with their start and end apart: 10, of which 7 were waited for; matrix products, arithmetic and copies ran while one was open for 9% of the time, Pallas kernels for 0%

profile of v10, /device:TPU:1, one launch (start us, length us, event | category | flops | bytes accessed | tf_op | source)
XLA Modules:
  0.0 109.7 jit_solution(14618432083523874438)
XLA Ops:
  0.6 1.1 constant_dynamic-update-slice_fusion
  1.7 1.1 copy_dynamic-update-slice_fusion
  2.8 4.0 %collective-permute-start = (bf16[192,1,256]{2,0,1:T(8,128)(2,1)S(1)}, bf16[192,1,256]{2,0,1:T(8,128)(2,1)S(1)}, u32[]{:S(2)}, u32[]{:S(2)}) collective-permute-start(bf16[192,1,256]{2,0,1:T(8,128)(2,1)S(1)} %get-tuple-element.25), channel_id=1, source_target_pairs={{0,8},{8,16},{16,24},{24,32},{32,40},{40,48},{48,56},{56,64},{64,7... | collective-permute-start | bytes 294920 | tf_op jit(solution)/shard_map/ppermute | solution.py:13
  6.8 1.3 %collective-permute-start.1 = (bf16[192,1,256]{2,0,1:T(8,128)(2,1)S(1)}, bf16[192,1,256]{2,0,1:T(8,128)(2,1)S(1)}, u32[]{:S(2)}, u32[]{:S(2)}) collective-permute-start(bf16[192,1,256]{2,0,1:T(8,128)(2,1)S(1)} %get-tuple-element.26), channel_id=1, source_target_pairs={{8,0},{16,8},{24,16},{32,24},{40,32},{48,40},{56,48},{64,56},{72,6... | collective-permute-start | bytes 294920 | tf_op jit(solution)/shard_map/ppermute | solution.py:14
  8.5 3.7 %collective-permute-done.1 = bf16[192,1,256]{2,0,1:T(8,128)(2,1)S(1)} collective-permute-done((bf16[192,1,256]{2,0,1:T(8,128)(2,1)S(1)}, bf16[192,1,256]{2,0,1:T(8,128)(2,1)S(1)}, u32[]{:S(2)}, u32[]{:S(2)}) %collective-permute-start.1) | collective-permute-done | bytes 98336 | tf_op jit(solution)/shard_map/ppermute | solution.py:14
  13.0 5.1 %collective-permute-start.2 = (bf16[192,10,1]{0,1,2:T(8,128)(2,1)S(1)}, bf16[192,10,1]{0,1,2:T(8,128)(2,1)S(1)}, u32[]{:S(2)}, u32[]{:S(2)}) collective-permute-start(bf16[192,10,1]{0,1,2:T(8,128)(2,1)S(1)} %copy.175), channel_id=1, source_target_pairs={{0,1},{1,2},{2,3},{3,4},{4,5},{5,6},{6,7},{8,9},{9,10},{10,11},{11... | collective-permute-start | bytes 11528 | tf_op jit(solution)/shard_map/ppermute | solution.py:13
  18.5 1.9 %collective-permute-start.3 = (bf16[192,10,1]{0,1,2:T(8,128)(2,1)S(1)}, bf16[192,10,1]{0,1,2:T(8,128)(2,1)S(1)}, u32[]{:S(2)}, u32[]{:S(2)}) collective-permute-start(bf16[192,10,1]{0,1,2:T(8,128)(2,1)S(1)} %copy.176), channel_id=1, source_target_pairs={{1,0},{2,1},{3,2},{4,3},{5,4},{6,5},{7,6},{9,8},{10,9},{11,10},{12... | collective-permute-start | bytes 11528 | tf_op jit(solution)/shard_map/ppermute | solution.py:14
  20.5 2.9 %collective-permute-done.3 = bf16[192,10,1]{0,1,2:T(8,128)(2,1)S(1)} collective-permute-done((bf16[192,10,1]{0,1,2:T(8,128)(2,1)S(1)}, bf16[192,10,1]{0,1,2:T(8,128)(2,1)S(1)}, u32[]{:S(2)}, u32[]{:S(2)}) %collective-permute-start.3) | collective-permute-done | bytes 3872 | tf_op jit(solution)/shard_map/ppermute | solution.py:14
  23.4 1.3 %select_select_fusion = bf16[192,10,258]{2,0,1:T(8,128)(2,1)S(1)} fusion(bf16[192,10,256]{2,0,1:T(8,128)(2,1)S(1)} %pad_maximum_fusion, pred[258]{0:T(512)(128)(4,1)S(1)} %get-tuple-element.42, pred[258]{0:T(512)(128)(4,1)S(1)} %get-tuple-element.43, bf16[192,10]{0,1:T(8,128)(2,1)S(1)} %bitcast.354, bf16[192,10]{0,1:T(8,128)(2,1)S(1)} %bitcast.353), kind=kLoop, calls=%fused_computation.33 | loop fusion | flops 990720 | bytes 1981956 | tf_op jit(solution)/shard_map/jit(_where)/select_n | solution.py:18
  24.7 1.8 %slice_bitcast_fusion = (bf16[8,12,8,256]{3,2,1,0:T(8,128)(2,1)S(1)}, bf16[8,12,8,256]{3,2,1,0:T(8,128)(2,1)S(1)}, bf16[8,12,8,256]{3,2,1,0:T(8,128)(2,1)S(1)}, ...) fusion(bf16[192,10,258]{2,0,1:T(8,128)(2,1)S(1)} %select_select, ...), kind=kLoop, calls=%fused_computation.76 | loop fusion | bytes 14155776
  34.5 3.2 %collective-permute-start.4 = (bf16[96,1,256]{2,0,1:T(8,128)(2,1)S(1)}, bf16[96,1,256]{2,0,1:T(8,128)(2,1)S(1)}, u32[]{:S(2)}, u32[]{:S(2)}) collective-permute-start(bf16[96,1,256]{2,0,1:T(8,128)(2,1)S(1)} %get-tuple-element.39), channel_id=1, source_target_pairs={{0,8},{8,16},{16,24},{24,32},{32,40},{40,48},{48,56},{56,64},{64,7... | collective-permute-start | bytes 147464 | tf_op jit(solution)/shard_map/ppermute | solution.py:13
  37.7 1.3 %collective-permute-start.5 = (bf16[96,1,256]{2,0,1:T(8,128)(2,1)S(1)}, bf16[96,1,256]{2,0,1:T(8,128)(2,1)S(1)}, u32[]{:S(2)}, u32[]{:S(2)}) collective-permute-start(bf16[96,1,256]{2,0,1:T(8,128)(2,1)S(1)} %get-tuple-element.38), channel_id=1, source_target_pairs={{8,0},{16,8},{24,16},{32,24},{40,32},{48,40},{56,48},{64,56},{72,6... | collective-permute-start | bytes 147464 | tf_op jit(solution)/shard_map/ppermute | solution.py:14
  41.2 1.4 %collective-permute-done.5 = bf16[96,1,256]{2,0,1:T(8,128)(2,1)S(1)} collective-permute-done((bf16[96,1,256]{2,0,1:T(8,128)(2,1)S(1)}, bf16[96,1,256]{2,0,1:T(8,128)(2,1)S(1)}, u32[]{:S(2)}, u32[]{:S(2)}) %collective-permute-start.5) | collective-permute-done | bytes 49184 | tf_op jit(solution)/shard_map/ppermute | solution.py:14
  43.4 3.6 %collective-permute-start.6 = (bf16[96,10,1]{2,0,1:T(8,128)(2,1)}, bf16[96,10,1]{2,0,1:T(8,128)(2,1)S(1)}, u32[]{:S(2)}, u32[]{:S(2)}) collective-permute-start(bf16[96,10,1]{2,0,1:T(8,128)(2,1)} %get-tuple-element.36), channel_id=1, source_target_pairs={{0,1},{1,2},{2,3},{3,4},{4,5},{5,6},{6,7},{8,9},{9,10},{10,11},{11... | collective-permute-start | bytes 5768 | tf_op jit(solution)/shard_map/ppermute | solution.py:13
  47.0 2.1 %collective-permute-start.7 = (bf16[96,10,1]{2,0,1:T(8,128)(2,1)S(1)}, bf16[96,10,1]{2,0,1:T(8,128)(2,1)S(1)}, u32[]{:S(2)}, u32[]{:S(2)}) collective-permute-start(bf16[96,10,1]{2,0,1:T(8,128)(2,1)S(1)} %get-tuple-element.37), channel_id=1, source_target_pairs={{1,0},{2,1},{3,2},{4,3},{5,4},{6,5},{7,6},{9,8},{10,9},{11,10},{12... | collective-permute-start | bytes 5768 | tf_op jit(solution)/shard_map/ppermute | solution.py:14
  50.9 3.6 %collective-permute-done.7 = bf16[96,10,1]{2,0,1:T(8,128)(2,1)S(1)} collective-permute-done((bf16[96,10,1]{2,0,1:T(8,128)(2,1)S(1)}, bf16[96,10,1]{2,0,1:T(8,128)(2,1)S(1)}, u32[]{:S(2)}, u32[]{:S(2)}) %collective-permute-start.7) | collective-permute-done | bytes 1952 | tf_op jit(solution)/shard_map/ppermute | solution.py:14
  55.4 1.0 fusion.26
  56.4 2.0 %slice_bitcast_fusion.18 = (bf16[8,12,8,256]{3,2,1,0:T(8,128)(2,1)S(1)}, bf16[8,12,8,256]{3,2,1,0:T(8,128)(2,1)S(1)}, bf16[8,12,8,256]{3,2,1,0:T(8,128)(2,1)S(1)...) fusion(bf16[96,10,258]{2,0,1:T(8,128)(2,1)S(1)} %select_select_, ...), kind=kLoop, calls=%fused_computation.96 | loop fusion | bytes 7077888
  58.4 0.9 fusion.25
  60.2 1.0 fusion.23
  61.2 1.0 fusion.22
  63.0 1.0 fusion.20
  64.0 1.0 fusion.19
  64.9 0.9 fusion.18
  65.8 1.5 %stack.77 = f32[1,32,8,324]{3,2,1,0:T(8,128)S(1)} reshape(f32[9,96,96]{2,1,0:T(8,128)} %fusion.18) | data formatting | bytes 663552 | tf_op jit(solution)/shard_map/stack | solution.py:59
  67.4 1.0 pad_maximum_fusion.1
  68.4 3.9 %all-to-all-start = ((f32[2,32,8,324]{3,1,0,2:T(8,128)}), f32[2,32,8,324]{3,1,0,2:T(8,128)S(1)}, u32[]{:S(2)}, u32[]{:S(2)}) async-start(f32[2,32,8,324]{3,1,0,2:T(8,128)} %pad_maximum_fusion.1), calls=%async_computation | async-start | bytes 1572864 | tf_op jit(solution)/shard_map/all_to_all | solution.py:60
  72.4 1.1 %fusion.52 = f32[2048,96]{0,1:T(8,128)S(1)} fusion(bf16[96,2048]{1,0:T(8,128)(2,1)S(1)} %bitcast.335, bf16[3,3,96,96]{3,2,1,0:T(8,128)(2,1)} %param.7), kind=kOutput, calls=%fused_computation.133 | convolution fusion | flops 37748736 | bytes 1204224 | tf_op jit(solution)/shard_map/dot_general | solution.py:43
  76.9 7.5 %all-to-all-done = f32[2,32,8,324]{3,1,0,2:T(8,128)S(1)} async-done(((f32[2,32,8,324]{3,1,0,2:T(8,128)}), f32[2,32,8,324]{3,1,0,2:T(8,128)S(1)}, u32[]{:S(2)}, u32[]{:S(2)}) %all-to-all-start) | async-done | bytes 663584 | tf_op jit(solution)/shard_map/all_to_all | solution.py:60
  85.2 14.8 %all-to-all-start.1 = ((f32[2,32,324]{2,0,1:T(2,128)}), f32[2,32,324]{2,0,1:T(2,128)S(1)}, u32[]{:S(2)}, u32[]{:S(2)}) async-start(f32[2,32,324]{2,0,1:T(2,128)} %copy.174), calls=%async_computation.1 | async-start | bytes 196608 | tf_op jit(solution)/shard_map/all_to_all | solution.py:61
  100.0 1.1 fusion.7
  101.9 7.2 %all-to-all-done.1 = f32[2,32,324]{2,0,1:T(2,128)S(1)} async-done(((f32[2,32,324]{2,0,1:T(2,128)}), f32[2,32,324]{2,0,1:T(2,128)S(1)}, u32[]{:S(2)}, u32[]{:S(2)}) %all-to-all-start.1) | async-done | bytes 82976 | tf_op jit(solution)/shard_map/all_to_all | solution.py:61
  (115 shorter events, 22.2 us)
Async XLA Ops:
  2.8 5.6 %collective-permute-start = (bf16[192,1,256]{2,0,1:T(8,128)(2,1)S(1)}, bf16[192,1,256]{2,0,1:T(8,128)(2,1)S(1)}, u32[]{:S(2)}, u32[]{:S(2)}) collective-permute-start(bf16[192,1,256]{2,0,1:T(8,128)(2,1)S(1)} %get-tuple-element.25), channel_id=1, source_target_pairs={{0,8},{8,16},{16,24},{24,32},{32,40},{40,48},{48,56},{56,64},{64,7... | collective-permute-start | bytes 294920 | tf_op jit(solution)/shard_map/ppermute | solution.py:13
  6.8 5.4 %collective-permute-start.1 = (bf16[192,1,256]{2,0,1:T(8,128)(2,1)S(1)}, bf16[192,1,256]{2,0,1:T(8,128)(2,1)S(1)}, u32[]{:S(2)}, u32[]{:S(2)}) collective-permute-start(bf16[192,1,256]{2,0,1:T(8,128)(2,1)S(1)} %get-tuple-element.26), channel_id=1, source_target_pairs={{8,0},{16,8},{24,16},{32,24},{40,32},{48,40},{56,48},{64,56},{72,6... | collective-permute-start | bytes 294920 | tf_op jit(solution)/shard_map/ppermute | solution.py:14
  12.3 8.1 %copy-start.4 = (bf16[96,8,256]{2,1,0:T(8,128)(2,1)S(1)}, bf16[96,8,256]{2,1,0:T(8,128)(2,1)}, u32[]{:S(2)}) copy-start(bf16[96,8,256]{2,1,0:T(8,128)(2,1)} %param.6) | copy-start | bytes 1179652
  13.0 7.5 %collective-permute-start.2 = (bf16[192,10,1]{0,1,2:T(8,128)(2,1)S(1)}, bf16[192,10,1]{0,1,2:T(8,128)(2,1)S(1)}, u32[]{:S(2)}, u32[]{:S(2)}) collective-permute-start(bf16[192,10,1]{0,1,2:T(8,128)(2,1)S(1)} %copy.175), channel_id=1, source_target_pairs={{0,1},{1,2},{2,3},{3,4},{4,5},{5,6},{6,7},{8,9},{9,10},{10,11},{11... | collective-permute-start | bytes 11528 | tf_op jit(solution)/shard_map/ppermute | solution.py:13
  18.5 5.0 %collective-permute-start.3 = (bf16[192,10,1]{0,1,2:T(8,128)(2,1)S(1)}, bf16[192,10,1]{0,1,2:T(8,128)(2,1)S(1)}, u32[]{:S(2)}, u32[]{:S(2)}) collective-permute-start(bf16[192,10,1]{0,1,2:T(8,128)(2,1)S(1)} %copy.176), channel_id=1, source_target_pairs={{1,0},{2,1},{3,2},{4,3},{5,4},{6,5},{7,6},{9,8},{10,9},{11,10},{12... | collective-permute-start | bytes 11528 | tf_op jit(solution)/shard_map/ppermute | solution.py:14
  27.0 0.9 copy-start.6
  29.8 0.9 copy-start.10
  33.0 0.7 copy-start.11
  34.5 6.6 %collective-permute-start.4 = (bf16[96,1,256]{2,0,1:T(8,128)(2,1)S(1)}, bf16[96,1,256]{2,0,1:T(8,128)(2,1)S(1)}, u32[]{:S(2)}, u32[]{:S(2)}) collective-permute-start(bf16[96,1,256]{2,0,1:T(8,128)(2,1)S(1)} %get-tuple-element.39), channel_id=1, source_target_pairs={{0,8},{8,16},{16,24},{24,32},{32,40},{40,48},{48,56},{56,64},{64,7... | collective-permute-start | bytes 147464 | tf_op jit(solution)/shard_map/ppermute | solution.py:13
  37.7 4.8 %collective-permute-start.5 = (bf16[96,1,256]{2,0,1:T(8,128)(2,1)S(1)}, bf16[96,1,256]{2,0,1:T(8,128)(2,1)S(1)}, u32[]{:S(2)}, u32[]{:S(2)}) collective-permute-start(bf16[96,1,256]{2,0,1:T(8,128)(2,1)S(1)} %get-tuple-element.38), channel_id=1, source_target_pairs={{8,0},{16,8},{24,16},{32,24},{40,32},{48,40},{56,48},{64,56},{72,6... | collective-permute-start | bytes 147464 | tf_op jit(solution)/shard_map/ppermute | solution.py:14
  43.4 7.2 %collective-permute-start.6 = (bf16[96,10,1]{2,0,1:T(8,128)(2,1)}, bf16[96,10,1]{2,0,1:T(8,128)(2,1)S(1)}, u32[]{:S(2)}, u32[]{:S(2)}) collective-permute-start(bf16[96,10,1]{2,0,1:T(8,128)(2,1)} %get-tuple-element.36), channel_id=1, source_target_pairs={{0,1},{1,2},{2,3},{3,4},{4,5},{5,6},{6,7},{8,9},{9,10},{10,11},{11... | collective-permute-start | bytes 5768 | tf_op jit(solution)/shard_map/ppermute | solution.py:13
  47.0 7.5 %collective-permute-start.7 = (bf16[96,10,1]{2,0,1:T(8,128)(2,1)S(1)}, bf16[96,10,1]{2,0,1:T(8,128)(2,1)S(1)}, u32[]{:S(2)}, u32[]{:S(2)}) collective-permute-start(bf16[96,10,1]{2,0,1:T(8,128)(2,1)S(1)} %get-tuple-element.37), channel_id=1, source_target_pairs={{1,0},{2,1},{3,2},{4,3},{5,4},{6,5},{7,6},{9,8},{10,9},{11,10},{12... | collective-permute-start | bytes 5768 | tf_op jit(solution)/shard_map/ppermute | solution.py:14
  49.4 6.0 %copy-start.8 = (bf16[96,8,256]{2,1,0:T(8,128)(2,1)S(1)}, bf16[96,8,256]{2,1,0:T(8,128)(2,1)}, u32[]{:S(2)}) copy-start(bf16[96,8,256]{2,1,0:T(8,128)(2,1)} %param.5) | copy-start | bytes 1179652
  56.4 2.0 %copy-start.9 = (bf16[96,8,256]{2,1,0:T(8,128)(2,1)S(1)}, bf16[96,8,256]{2,1,0:T(8,128)(2,1)}, u32[]{:S(2)}) copy-start(bf16[96,8,256]{2,1,0:T(8,128)(2,1)} %param.5) | copy-start | bytes 1179652
  65.8 1.6 %copy-start.5 = (f32[1,32,8,324]{3,1,0,2:T(8,128)S(1)}, f32[1,32,8,324]{3,1,0,2:T(8,128)}, u32[]{:S(2)}) copy-start(f32[1,32,8,324]{3,1,0,2:T(8,128)} %copy.173) | copy-start | bytes 995332
  68.4 16.1 %all-to-all-start = ((f32[2,32,8,324]{3,1,0,2:T(8,128)}), f32[2,32,8,324]{3,1,0,2:T(8,128)S(1)}, u32[]{:S(2)}, u32[]{:S(2)}) async-start(f32[2,32,8,324]{3,1,0,2:T(8,128)} %pad_maximum_fusion.1), calls=%async_computation | async-start | bytes 1572864 | tf_op jit(solution)/shard_map/all_to_all | solution.py:60
  72.3 1.2 %copy-start.3 = (bf16[8,12,8,256]{3,2,1,0:T(8,128)(2,1)S(1)}, bf16[8,12,8,256]{3,2,1,0:T(8,128)(2,1)}, u32[]{:S(2)}) copy-start(bf16[8,12,8,256]{3,2,1,0:T(8,128)(2,1)} %get-tuple-element.34) | copy-start | bytes 1179652
  72.3 1.2 %copy-start.2 = (bf16[8,12,8,256]{3,2,1,0:T(8,128)(2,1)S(1)}, bf16[8,12,8,256]{3,2,1,0:T(8,128)(2,1)}, u32[]{:S(2)}) copy-start(bf16[8,12,8,256]{3,2,1,0:T(8,128)(2,1)} %get-tuple-element.33) | copy-start | bytes 1179652
  72.3 1.3 %copy-start.1 = (bf16[8,12,8,256]{3,2,1,0:T(8,128)(2,1)S(1)}, bf16[8,12,8,256]{3,2,1,0:T(8,128)(2,1)}, u32[]{:S(2)}) copy-start(bf16[8,12,8,256]{3,2,1,0:T(8,128)(2,1)} %get-tuple-element.32) | copy-start | bytes 1179652
  73.5 1.0 copy-start
  73.6 1.0 copy-start.7
  85.2 23.8 %all-to-all-start.1 = ((f32[2,32,324]{2,0,1:T(2,128)}), f32[2,32,324]{2,0,1:T(2,128)S(1)}, u32[]{:S(2)}, u32[]{:S(2)}) async-start(f32[2,32,324]{2,0,1:T(2,128)} %copy.174), calls=%async_computation.1 | async-start | bytes 196608 | tf_op jit(solution)/shard_map/all_to_all | solution.py:61

commit v11 on v9

--- a/solution.py
+++ b/solution.py
@@ -12,9 +12,11 @@
         tail = lax.slice_in_dim(cells, cells.shape[dim] - width, cells.shape[dim], axis=dim)
         before = lax.ppermute(tail, axis, [(i, (i + 1) % count) for i in range(ends)])
         after = lax.ppermute(head, axis, [((i + 1) % count, i) for i in range(ends)])
-        if dim == cells.ndim - 1 and width == 1:
-            spread = [(0, 0)] * dim + [(1, 1)]
-            lane = lax.broadcasted_iota(jnp.int32, (cells.shape[dim] + 2,), 0)
+        if width == 1:
+            spread = [(0, 0)] * dim + [(1, 1)] + [(0, 0)] * (cells.ndim - 1 - dim)
+            shape = [1] * cells.ndim
+            shape[dim] = cells.shape[dim] + 2
+            lane = lax.broadcasted_iota(jnp.int32, tuple(shape), dim)
             cells = jnp.where(
                 lane == 0,
                 before,

time: 104 us -> 109 us (1.048)
  waiting for transfers between devices: 25.6 us -> 30.4 us
    ppermute x4, waiting for transfers between devices: 0.32 us -> 4.03 us  [padded_2(): lax.ppermute(tail, axis, [(i, (i + 1) % count) for i in range(ends)])]
    ppermute x4, waiting for transfers between devices: 11.6 us -> 12.7 us  [padded_2(): lax.ppermute(head, axis, [((i + 1) % count, i) for i in range(ends)])]
    unnamed x31 -> x27, local copies, waits for them, and re-layouts: 9.4 us -> 8.61 us
    select_n x2 -> x4, other arithmetic: 1.91 us -> 2.22 us  [padded_2(): jnp.where(lane == 0, before, jnp.where(lane == cells.shape[dim] + 1, afte...]
  transfers between devices with their start and end apart: 10 -> 10, of which waited for: 7 -> 8; matrix products, arithmetic and copies ran while one was open for 10% -> 10% of each run, Pallas kernels for 0% -> 0%
where the time goes in v11:
time: 109 us
  starting transfers between devices  41 us (38%)
  waiting for transfers between devices  30.4 us (28%)
  local copies, waits for them, and re-layouts  15 us (14%)
  matrix products  14.8 us (14%)
  other arithmetic  5.69 us (5%)
  between operations  1.53 us (1%)
    ppermute x4, starting transfers between devices, padded_2(): lax.ppermute(tail, axis, [(i, (i + 1) % count) for i in range(ends)])  15.5 us
    all_to_all x1, starting transfers between devices, reduce_weights(): summed = lax.all_to_all(stacked, 'row', 1, 1, tiled=True).sum(axis=1)  14.8 us
    ppermute x4, waiting for transfers between devices, padded_2(): lax.ppermute(head, axis, [((i + 1) % count, i) for i in range(ends)])  12.7 us
    unnamed x27, local copies, waits for them, and re-layouts  8.61 us
    dot_general x18, matrix products, backward_taps(): lax.dot_general(kernel[offset_y, offset_x], patch, (((0,), (0,)), ((), ()...  7.27 us
    all_to_all x1, waiting for transfers between devices, reduce_weights(): summed = lax.all_to_all(stacked, 'row', 1, 1, tiled=True).sum(axis=1)  7.2 us
    ppermute x4, starting transfers between devices, padded_2(): lax.ppermute(head, axis, [((i + 1) % count, i) for i in range(ends)])  6.61 us
    all_to_all x1, waiting for transfers between devices, reduce_weights(): stacked = lax.all_to_all(stacked, 'col', 2, 2, tiled=True).sum(axis=2)  6.51 us
  transfers between devices with their start and end apart: 10, of which 8 were waited for; matrix products, arithmetic and copies ran while one was open for 10% of the time, Pallas kernels for 0%

profile of v11, /device:TPU:1, one launch (start us, length us, event | category | flops | bytes accessed | tf_op | source)
XLA Modules:
  0.0 108.5 jit_solution(13108884890033694072)
XLA Ops:
  0.6 1.1 constant_dynamic-update-slice_fusion
  1.7 1.1 copy_dynamic-update-slice_fusion
  2.8 4.0 %collective-permute-start = (bf16[192,1,256]{2,0,1:T(8,128)(2,1)S(1)}, bf16[192,1,256]{2,0,1:T(8,128)(2,1)S(1)}, u32[]{:S(2)}, u32[]{:S(2)}) collective-permute-start(bf16[192,1,256]{2,0,1:T(8,128)(2,1)S(1)} %get-tuple-element.25), channel_id=1, source_target_pairs={{0,8},{8,16},{16,24},{24,32},{32,40},{40,48},{48,56},{56,64},{64,7... | collective-permute-start | bytes 294920 | tf_op jit(solution)/shard_map/ppermute | solution.py:13
  6.8 1.3 %collective-permute-start.1 = (bf16[192,1,256]{2,0,1:T(8,128)(2,1)S(1)}, bf16[192,1,256]{2,0,1:T(8,128)(2,1)S(1)}, u32[]{:S(2)}, u32[]{:S(2)}) collective-permute-start(bf16[192,1,256]{2,0,1:T(8,128)(2,1)S(1)} %get-tuple-element.26), channel_id=1, source_target_pairs={{8,0},{16,8},{24,16},{32,24},{40,32},{48,40},{56,48},{64,56},{72,6... | collective-permute-start | bytes 294920 | tf_op jit(solution)/shard_map/ppermute | solution.py:14
  8.5 3.7 %collective-permute-done.1 = bf16[192,1,256]{2,0,1:T(8,128)(2,1)S(1)} collective-permute-done((bf16[192,1,256]{2,0,1:T(8,128)(2,1)S(1)}, bf16[192,1,256]{2,0,1:T(8,128)(2,1)S(1)}, u32[]{:S(2)}, u32[]{:S(2)}) %collective-permute-start.1) | collective-permute-done | bytes 98336 | tf_op jit(solution)/shard_map/ppermute | solution.py:14
  12.6 5.1 %collective-permute-start.2 = (bf16[192,10,1]{2,0,1:T(8,128)(2,1)S(1)}, bf16[192,10,1]{2,0,1:T(8,128)(2,1)S(1)}, u32[]{:S(2)}, u32[]{:S(2)}) collective-permute-start(bf16[192,10,1]{2,0,1:T(8,128)(2,1)S(1)} %get-tuple-element.23), channel_id=1, source_target_pairs={{0,1},{1,2},{2,3},{3,4},{4,5},{5,6},{6,7},{8,9},{9,10},{10,11},{11... | collective-permute-start | bytes 11528 | tf_op jit(solution)/shard_map/ppermute | solution.py:13
  17.8 1.9 %collective-permute-start.3 = (bf16[192,10,1]{2,0,1:T(8,128)(2,1)S(1)}, bf16[192,10,1]{2,0,1:T(8,128)(2,1)S(1)}, u32[]{:S(2)}, u32[]{:S(2)}) collective-permute-start(bf16[192,10,1]{2,0,1:T(8,128)(2,1)S(1)} %get-tuple-element.24), channel_id=1, source_target_pairs={{1,0},{2,1},{3,2},{4,3},{5,4},{6,5},{7,6},{9,8},{10,9},{11,10},{12... | collective-permute-start | bytes 11528 | tf_op jit(solution)/shard_map/ppermute | solution.py:14
  19.8 3.7 %collective-permute-done.2 = bf16[192,10,1]{2,0,1:T(8,128)(2,1)S(1)} collective-permute-done((bf16[192,10,1]{2,0,1:T(8,128)(2,1)S(1)}, bf16[192,10,1]{2,0,1:T(8,128)(2,1)S(1)}, u32[]{:S(2)}, u32[]{:S(2)}) %collective-permute-start.2) | collective-permute-done | bytes 3872 | tf_op jit(solution)/shard_map/ppermute | solution.py:13
  23.9 4.0 %collective-permute-done.3 = bf16[192,10,1]{2,0,1:T(8,128)(2,1)S(1)} collective-permute-done((bf16[192,10,1]{2,0,1:T(8,128)(2,1)S(1)}, bf16[192,10,1]{2,0,1:T(8,128)(2,1)S(1)}, u32[]{:S(2)}, u32[]{:S(2)}) %collective-permute-start.3) | collective-permute-done | bytes 3872 | tf_op jit(solution)/shard_map/ppermute | solution.py:14
  28.3 1.3 %select_select_fusion = bf16[192,10,258]{2,0,1:T(8,128)(2,1)S(1)} fusion(bf16[192,10,256]{2,0,1:T(8,128)(2,1)S(1)} %select_select_fusion.1, pred[258]{0:T(512)(128)(4,1)S(1)} %get-tuple-element.44, pred[258]{0:T(512)(128)(4,1)S(1)} %get-tuple-element.45, bf16[192,10]{0,1:T(8,128)(2,1)S(1)} %reduce.1, bf16[192,10]{0,1:T(8,128)(2,1)S(1)} %reduce), kind=kLoop, calls=%fused_computation.33 | loop fusion | flops 990720 | bytes 1981956 | tf_op jit(solution)/shard_map/jit(_where)/select_n | solution.py:20
  29.6 1.8 %slice_bitcast_fusion = (bf16[8,12,8,256]{3,2,1,0:T(8,128)(2,1)S(1)}, bf16[8,12,8,256]{3,2,1,0:T(8,128)(2,1)S(1)}, bf16[8,12,8,256]{3,2,1,0:T(8,128)(2,1)S(1)}, ...) fusion(bf16[192,10,258]{2,0,1:T(8,128)(2,1)S(1)} %select_select, ...), kind=kLoop, calls=%fused_computation.77 | loop fusion | bytes 14155776
  32.1 0.8 copy-done.5
  35.0 0.7 copy-done.9
  39.4 3.2 %collective-permute-start.4 = (bf16[96,1,256]{2,0,1:T(8,128)(2,1)S(1)}, bf16[96,1,256]{2,0,1:T(8,128)(2,1)S(1)}, u32[]{:S(2)}, u32[]{:S(2)}) collective-permute-start(bf16[96,1,256]{2,0,1:T(8,128)(2,1)S(1)} %get-tuple-element.38), channel_id=1, source_target_pairs={{0,8},{8,16},{16,24},{24,32},{32,40},{40,48},{48,56},{56,64},{64,7... | collective-permute-start | bytes 147464 | tf_op jit(solution)/shard_map/ppermute | solution.py:13
  42.7 1.3 %collective-permute-start.5 = (bf16[96,1,256]{2,0,1:T(8,128)(2,1)S(1)}, bf16[96,1,256]{2,0,1:T(8,128)(2,1)S(1)}, u32[]{:S(2)}, u32[]{:S(2)}) collective-permute-start(bf16[96,1,256]{2,0,1:T(8,128)(2,1)S(1)} %get-tuple-element.39), channel_id=1, source_target_pairs={{8,0},{16,8},{24,16},{32,24},{40,32},{48,40},{56,48},{64,56},{72,6... | collective-permute-start | bytes 147464 | tf_op jit(solution)/shard_map/ppermute | solution.py:14
  46.4 1.1 %collective-permute-done.5 = bf16[96,1,256]{2,0,1:T(8,128)(2,1)S(1)} collective-permute-done((bf16[96,1,256]{2,0,1:T(8,128)(2,1)S(1)}, bf16[96,1,256]{2,0,1:T(8,128)(2,1)S(1)}, u32[]{:S(2)}, u32[]{:S(2)}) %collective-permute-start.5) | collective-permute-done | bytes 49184 | tf_op jit(solution)/shard_map/ppermute | solution.py:14
  47.8 3.2 %collective-permute-start.6 = (bf16[96,10,1]{2,0,1:T(8,128)(2,1)S(1)}, bf16[96,10,1]{2,0,1:T(8,128)(2,1)S(1)}, u32[]{:S(2)}, u32[]{:S(2)}) collective-permute-start(bf16[96,10,1]{2,0,1:T(8,128)(2,1)S(1)} %get-tuple-element.36), channel_id=1, source_target_pairs={{0,1},{1,2},{2,3},{3,4},{4,5},{5,6},{6,7},{8,9},{9,10},{10,11},{11... | collective-permute-start | bytes 5768 | tf_op jit(solution)/shard_map/ppermute | solution.py:13
  51.0 2.1 %collective-permute-start.7 = (bf16[96,10,1]{2,0,1:T(8,128)(2,1)S(1)}, bf16[96,10,1]{2,0,1:T(8,128)(2,1)S(1)}, u32[]{:S(2)}, u32[]{:S(2)}) collective-permute-start(bf16[96,10,1]{2,0,1:T(8,128)(2,1)S(1)} %get-tuple-element.37), channel_id=1, source_target_pairs={{1,0},{2,1},{3,2},{4,3},{5,4},{6,5},{7,6},{9,8},{10,9},{11,10},{12... | collective-permute-start | bytes 5768 | tf_op jit(solution)/shard_map/ppermute | solution.py:14
  53.6 0.8 copy.167
  54.7 3.8 %collective-permute-done.7 = bf16[96,10,1]{2,0,1:T(8,128)(2,1)S(1)} collective-permute-done((bf16[96,10,1]{2,0,1:T(8,128)(2,1)S(1)}, bf16[96,10,1]{2,0,1:T(8,128)(2,1)S(1)}, u32[]{:S(2)}, u32[]{:S(2)}) %collective-permute-start.7) | collective-permute-done | bytes 1952 | tf_op jit(solution)/shard_map/ppermute | solution.py:14
  59.8 2.2 %slice_bitcast_fusion.18 = (bf16[8,12,8,256]{3,2,1,0:T(8,128)(2,1)S(1)}, bf16[8,12,8,256]{3,2,1,0:T(8,128)(2,1)S(1)}, bf16[8,12,8,256]{3,2,1,0:T(8,128)(2,1)S(1)...) fusion(bf16[96,10,258]{2,0,1:T(8,128)(2,1)S(1)} %select_select_, ...), kind=kLoop, calls=%fused_computation.97 | loop fusion | bytes 7077888
  65.0 2.0 %pad_maximum_fusion = f32[2,32,8,324]{3,1,0,2:T(8,128)} fusion(f32[1,32,8,324]{3,1,0,2:T(8,128)} %copy.167, f32[1,32,8,324]{3,1,0,2:T(8,128)S(1)} %copy.166), kind=kLoop, calls=%fused_computation.71 | loop fusion | flops 165888 | bytes 1327104 | tf_op jit(solution)/shard_map/stack | solution.py:61
  67.0 4.1 %all-to-all-start = ((f32[2,32,8,324]{3,1,0,2:T(8,128)}), f32[2,32,8,324]{3,1,0,2:T(8,128)S(1)}, u32[]{:S(2)}, u32[]{:S(2)}) async-start(f32[2,32,8,324]{3,1,0,2:T(8,128)} %pad_maximum_fusion), calls=%async_computation | async-start | bytes 1572864 | tf_op jit(solution)/shard_map/all_to_all | solution.py:62
  71.1 1.1 %copy.188 = bf16[8,12,8,256]{3,2,0,1:T(8,128)(2,1)S(1)} copy(bf16[8,12,8,256]{3,2,1,0:T(8,128)(2,1)} %get-tuple-element.35) | data formatting | bytes 786432 | tf_op jit(solution)/shard_map/reshape | solution.py:35
  72.2 1.1 %fusion.52 = f32[2048,96]{0,1:T(8,128)S(1)} fusion(bf16[96,2048]{1,0:T(8,128)(2,1)S(1)} %bitcast.335, bf16[3,3,96,96]{3,2,1,0:T(8,128)(2,1)} %param.7), kind=kOutput, calls=%fused_computation.133 | convolution fusion | flops 37748736 | bytes 1204224 | tf_op jit(solution)/shard_map/dot_general | solution.py:45
  73.5 0.8 copy-done
  76.7 6.5 %all-to-all-done = f32[2,32,8,324]{3,1,0,2:T(8,128)S(1)} async-done(((f32[2,32,8,324]{3,1,0,2:T(8,128)}), f32[2,32,8,324]{3,1,0,2:T(8,128)S(1)}, u32[]{:S(2)}, u32[]{:S(2)}) %all-to-all-start) | async-done | bytes 663584 | tf_op jit(solution)/shard_map/all_to_all | solution.py:62
  83.3 0.7 copy.168
  84.0 14.8 %all-to-all-start.1 = ((f32[2,32,324]{2,0,1:T(2,128)}), f32[2,32,324]{2,0,1:T(2,128)S(1)}, u32[]{:S(2)}, u32[]{:S(2)}) async-start(f32[2,32,324]{2,0,1:T(2,128)} %copy.168), calls=%async_computation.1 | async-start | bytes 196608 | tf_op jit(solution)/shard_map/all_to_all | solution.py:63
  98.8 1.1 fusion.7
  99.8 0.8 copy.198
  100.6 7.2 %all-to-all-done.1 = f32[2,32,324]{2,0,1:T(2,128)S(1)} async-done(((f32[2,32,324]{2,0,1:T(2,128)}), f32[2,32,324]{2,0,1:T(2,128)S(1)}, u32[]{:S(2)}, u32[]{:S(2)}) %all-to-all-start.1) | async-done | bytes 82976 | tf_op jit(solution)/shard_map/all_to_all | solution.py:63
  (114 shorter events, 18.6 us)
Async XLA Ops:
  2.8 5.6 %collective-permute-start = (bf16[192,1,256]{2,0,1:T(8,128)(2,1)S(1)}, bf16[192,1,256]{2,0,1:T(8,128)(2,1)S(1)}, u32[]{:S(2)}, u32[]{:S(2)}) collective-permute-start(bf16[192,1,256]{2,0,1:T(8,128)(2,1)S(1)} %get-tuple-element.25), channel_id=1, source_target_pairs={{0,8},{8,16},{16,24},{24,32},{32,40},{40,48},{48,56},{56,64},{64,7... | collective-permute-start | bytes 294920 | tf_op jit(solution)/shard_map/ppermute | solution.py:13
  6.8 5.4 %collective-permute-start.1 = (bf16[192,1,256]{2,0,1:T(8,128)(2,1)S(1)}, bf16[192,1,256]{2,0,1:T(8,128)(2,1)S(1)}, u32[]{:S(2)}, u32[]{:S(2)}) collective-permute-start(bf16[192,1,256]{2,0,1:T(8,128)(2,1)S(1)} %get-tuple-element.26), channel_id=1, source_target_pairs={{8,0},{16,8},{24,16},{32,24},{40,32},{48,40},{56,48},{64,56},{72,6... | collective-permute-start | bytes 294920 | tf_op jit(solution)/shard_map/ppermute | solution.py:14
  12.4 7.3 %copy-start.4 = (bf16[96,8,256]{2,1,0:T(8,128)(2,1)S(1)}, bf16[96,8,256]{2,1,0:T(8,128)(2,1)}, u32[]{:S(2)}) copy-start(bf16[96,8,256]{2,1,0:T(8,128)(2,1)} %param.6) | copy-start | bytes 1179652
  12.6 10.9 %collective-permute-start.2 = (bf16[192,10,1]{2,0,1:T(8,128)(2,1)S(1)}, bf16[192,10,1]{2,0,1:T(8,128)(2,1)S(1)}, u32[]{:S(2)}, u32[]{:S(2)}) collective-permute-start(bf16[192,10,1]{2,0,1:T(8,128)(2,1)S(1)} %get-tuple-element.23), channel_id=1, source_target_pairs={{0,1},{1,2},{2,3},{3,4},{4,5},{5,6},{6,7},{8,9},{9,10},{10,11},{11... | collective-permute-start | bytes 11528 | tf_op jit(solution)/shard_map/ppermute | solution.py:13
  17.8 10.1 %collective-permute-start.3 = (bf16[192,10,1]{2,0,1:T(8,128)(2,1)S(1)}, bf16[192,10,1]{2,0,1:T(8,128)(2,1)S(1)}, u32[]{:S(2)}, u32[]{:S(2)}) collective-permute-start(bf16[192,10,1]{2,0,1:T(8,128)(2,1)S(1)} %get-tuple-element.24), channel_id=1, source_target_pairs={{1,0},{2,1},{3,2},{4,3},{5,4},{6,5},{7,6},{9,8},{10,9},{11,10},{12... | collective-permute-start | bytes 11528 | tf_op jit(solution)/shard_map/ppermute | solution.py:14
  32.0 0.9 copy-start.5
  34.7 0.9 copy-start.9
  37.9 0.7 copy-start.10
  39.4 6.9 %collective-permute-start.4 = (bf16[96,1,256]{2,0,1:T(8,128)(2,1)S(1)}, bf16[96,1,256]{2,0,1:T(8,128)(2,1)S(1)}, u32[]{:S(2)}, u32[]{:S(2)}) collective-permute-start(bf16[96,1,256]{2,0,1:T(8,128)(2,1)S(1)} %get-tuple-element.38), channel_id=1, source_target_pairs={{0,8},{8,16},{16,24},{24,32},{32,40},{40,48},{48,56},{56,64},{64,7... | collective-permute-start | bytes 147464 | tf_op jit(solution)/shard_map/ppermute | solution.py:13
  42.7 4.8 %collective-permute-start.5 = (bf16[96,1,256]{2,0,1:T(8,128)(2,1)S(1)}, bf16[96,1,256]{2,0,1:T(8,128)(2,1)S(1)}, u32[]{:S(2)}, u32[]{:S(2)}) collective-permute-start(bf16[96,1,256]{2,0,1:T(8,128)(2,1)S(1)} %get-tuple-element.39), channel_id=1, source_target_pairs={{8,0},{16,8},{24,16},{32,24},{40,32},{48,40},{56,48},{64,56},{72,6... | collective-permute-start | bytes 147464 | tf_op jit(solution)/shard_map/ppermute | solution.py:14
  47.8 6.7 %collective-permute-start.6 = (bf16[96,10,1]{2,0,1:T(8,128)(2,1)S(1)}, bf16[96,10,1]{2,0,1:T(8,128)(2,1)S(1)}, u32[]{:S(2)}, u32[]{:S(2)}) collective-permute-start(bf16[96,10,1]{2,0,1:T(8,128)(2,1)S(1)} %get-tuple-element.36), channel_id=1, source_target_pairs={{0,1},{1,2},{2,3},{3,4},{4,5},{5,6},{6,7},{8,9},{9,10},{10,11},{11... | collective-permute-start | bytes 5768 | tf_op jit(solution)/shard_map/ppermute | solution.py:13
  51.0 7.5 %collective-permute-start.7 = (bf16[96,10,1]{2,0,1:T(8,128)(2,1)S(1)}, bf16[96,10,1]{2,0,1:T(8,128)(2,1)S(1)}, u32[]{:S(2)}, u32[]{:S(2)}) collective-permute-start(bf16[96,10,1]{2,0,1:T(8,128)(2,1)S(1)} %get-tuple-element.37), channel_id=1, source_target_pairs={{1,0},{2,1},{3,2},{4,3},{5,4},{6,5},{7,6},{9,8},{10,9},{11,10},{12... | collective-permute-start | bytes 5768 | tf_op jit(solution)/shard_map/ppermute | solution.py:14
  53.1 6.3 %copy-start.7 = (bf16[96,8,256]{2,1,0:T(8,128)(2,1)S(1)}, bf16[96,8,256]{2,1,0:T(8,128)(2,1)}, u32[]{:S(2)}) copy-start(bf16[96,8,256]{2,1,0:T(8,128)(2,1)} %param.5) | copy-start | bytes 1179652
  59.7 2.2 %copy-start.8 = (bf16[96,8,256]{2,1,0:T(8,128)(2,1)S(1)}, bf16[96,8,256]{2,1,0:T(8,128)(2,1)}, u32[]{:S(2)}) copy-start(bf16[96,8,256]{2,1,0:T(8,128)(2,1)} %param.5) | copy-start | bytes 1179652
  67.0 16.2 %all-to-all-start = ((f32[2,32,8,324]{3,1,0,2:T(8,128)}), f32[2,32,8,324]{3,1,0,2:T(8,128)S(1)}, u32[]{:S(2)}, u32[]{:S(2)}) async-start(f32[2,32,8,324]{3,1,0,2:T(8,128)} %pad_maximum_fusion), calls=%async_computation | async-start | bytes 1572864 | tf_op jit(solution)/shard_map/all_to_all | solution.py:62
  71.1 2.2 %copy-start.3 = (bf16[8,12,8,256]{3,2,1,0:T(8,128)(2,1)S(1)}, bf16[8,12,8,256]{3,2,1,0:T(8,128)(2,1)}, u32[]{:S(2)}) copy-start(bf16[8,12,8,256]{3,2,1,0:T(8,128)(2,1)} %get-tuple-element.34) | copy-start | bytes 1179652
  71.1 2.3 %copy-start.2 = (bf16[8,12,8,256]{3,2,1,0:T(8,128)(2,1)S(1)}, bf16[8,12,8,256]{3,2,1,0:T(8,128)(2,1)}, u32[]{:S(2)}) copy-start(bf16[8,12,8,256]{3,2,1,0:T(8,128)(2,1)} %get-tuple-element.33) | copy-start | bytes 1179652
  72.2 1.2 %copy-start.1 = (bf16[8,12,8,256]{3,2,1,0:T(8,128)(2,1)S(1)}, bf16[8,12,8,256]{3,2,1,0:T(8,128)(2,1)}, u32[]{:S(2)}) copy-start(bf16[8,12,8,256]{3,2,1,0:T(8,128)(2,1)} %get-tuple-element.32) | copy-start | bytes 1179652
  73.3 1.0 copy-start
  73.4 1.0 copy-start.6
  84.0 23.9 %all-to-all-start.1 = ((f32[2,32,324]{2,0,1:T(2,128)}), f32[2,32,324]{2,0,1:T(2,128)S(1)}, u32[]{:S(2)}, u32[]{:S(2)}) async-start(f32[2,32,324]{2,0,1:T(2,128)} %copy.168), calls=%async_computation.1 | async-start | bytes 196608 | tf_op jit(solution)/shard_map/all_to_all | solution.py:63
